TPU v7x, 32 devices: a whole 2x2x4 slice. The times are simulated.
32 devices in a mesh: row: 4 (over z), col: 8 (over y, x, core).
Axes of the slice: x: 2, y: 2, z: 4, core: 2. Of those that a mesh axis runs over, the one named last changes fastest.
Arguments:
- images: bfloat16 [16384, 2, 4096], P(('row', 'col')), may hold values from -320 to 320
- precision: float32 [16384], P(('row', 'col')), may hold values from 0.001 to 0.01
- templates: bfloat16 [128, 2, 4096], P(('row', 'col')), may hold values from -4 to 4
- template_id: int32 [128], replicated, may hold values from 0 to 127, as said below
- shift_table: int32 [128, 8], replicated, may hold values from 0 to 63, as said below
Outputs:
- updated: float32 [128, 2, 4096], P(('row', 'col'))
Inputs may be any that keep to these rules, and one draw needn't show every extreme that they name: `template_id`: A permutation of 0 to 127. `shift_table`: each row holds 8 different shift numbers.
All inputs are finite; a program needn't handle non-finite values.
Results may differ from a plain program's by a relative error of at most 0.00058.
Values may be sent and summed in bfloat16 or wider, within the bound.
No kernel may reach another device: no remote copies, remote signals or barrier semaphores. Data moves between devices by JAX's collectives and lax.ppermute only.
A program may use at most 192 MiB of HBM per device.

v0:
```python
import functools
import math

import jax
import jax.numpy as jnp
from jax import lax
from jax.experimental import pallas as pl
from jax.experimental.pallas import tpu as pltpu
from jax.sharding import PartitionSpec as P


GRID = 64
SHIFT_SIDE = 8
PRIOR_WEIGHT = 4.0
LANES = 128
PAIR = 2 * LANES
RS_CHUNKS = 1
WIRE = jnp.float32
VMEM_LIMIT = 24 << 20

PARAMS = pltpu.CompilerParams(vmem_limit_bytes=VMEM_LIMIT)


def relay_kernel(in_ref, out_ref, wide_ref):
    count, rows, _ = in_ref.shape
    wide_ref[...] = in_ref[...].astype(jnp.float32).reshape(count * rows, LANES)
    for r in range(rows):
        picked = wide_ref[pl.ds(r, count, stride=rows), :]
        out_ref[:, r * LANES : (r + 1) * LANES] = picked.astype(jnp.bfloat16)


def relay(images, rows=8):
    count, parts, coeffs = images.shape
    groups = coeffs // LANES
    per = parts * groups
    flat = images.reshape(count, parts, groups, LANES)
    flat = flat.transpose(0, 2, 1, 3).reshape(count, per, LANES)
    return pl.pallas_call(
        relay_kernel,
        grid=(per // rows,),
        in_specs=[pl.BlockSpec((count, rows, LANES), lambda i: (0, i, 0))],
        out_specs=pl.BlockSpec((count, rows * LANES), lambda i: (0, i)),
        out_shape=jax.ShapeDtypeStruct((count, per * LANES), jnp.bfloat16),
        scratch_shapes=[pltpu.VMEM((count * rows, LANES), jnp.float32)],
        compiler_params=PARAMS,
        cost_estimate=pl.CostEstimate(
            flops=count * per * LANES,
            bytes_accessed=4 * count * per * LANES,
            transcendentals=0,
        ),
    )(flat)


def score_kernel(pieces, groups, *refs):
    piece_refs = refs[:pieces]
    cos0, sin0, cos_step, sin_step, x_ref = refs[pieces : pieces + 5]
    rest = refs[pieces + 5 :]
    out_ref, norm_ref, cos_ref, sin_ref, rot_ref = rest
    shifts, held, _ = cos0.shape
    step = pl.program_id(0)

    @pl.when(step == 0)
    def _():
        cos_ref[...] = cos0[...]
        sin_ref[...] = sin0[...]
        norm_ref[...] = jnp.zeros_like(norm_ref)
        out_ref[...] = jnp.zeros_like(out_ref)

    piece_rows = held // pieces
    for g in range(groups):
        at = g * PAIR
        for i in range(pieces):
            here = slice(i * piece_rows, (i + 1) * piece_rows)
            real = piece_refs[i][:, at : at + LANES].astype(jnp.float32)
            imag = piece_refs[i][:, at + LANES : at + PAIR].astype(jnp.float32)
            norm_ref[here, :] += real * real + imag * imag
            for j in range(shifts):
                c, s = cos_ref[j, here, :], sin_ref[j, here, :]
                dc, ds = cos_step[j, here, :], sin_step[j, here, :]
                row = slice(j * held + i * piece_rows, j * held + (i + 1) * piece_rows)
                rot_ref[row, at : at + LANES] = (real * c + imag * s).astype(jnp.bfloat16)
                rot_ref[row, at + LANES : at + PAIR] = (imag * c - real * s).astype(
                    jnp.bfloat16
                )
                cos_ref[j, here, :] = c * dc - s * ds
                sin_ref[j, here, :] = s * dc + c * ds
        if (g + 1) % 2 == 0:
            span = slice((g - 1) * PAIR, (g + 1) * PAIR)
            out_ref[...] += lax.dot_general(
                rot_ref[:, span],
                x_ref[:, span],
                (((1,), (1,)), ((), ())),
                preferred_element_type=jnp.float32,
            )


def scores_of(piece_list, phases, steps, half, x, groups=4):
    pieces = len(piece_list)
    rows, width = piece_list[0].shape
    held = pieces * rows
    shifts = phases[0].shape[0]
    images = x.shape[0]
    block = groups * PAIR
    count = width // block
    whole = pl.BlockSpec((shifts, held, LANES), lambda i: (0, half, 0))
    out_spec = pl.BlockSpec((shifts * held, images), lambda i: (0, 0))
    in_specs = [pl.BlockSpec((rows, block), lambda i: (0, i))] * pieces
    in_specs += [whole] * 4
    in_specs += [pl.BlockSpec((images, block), lambda i: (0, i))]
    return pl.pallas_call(
        functools.partial(score_kernel, pieces, groups),
        grid=(count,),
        in_specs=in_specs,
        out_specs=(out_spec, pl.BlockSpec((held, LANES), lambda i: (0, 0))),
        out_shape=(
            jax.ShapeDtypeStruct((shifts * held, images), jnp.float32),
            jax.ShapeDtypeStruct((held, LANES), jnp.float32),
        ),
        scratch_shapes=[
            pltpu.VMEM((shifts, held, LANES), jnp.float32),
            pltpu.VMEM((shifts, held, LANES), jnp.float32),
            pltpu.VMEM((shifts * held, block), jnp.bfloat16),
        ],
        compiler_params=PARAMS,
        cost_estimate=pl.CostEstimate(
            flops=2 * shifts * held * images * width,
            bytes_accessed=2 * images * width + 8 * shifts * held * images,
            transcendentals=0,
        ),
    )(*piece_list, *phases, *steps, x)


def weight_kernel(own_ref, other_ref, own_norm, other_norm, prec_ref, *outs):
    outs, raised_refs = outs[:4], outs[4:]
    prec = prec_ref[...][None]
    halves = ((own_ref, own_norm), (other_ref, other_norm))
    bias, tops = [], []
    for ref, norm_ref in halves:
        norm = 0.5 * jnp.sum(norm_ref[...], axis=1, keepdims=True)
        bias.append(norm[None])
        value = prec * (ref[...] - norm[None])
        tops.append(jnp.max(jnp.max(value, axis=0), axis=0, keepdims=True))
    top = jnp.maximum(*tops)[None]
    norm = 0.0
    for (ref, _), offset, raised_ref in zip(halves, bias, raised_refs):
        raised = jnp.exp(prec * (ref[...] - offset) - top)
        raised_ref[...] = raised
        norm = norm + jnp.sum(jnp.sum(raised, axis=0), axis=0, keepdims=True)
    inverse = (1.0 / norm)[None]
    for h, ref in enumerate(raised_refs):
        weight = (ref[...] * inverse).astype(jnp.bfloat16)
        outs[h][...] = weight
        wide = weight.astype(jnp.float32)
        total = jnp.sum(jnp.sum(wide, axis=0), axis=1, keepdims=True)
        outs[2 + h][...] = jnp.broadcast_to(total, outs[2 + h].shape)


def weights_of(own, other, precision, shifts):
    rows, images = own[0].shape
    held = rows // shifts
    cube = jax.ShapeDtypeStruct((shifts, held, images), jnp.bfloat16)
    total = jax.ShapeDtypeStruct((held, LANES), jnp.float32)
    own_w, other_w, own_t, other_t = pl.pallas_call(
        weight_kernel,
        out_shape=(cube, cube, total, total),
        scratch_shapes=[pltpu.VMEM((shifts, held, images), jnp.float32)] * 2,
        compiler_params=PARAMS,
        cost_estimate=pl.CostEstimate(
            flops=20 * rows * images,
            bytes_accessed=12 * rows * images,
            transcendentals=2 * rows * images,
        ),
    )(
        own[0].reshape(shifts, held, images),
        other[0].reshape(shifts, held, images),
        own[1],
        other[1],
        precision.reshape(1, images),
    )
    return own_w.reshape(rows, images), other_w.reshape(rows, images), own_t, other_t


def back_kernel(groups, w_ref, x_ref, cos0, sin0, cos_step, sin_step, out_ref, cos_ref, sin_ref):
    shifts, held, _ = cos0.shape
    step = pl.program_id(0)

    @pl.when(step == 0)
    def _():
        cos_ref[...] = cos0[...]
        sin_ref[...] = sin0[...]

    for g in range(groups):
        at = g * PAIR
        mixed = jnp.dot(
            w_ref[...], x_ref[:, at : at + PAIR], preferred_element_type=jnp.float32
        )
        for i in range(held // 8):
            here = slice(i * 8, (i + 1) * 8)
            back_real = jnp.zeros((8, LANES), jnp.float32)
            back_imag = jnp.zeros((8, LANES), jnp.float32)
            for j in range(shifts):
                row = slice(j * held + i * 8, j * held + (i + 1) * 8)
                c, s = cos_ref[j, here, :], sin_ref[j, here, :]
                dc, ds = cos_step[j, here, :], sin_step[j, here, :]
                real, imag = mixed[row, :LANES], mixed[row, LANES:]
                back_real = back_real + (real * c - imag * s)
                back_imag = back_imag + (imag * c + real * s)
                cos_ref[j, here, :] = c * dc - s * ds
                sin_ref[j, here, :] = s * dc + c * ds
            out_ref[here, at : at + LANES] = back_real.astype(out_ref.dtype)
            out_ref[here, at + LANES : at + PAIR] = back_imag.astype(out_ref.dtype)


def back_of(weight, x, phases, steps, half, chunk, chunks, groups=4):
    rows, images = weight.shape
    shifts = phases[0].shape[0]
    held = rows // shifts
    width = x.shape[1] // chunks
    groups = min(groups, width // PAIR)
    block = groups * PAIR
    count = width // block
    whole = pl.BlockSpec((shifts, held, LANES), lambda i: (0, half, 0))
    return pl.pallas_call(
        functools.partial(back_kernel, groups),
        grid=(count,),
        in_specs=[
            pl.BlockSpec((rows, images), lambda i: (0, 0)),
            pl.BlockSpec((images, block), lambda i: (0, chunk * count + i)),
        ]
        + [whole] * 4,
        out_specs=pl.BlockSpec((held, block), lambda i: (0, i)),
        out_shape=jax.ShapeDtypeStruct((held, width), jnp.float32),
        scratch_shapes=[
            pltpu.VMEM((shifts, held, LANES), jnp.float32),
            pltpu.VMEM((shifts, held, LANES), jnp.float32),
        ],
        compiler_params=PARAMS,
        cost_estimate=pl.CostEstimate(
            flops=2 * rows * images * width,
            bytes_accessed=2 * images * width + 2 * rows * images + 4 * held * width,
            transcendentals=0,
        ),
    )(weight, x, *phases, *steps)


def exchange(value, axis, size, bit):
    return lax.ppermute(value, axis, [(i, i ^ bit) for i in range(size)])


def body(images, precision, templates, template_id, shift_table):
    _, parts, coeffs = images.shape
    local = templates.shape[0]
    shifts = shift_table.shape[1]
    rows, cols = lax.axis_size("row"), lax.axis_size("col")
    quads = cols // 2
    groups = coeffs // LANES
    width = parts * coeffs
    held = local * rows * quads

    mine = templates.reshape(local, parts, groups, LANES)
    mine = mine.transpose(0, 2, 1, 3).reshape(local, width)

    row_set = [mine]
    row_set += [exchange(mine, "row", rows, d) for d in range(1, rows)]
    row_set = jnp.concatenate(row_set, axis=0)
    own_set = [row_set]
    own_set += [exchange(row_set, "col", cols, 2 * d) for d in range(1, quads)]
    other_set = [exchange(value, "col", cols, 1) for value in own_set]

    x = relay(images)

    position = jnp.arange(2 * held, dtype=jnp.int32)
    at_local = position % local
    at_row = (position // local % rows) ^ lax.axis_index("row")
    at_quad = position // (local * rows) % quads
    at_col = (2 * at_quad + position // held) ^ lax.axis_index("col")
    slots = (at_row * cols + at_col) * local + at_local
    shift = shift_table[template_id[slots]].T.reshape(-1, 1)

    number = jnp.arange(SHIFT_SIDE * SHIFT_SIDE, dtype=jnp.int32)[:, None]
    step_x = number // SHIFT_SIDE - SHIFT_SIDE // 2
    step_y = number % SHIFT_SIDE - SHIFT_SIDE // 2
    lane = jnp.arange(LANES, dtype=jnp.int32)[None, :]
    freq_x = lane // GRID - GRID // 2
    freq_y = lane % GRID - GRID // 2
    first = (step_x * freq_x + step_y * freq_y) % GRID
    stride = jnp.broadcast_to(step_x * (LANES // GRID) % GRID, first.shape)
    angle = jnp.concatenate([first, stride], axis=1).astype(jnp.float32)
    angle = angle * (2.0 * math.pi / GRID)
    table = jnp.concatenate([jnp.cos(angle), jnp.sin(angle)], axis=1)
    chosen = (shift == number.T).astype(jnp.float32)
    unit = []
    for at in range(4):
        part = lax.dot(
            chosen, table[:, at * LANES : (at + 1) * LANES], precision=lax.Precision.HIGHEST
        )
        unit.append(part.reshape(shifts, 2 * held, LANES))
    start, steps = (unit[0], unit[2]), (unit[1], unit[3])

    own_scores = scores_of(own_set, start, steps, 0, x)
    other_scores = scores_of(other_set, start, steps, 1, x)
    own_w, other_w, own_total, other_total = weights_of(
        own_scores, other_scores, precision, shifts
    )

    def reduce_to_owner(own, other, wire):
        def send(value, axis, size, bit):
            return exchange(value.astype(wire), axis, size, bit).astype(jnp.float32)

        got = send(other, "col", cols, 1)
        total = own + got
        per = local * rows
        part = total[:per]
        got = [
            send(total[d * per : (d + 1) * per], "col", cols, 2 * d)
            for d in range(1, quads)
        ]
        part = sum(got, part)
        got = [
            send(part[d * local : (d + 1) * local], "row", rows, d)
            for d in range(1, rows)
        ]
        return sum(got, part[:local])

    totals = reduce_to_owner(own_total, other_total, jnp.float32)
    results = []
    for b in range(RS_CHUNKS):
        other = back_of(other_w, x, start, steps, 1, b, RS_CHUNKS)
        own = back_of(own_w, x, start, steps, 0, b, RS_CHUNKS)
        span = width // RS_CHUNKS
        summed = reduce_to_owner(own, other, WIRE)
        prior = mine[:, b * span : (b + 1) * span].astype(jnp.float32)
        results.append((summed + PRIOR_WEIGHT * prior) / (totals[:, :1] + PRIOR_WEIGHT))
    out = results[0] if RS_CHUNKS == 1 else jnp.concatenate(results, axis=1)
    out = out.reshape(local, groups, parts, LANES).transpose(0, 2, 1, 3)
    return out.reshape(local, parts, coeffs)


def solution(mesh):
    return jax.shard_map(
        body,
        mesh=mesh,
        in_specs=(
            P(("row", "col"), None, None),
            P(("row", "col")),
            P(("row", "col"), None, None),
            P(),
            P(),
        ),
        out_specs=P(("row", "col"), None, None),
        check_vma=False,
    )
```

profile of v0, /device:TPU:0, one launch (start us, length us, event | category | flops | bytes accessed | tf_op | source)
XLA Modules:
  0.0 113.3 jit_solution(16708932949438945589)
XLA Ops:
  0.0 0.9 reshape.389
  0.9 5.1 %collective-permute-start.2 = (bf16[4,8192]{1,0:T(4,128)(2,1)S(1)}, bf16[4,8192]{1,0:T(4,128)(2,1)S(1)}, u32[]{:S(2)}, u32[]{:S(2)}) collective-permute-start(bf16[4,8192]{1,0:T(4,128)(2,1)S(1)} %reshape.389), channel_id=1, source_target_pairs={{0,24},{8,16},{16,8},{24,0},{1,25},{9,17},{17,9},{25,1},{2,26},{10... | collective-permute-start | bytes 196616 | tf_op jit(solution)/shard_map/ppermute | solution.py:247
  6.0 0.6 collective-permute-start
  6.7 1.2 %gather_fusion = s32[128]{0:T(128)S(1)} fusion(s32[128]{0:T(128)S(1)} %copy-done, s32[1024]{0:T(1024)S(1)} %pad_clamp_fusion.1), kind=kCustom, calls=%fused_computation | custom fusion | bytes 1536 | tf_op jit(solution)/shard_map/gather | solution.py:278
  8.0 0.8 copy.11
  8.8 0.6 gather_fusion.1
  9.5 0.1 add_select_fusion
  9.7 0.2 fusion.15
  9.9 0.5 fusion.2
  10.4 0.5 fusion.4
  10.9 0.7 collective-permute-done.1
  11.6 0.2 pad_maximum_fusion.refs_0_
  11.8 2.5 %collective-permute-start.5 = (bf16[16,8192]{1,0:T(8,128)(2,1)S(1)}, bf16[16,8192]{1,0:T(8,128)(2,1)S(1)}, u32[]{:S(2)}, u32[]{:S(2)}) collective-permute-start(bf16[16,8192]{1,0:T(8,128)(2,1)S(1)} %pad_maximum_fusion.refs_0_), channel_id=1, source_target_pairs={{0,6},{1,7},{2,4},{3,5},{4,2},{5,3},{6,0},{7,1},{8,14},{9,15},{10,... | collective-permute-start | bytes 786440 | tf_op jit(solution)/shard_map/ppermute | solution.py:247
  14.3 0.5 collective-permute-start.4
  14.8 0.5 collective-permute-start.3
  15.3 0.5 fusion.3
  15.8 3.4 %copy-done.1 = bf16[512,2,4096]{2,1,0:T(2,128)(2,1)S(1)} copy-done((bf16[512,2,4096]{2,1,0:T(2,128)(2,1)S(1)}, bf16[512,2,4096]{2,1,0:T(2,128)(2,1)}, u32[]{:S(2)}) %copy-start.1) | copy-done | bytes 8388632
  19.2 7.8 %shard_map.55.refs_8_.x_ref = bf16[512,8192]{1,0:T(8,128)(2,1)S(1)} custom-call(bf16[512,64,128]{2,1,0:T(8,128)(2,1)S(1)} %bitcast.28), custom_call_target="tpu_custom_call" | custom-call | flops 4194304 | bytes 16777216 | tf_op jit(solution)/shard_map/pallas_call | solution.py:38
  27.0 0.5 fusion.5
  27.6 0.5 collective-permute-start.9
  28.2 0.4 collective-permute-start.7
  28.6 9.3 %shard_map.56 = (f32[512,512]{1,0:T(8,128)S(1)}, f32[64,128]{1,0:T(8,128)S(1)}) custom-call(bf16[16,8192]{1,0:T(8,128)(2,1)S(1)} %pad_maximum_fusion.refs_0_, bf16[16,8192]{1,0:T(8,128)(2,1)S(1)} %collective-permute-done.3.refs_1_, bf16[16,8192]{1,0:T(8,128)(2,1)S(1)} %collective-permute-done.4.refs_2_, bf16[16,8192]{1,0:T(8,128)(2,1)S(1)} %collective-permute-done.5.refs_3_, ...), custom_call_target="tpu_custom_call" | custom-call | flops 4294967296 | bytes 10485760 | tf_op jit(solution)/shard_map/pallas_call | solution.py:110
  37.9 9.3 %shard_map.57 = (f32[512,512]{1,0:T(8,128)S(1)}, f32[64,128]{1,0:T(8,128)S(1)}) custom-call(bf16[16,8192]{1,0:T(8,128)(2,1)S(1)} %collective-permute-done.6.refs_0_, bf16[16,8192]{1,0:T(8,128)(2,1)S(1)} %collective-permute-done.7.refs_1_, bf16[16,8192]{1,0:T(8,128)(2,1)S(1)} %collective-permute-done.8.refs_2_, ...), custom_call_target="tpu_custom_call" | custom-call | flops 4294967296 | bytes 10485760 | tf_op jit(solution)/shard_map/pallas_call | solution.py:110
  47.2 1.3 %shard_map.58 = (bf16[8,64,512]{2,1,0:T(8,128)(2,1)S(1)}, bf16[8,64,512]{2,1,0:T(8,128)(2,1)S(1)}, f32[64,128]{1,0:T(8,128)S(1)}, f32[64,128]{1,0:T(8,128)S(1)}) custom-call(f32[8,64,512]{2,1,0:T(8,128)S(1)} %bitcast.29, f32[8,64,512]{2,1,0:T(8,128)S(1)} %bitcast.30, f32[64,128]{1,0:T(8,128)S(1)} %get-tuple-element.15.own_norm, ...), custom_call_target="tpu_custom_call" | custom-call | flops 5242880 | bytes 3145728 | tf_op jit(solution)/shard_map/pallas_call | solution.py:163
  48.6 8.0 %shard_map.60 = f32[64,8192]{1,0:T(8,128)S(1)} custom-call(bf16[512,512]{1,0:T(8,128)(2,1)S(1)} %bitcast.49, bf16[512,8192]{1,0:T(8,128)(2,1)S(1)} %shard_map.55.refs_8_.x_ref, f32[8,128,128]{2,1,0:T(8,128)S(1)} %bitcast.45, f32[8,128,128]{2,1,0:T(8,128)S(1)} %bitcast.37, f32[8,128,128]{2,1,0:T(8,128)S(1)} %bitcast.41, f32[8,128,128]{2,1,0:T(8,128)S(1)} %bitcast.33), custom_call_target="tpu_custom_call" | custom-call | flops 4294967296 | bytes 11010048 | tf_op jit(solution)/shard_map/pallas_call | solution.py:223
  56.6 0.2 collective-permute-start.10
  56.7 0.4 collective-permute-start.17
  57.2 8.0 %shard_map.59 = f32[64,8192]{1,0:T(8,128)S(1)} custom-call(bf16[512,512]{1,0:T(8,128)(2,1)S(1)} %bitcast.48, bf16[512,8192]{1,0:T(8,128)(2,1)S(1)} %shard_map.55.refs_8_.x_ref, f32[8,128,128]{2,1,0:T(8,128)S(1)} %bitcast.46, f32[8,128,128]{2,1,0:T(8,128)S(1)} %bitcast.38, f32[8,128,128]{2,1,0:T(8,128)S(1)} %bitcast.42, f32[8,128,128]{2,1,0:T(8,128)S(1)} %bitcast.34), custom_call_target="tpu_custom_call" | custom-call | flops 4294967296 | bytes 11010048 | tf_op jit(solution)/shard_map/pallas_call | solution.py:223
  65.2 0.3 add.252
  65.7 1.6 %collective-permute-start.11 = (f32[16,8192]{1,0:T(8,128)S(1)}, f32[16,8192]{1,0:T(8,128)S(1)}, u32[]{:S(2)}, u32[]{:S(2)}) collective-permute-start(f32[16,8192]{1,0:T(8,128)S(1)} %get-tuple-element.21), channel_id=1, source_target_pairs={{0,2},{1,3},{2,0},{3,1},{4,6},{5,7},{6,4},{7,5},{8,10},{9,11},{10,... | collective-permute-start | bytes 1572872 | tf_op jit(solution)/shard_map/ppermute | solution.py:247
  67.2 1.5 %collective-permute-start.13 = (f32[16,8192]{1,0:T(8,128)S(1)}, f32[16,8192]{1,0:T(8,128)S(1)}, u32[]{:S(2)}, u32[]{:S(2)}) collective-permute-start(f32[16,8192]{1,0:T(8,128)S(1)} %get-tuple-element.22), channel_id=1, source_target_pairs={{0,6},{1,7},{2,4},{3,5},{4,2},{5,3},{6,0},{7,1},{8,14},{9,15},{10,... | collective-permute-start | bytes 1572872 | tf_op jit(solution)/shard_map/ppermute | solution.py:247
  68.7 0.5 collective-permute-start.12
  69.2 1.5 %collective-permute-start.18 = (f32[16,128]{1,0:T(8,128)S(1)}, f32[16,128]{1,0:T(8,128)S(1)}, u32[]{:S(2)}, u32[]{:S(2)}) collective-permute-start(f32[16,128]{1,0:T(8,128)S(1)} %get-tuple-element.29), channel_id=1, source_target_pairs={{0,2},{1,3},{2,0},{3,1},{4,6},{5,7},{6,4},{7,5},{8,10},{9,11},{10,... | collective-permute-start | bytes 24584 | tf_op jit(solution)/shard_map/ppermute | solution.py:247
  70.7 1.5 %collective-permute-start.20 = (f32[16,128]{1,0:T(8,128)S(1)}, f32[16,128]{1,0:T(8,128)S(1)}, u32[]{:S(2)}, u32[]{:S(2)}) collective-permute-start(f32[16,128]{1,0:T(8,128)S(1)} %get-tuple-element.30), channel_id=1, source_target_pairs={{0,6},{1,7},{2,4},{3,5},{4,2},{5,3},{6,0},{7,1},{8,14},{9,15},{10,... | collective-permute-start | bytes 24584 | tf_op jit(solution)/shard_map/ppermute | solution.py:247
  72.2 19.0 %collective-permute-done.18 = f32[16,128]{1,0:T(8,128)S(1)} collective-permute-done((f32[16,128]{1,0:T(8,128)S(1)}, f32[16,128]{1,0:T(8,128)S(1)}, u32[]{:S(2)}, u32[]{:S(2)}) %collective-permute-start.18) | collective-permute-done | bytes 8224 | tf_op jit(solution)/shard_map/ppermute | solution.py:247
  91.2 1.5 %collective-permute-start.19 = (f32[16,128]{1,0:T(8,128)S(1)}, f32[16,128]{1,0:T(8,128)S(1)}, u32[]{:S(2)}, u32[]{:S(2)}) collective-permute-start(f32[16,128]{1,0:T(8,128)S(1)} %get-tuple-element.31), channel_id=1, source_target_pairs={{0,4},{1,5},{2,6},{3,7},{4,0},{5,1},{6,2},{7,3},{8,12},{9,13},{10,... | collective-permute-start | bytes 24584 | tf_op jit(solution)/shard_map/ppermute | solution.py:247
  92.7 2.1 %collective-permute-done.19 = f32[16,128]{1,0:T(8,128)S(1)} collective-permute-done((f32[16,128]{1,0:T(8,128)S(1)}, f32[16,128]{1,0:T(8,128)S(1)}, u32[]{:S(2)}, u32[]{:S(2)}) %collective-permute-start.19) | collective-permute-done | bytes 8224 | tf_op jit(solution)/shard_map/ppermute | solution.py:247
  94.8 1.1 %collective-permute-start.21 = (f32[4,128]{1,0:T(4,128)S(1)}, f32[4,128]{1,0:T(4,128)S(1)}, u32[]{:S(2)}, u32[]{:S(2)}) collective-permute-start(f32[4,128]{1,0:T(4,128)S(1)} %get-tuple-element.32), channel_id=1, source_target_pairs={{0,8},{8,0},{16,24},{24,16},{1,9},{9,1},{17,25},{25,17},{2,10},{10... | collective-permute-start | bytes 6152 | tf_op jit(solution)/shard_map/ppermute | solution.py:247
  96.0 2.0 %collective-permute-start.23 = (f32[4,128]{1,0:T(4,128)S(1)}, f32[4,128]{1,0:T(4,128)S(1)}, u32[]{:S(2)}, u32[]{:S(2)}) collective-permute-start(f32[4,128]{1,0:T(4,128)S(1)} %get-tuple-element.33), channel_id=1, source_target_pairs={{0,24},{8,16},{16,8},{24,0},{1,25},{9,17},{17,9},{25,1},{2,26},{10... | collective-permute-start | bytes 6152 | tf_op jit(solution)/shard_map/ppermute | solution.py:247
  98.0 0.5 collective-permute-start.22
  98.5 0.1 fusion.1
  98.7 2.0 %collective-permute-start.14 = (f32[4,8192]{1,0:T(4,128)S(1)}, f32[4,8192]{1,0:T(4,128)S(1)}, u32[]{:S(2)}, u32[]{:S(2)}) collective-permute-start(f32[4,8192]{1,0:T(4,128)S(1)} %get-tuple-element.24), channel_id=1, source_target_pairs={{0,8},{8,0},{16,24},{24,16},{1,9},{9,1},{17,25},{25,17},{2,10},{10... | collective-permute-start | bytes 393224 | tf_op jit(solution)/shard_map/ppermute | solution.py:247
  100.7 2.0 %collective-permute-start.16 = (f32[4,8192]{1,0:T(4,128)S(1)}, f32[4,8192]{1,0:T(4,128)S(1)}, u32[]{:S(2)}, u32[]{:S(2)}) collective-permute-start(f32[4,8192]{1,0:T(4,128)S(1)} %get-tuple-element.25), channel_id=1, source_target_pairs={{0,24},{8,16},{16,8},{24,0},{1,25},{9,17},{17,9},{25,1},{2,26},{10... | collective-permute-start | bytes 393224 | tf_op jit(solution)/shard_map/ppermute | solution.py:247
  102.7 0.1 add_reduce_fusion
  102.8 2.7 %collective-permute-done.14 = f32[4,8192]{1,0:T(4,128)S(1)} collective-permute-done((f32[4,8192]{1,0:T(4,128)S(1)}, f32[4,8192]{1,0:T(4,128)S(1)}, u32[]{:S(2)}, u32[]{:S(2)}) %collective-permute-start.14) | collective-permute-done | bytes 131104 | tf_op jit(solution)/shard_map/ppermute | solution.py:247
  105.5 2.6 %collective-permute-done.16 = f32[4,8192]{1,0:T(4,128)S(1)} collective-permute-done((f32[4,8192]{1,0:T(4,128)S(1)}, f32[4,8192]{1,0:T(4,128)S(1)}, u32[]{:S(2)}, u32[]{:S(2)}) %collective-permute-start.16) | collective-permute-done | bytes 131104 | tf_op jit(solution)/shard_map/ppermute | solution.py:247
  108.1 4.2 %collective-permute-done.15 = f32[4,8192]{1,0:T(4,128)S(1)} collective-permute-done((f32[4,8192]{1,0:T(4,128)S(1)}, f32[4,8192]{1,0:T(4,128)S(1)}, u32[]{:S(2)}, u32[]{:S(2)}) %collective-permute-start.15) | collective-permute-done | bytes 131104 | tf_op jit(solution)/shard_map/ppermute | solution.py:247
  112.5 0.8 reshape.401
  (44 shorter events, 0.7 us)
Async XLA Ops:
  0.0 6.7 %copy-start = (s32[128]{0:T(128)S(1)}, s32[128]{0:T(128)}, u32[]{:S(2)}) copy-start(s32[128]{0:T(128)} %param.8) | copy-start | bytes 1540
  0.9 10.0 %collective-permute-start.2 = (bf16[4,8192]{1,0:T(4,128)(2,1)S(1)}, bf16[4,8192]{1,0:T(4,128)(2,1)S(1)}, u32[]{:S(2)}, u32[]{:S(2)}) collective-permute-start(bf16[4,8192]{1,0:T(4,128)(2,1)S(1)} %reshape.389), channel_id=1, source_target_pairs={{0,24},{8,16},{16,8},{24,0},{1,25},{9,17},{17,9},{25,1},{2,26},{10... | collective-permute-start | bytes 196616 | tf_op jit(solution)/shard_map/ppermute | solution.py:247
  6.0 5.6 %collective-permute-start.1 = (bf16[4,8192]{1,0:T(4,128)(2,1)S(1)}, bf16[4,8192]{1,0:T(4,128)(2,1)S(1)}, u32[]{:S(2)}, u32[]{:S(2)}) collective-permute-start(bf16[4,8192]{1,0:T(4,128)(2,1)S(1)} %reshape.389), channel_id=1, source_target_pairs={{0,16},{8,24},{16,0},{24,8},{1,17},{9,25},{17,1},{25,9},{2,18},{10... | collective-permute-start | bytes 196616 | tf_op jit(solution)/shard_map/ppermute | solution.py:247
  6.0 5.6 %collective-permute-start = (bf16[4,8192]{1,0:T(4,128)(2,1)S(1)}, bf16[4,8192]{1,0:T(4,128)(2,1)S(1)}, u32[]{:S(2)}, u32[]{:S(2)}) collective-permute-start(bf16[4,8192]{1,0:T(4,128)(2,1)S(1)} %reshape.389), channel_id=1, source_target_pairs={{0,8},{8,0},{16,24},{24,16},{1,9},{9,1},{17,25},{25,17},{2,10},{10... | collective-permute-start | bytes 196616 | tf_op jit(solution)/shard_map/ppermute | solution.py:247
  11.8 15.8 %collective-permute-start.5 = (bf16[16,8192]{1,0:T(8,128)(2,1)S(1)}, bf16[16,8192]{1,0:T(8,128)(2,1)S(1)}, u32[]{:S(2)}, u32[]{:S(2)}) collective-permute-start(bf16[16,8192]{1,0:T(8,128)(2,1)S(1)} %pad_maximum_fusion.refs_0_), channel_id=1, source_target_pairs={{0,6},{1,7},{2,4},{3,5},{4,2},{5,3},{6,0},{7,1},{8,14},{9,15},{10,... | collective-permute-start | bytes 786440 | tf_op jit(solution)/shard_map/ppermute | solution.py:247
  14.3 13.8 %collective-permute-start.4 = (bf16[16,8192]{1,0:T(8,128)(2,1)S(1)}, bf16[16,8192]{1,0:T(8,128)(2,1)S(1)}, u32[]{:S(2)}, u32[]{:S(2)}) collective-permute-start(bf16[16,8192]{1,0:T(8,128)(2,1)S(1)} %pad_maximum_fusion.refs_0_), channel_id=1, source_target_pairs={{0,4},{1,5},{2,6},{3,7},{4,0},{5,1},{6,2},{7,3},{8,12},{9,13},{10,... | collective-permute-start | bytes 786440 | tf_op jit(solution)/shard_map/ppermute | solution.py:247
  14.8 13.4 %collective-permute-start.3 = (bf16[16,8192]{1,0:T(8,128)(2,1)S(1)}, bf16[16,8192]{1,0:T(8,128)(2,1)S(1)}, u32[]{:S(2)}, u32[]{:S(2)}) collective-permute-start(bf16[16,8192]{1,0:T(8,128)(2,1)S(1)} %pad_maximum_fusion.refs_0_), channel_id=1, source_target_pairs={{0,2},{1,3},{2,0},{3,1},{4,6},{5,7},{6,4},{7,5},{8,10},{9,11},{10,... | collective-permute-start | bytes 786440 | tf_op jit(solution)/shard_map/ppermute | solution.py:247
  15.8 3.4 %copy-start.1 = (bf16[512,2,4096]{2,1,0:T(2,128)(2,1)S(1)}, bf16[512,2,4096]{2,1,0:T(2,128)(2,1)}, u32[]{:S(2)}) copy-start(bf16[512,2,4096]{2,1,0:T(2,128)(2,1)} %param.5) | copy-start | bytes 25165828
  27.5 10.4 %collective-permute-start.6 = (bf16[16,8192]{1,0:T(8,128)(2,1)S(1)}, bf16[16,8192]{1,0:T(8,128)(2,1)S(1)}, u32[]{:S(2)}, u32[]{:S(2)}) collective-permute-start(bf16[16,8192]{1,0:T(8,128)(2,1)S(1)} %pad_maximum_fusion.refs_0_), channel_id=1, source_target_pairs={{0,1},{1,0},{2,3},{3,2},{4,5},{5,4},{6,7},{7,6},{8,9},{9,8},{10,11... | collective-permute-start | bytes 786440 | tf_op jit(solution)/shard_map/ppermute | solution.py:247
  27.6 10.3 %collective-permute-start.9 = (bf16[16,8192]{1,0:T(8,128)(2,1)S(1)}, bf16[16,8192]{1,0:T(8,128)(2,1)S(1)}, u32[]{:S(2)}, u32[]{:S(2)}) collective-permute-start(bf16[16,8192]{1,0:T(8,128)(2,1)S(1)} %collective-permute-done.5.refs_3_), channel_id=1, source_target_pairs={{0,1},{1,0},{2,3},{3,2},{4,5},{5,4},{6,7},{7,6},{8,9},{9,8},{10,11... | collective-permute-start | bytes 786440 | tf_op jit(solution)/shard_map/ppermute | solution.py:247
  28.1 9.8 %collective-permute-start.8 = (bf16[16,8192]{1,0:T(8,128)(2,1)S(1)}, bf16[16,8192]{1,0:T(8,128)(2,1)S(1)}, u32[]{:S(2)}, u32[]{:S(2)}) collective-permute-start(bf16[16,8192]{1,0:T(8,128)(2,1)S(1)} %collective-permute-done.4.refs_2_), channel_id=1, source_target_pairs={{0,1},{1,0},{2,3},{3,2},{4,5},{5,4},{6,7},{7,6},{8,9},{9,8},{10,11... | collective-permute-start | bytes 786440 | tf_op jit(solution)/shard_map/ppermute | solution.py:247
  28.2 9.8 %collective-permute-start.7 = (bf16[16,8192]{1,0:T(8,128)(2,1)S(1)}, bf16[16,8192]{1,0:T(8,128)(2,1)S(1)}, u32[]{:S(2)}, u32[]{:S(2)}) collective-permute-start(bf16[16,8192]{1,0:T(8,128)(2,1)S(1)} %collective-permute-done.3.refs_1_), channel_id=1, source_target_pairs={{0,1},{1,0},{2,3},{3,2},{4,5},{5,4},{6,7},{7,6},{8,9},{9,8},{10,11... | collective-permute-start | bytes 786440 | tf_op jit(solution)/shard_map/ppermute | solution.py:247
  37.9 9.4 %copy-start.2 = (f32[512]{0:T(512)S(1)}, f32[512]{0:T(512)}, u32[]{:S(2)}) copy-start(f32[512]{0:T(512)} %param.6) | copy-start | bytes 6148
  56.6 8.6 %collective-permute-start.10 = (f32[64,8192]{1,0:T(8,128)S(1)}, f32[64,8192]{1,0:T(8,128)S(1)}, u32[]{:S(2)}, u32[]{:S(2)}) collective-permute-start(f32[64,8192]{1,0:T(8,128)S(1)} %shard_map.60), channel_id=1, source_target_pairs={{0,1},{1,0},{2,3},{3,2},{4,5},{5,4},{6,7},{7,6},{8,9},{9,8},{10,11... | collective-permute-start | bytes 6291464 | tf_op jit(solution)/shard_map/ppermute | solution.py:247
  56.7 8.4 %collective-permute-start.17 = (f32[64,128]{1,0:T(8,128)S(1)}, f32[64,128]{1,0:T(8,128)S(1)}, u32[]{:S(2)}, u32[]{:S(2)}) collective-permute-start(f32[64,128]{1,0:T(8,128)S(1)} %get-tuple-element.20), channel_id=1, source_target_pairs={{0,1},{1,0},{2,3},{3,2},{4,5},{5,4},{6,7},{7,6},{8,9},{9,8},{10,11... | collective-permute-start | bytes 98312 | tf_op jit(solution)/shard_map/ppermute | solution.py:247
  65.7 32.4 %collective-permute-start.11 = (f32[16,8192]{1,0:T(8,128)S(1)}, f32[16,8192]{1,0:T(8,128)S(1)}, u32[]{:S(2)}, u32[]{:S(2)}) collective-permute-start(f32[16,8192]{1,0:T(8,128)S(1)} %get-tuple-element.21), channel_id=1, source_target_pairs={{0,2},{1,3},{2,0},{3,1},{4,6},{5,7},{6,4},{7,5},{8,10},{9,11},{10,... | collective-permute-start | bytes 1572872 | tf_op jit(solution)/shard_map/ppermute | solution.py:247
  67.2 31.3 %collective-permute-start.13 = (f32[16,8192]{1,0:T(8,128)S(1)}, f32[16,8192]{1,0:T(8,128)S(1)}, u32[]{:S(2)}, u32[]{:S(2)}) collective-permute-start(f32[16,8192]{1,0:T(8,128)S(1)} %get-tuple-element.22), channel_id=1, source_target_pairs={{0,6},{1,7},{2,4},{3,5},{4,2},{5,3},{6,0},{7,1},{8,14},{9,15},{10,... | collective-permute-start | bytes 1572872 | tf_op jit(solution)/shard_map/ppermute | solution.py:247
  68.7 29.8 %collective-permute-start.12 = (f32[16,8192]{1,0:T(8,128)S(1)}, f32[16,8192]{1,0:T(8,128)S(1)}, u32[]{:S(2)}, u32[]{:S(2)}) collective-permute-start(f32[16,8192]{1,0:T(8,128)S(1)} %get-tuple-element.23), channel_id=1, source_target_pairs={{0,4},{1,5},{2,6},{3,7},{4,0},{5,1},{6,2},{7,3},{8,12},{9,13},{10,... | collective-permute-start | bytes 1572872 | tf_op jit(solution)/shard_map/ppermute | solution.py:247
  69.2 22.0 %collective-permute-start.18 = (f32[16,128]{1,0:T(8,128)S(1)}, f32[16,128]{1,0:T(8,128)S(1)}, u32[]{:S(2)}, u32[]{:S(2)}) collective-permute-start(f32[16,128]{1,0:T(8,128)S(1)} %get-tuple-element.29), channel_id=1, source_target_pairs={{0,2},{1,3},{2,0},{3,1},{4,6},{5,7},{6,4},{7,5},{8,10},{9,11},{10,... | collective-permute-start | bytes 24584 | tf_op jit(solution)/shard_map/ppermute | solution.py:247
  70.7 22.0 %collective-permute-start.20 = (f32[16,128]{1,0:T(8,128)S(1)}, f32[16,128]{1,0:T(8,128)S(1)}, u32[]{:S(2)}, u32[]{:S(2)}) collective-permute-start(f32[16,128]{1,0:T(8,128)S(1)} %get-tuple-element.30), channel_id=1, source_target_pairs={{0,6},{1,7},{2,4},{3,5},{4,2},{5,3},{6,0},{7,1},{8,14},{9,15},{10,... | collective-permute-start | bytes 24584 | tf_op jit(solution)/shard_map/ppermute | solution.py:247
  91.2 3.7 %collective-permute-start.19 = (f32[16,128]{1,0:T(8,128)S(1)}, f32[16,128]{1,0:T(8,128)S(1)}, u32[]{:S(2)}, u32[]{:S(2)}) collective-permute-start(f32[16,128]{1,0:T(8,128)S(1)} %get-tuple-element.31), channel_id=1, source_target_pairs={{0,4},{1,5},{2,6},{3,7},{4,0},{5,1},{6,2},{7,3},{8,12},{9,13},{10,... | collective-permute-start | bytes 24584 | tf_op jit(solution)/shard_map/ppermute | solution.py:247
  94.8 7.8 %collective-permute-start.21 = (f32[4,128]{1,0:T(4,128)S(1)}, f32[4,128]{1,0:T(4,128)S(1)}, u32[]{:S(2)}, u32[]{:S(2)}) collective-permute-start(f32[4,128]{1,0:T(4,128)S(1)} %get-tuple-element.32), channel_id=1, source_target_pairs={{0,8},{8,0},{16,24},{24,16},{1,9},{9,1},{17,25},{25,17},{2,10},{10... | collective-permute-start | bytes 6152 | tf_op jit(solution)/shard_map/ppermute | solution.py:247
  96.0 6.7 %collective-permute-start.23 = (f32[4,128]{1,0:T(4,128)S(1)}, f32[4,128]{1,0:T(4,128)S(1)}, u32[]{:S(2)}, u32[]{:S(2)}) collective-permute-start(f32[4,128]{1,0:T(4,128)S(1)} %get-tuple-element.33), channel_id=1, source_target_pairs={{0,24},{8,16},{16,8},{24,0},{1,25},{9,17},{17,9},{25,1},{2,26},{10... | collective-permute-start | bytes 6152 | tf_op jit(solution)/shard_map/ppermute | solution.py:247
  98.0 4.7 %collective-permute-start.22 = (f32[4,128]{1,0:T(4,128)S(1)}, f32[4,128]{1,0:T(4,128)S(1)}, u32[]{:S(2)}, u32[]{:S(2)}) collective-permute-start(f32[4,128]{1,0:T(4,128)S(1)} %get-tuple-element.34), channel_id=1, source_target_pairs={{0,16},{8,24},{16,0},{24,8},{1,17},{9,25},{17,1},{25,9},{2,18},{10... | collective-permute-start | bytes 6152 | tf_op jit(solution)/shard_map/ppermute | solution.py:247
  98.7 6.8 %collective-permute-start.14 = (f32[4,8192]{1,0:T(4,128)S(1)}, f32[4,8192]{1,0:T(4,128)S(1)}, u32[]{:S(2)}, u32[]{:S(2)}) collective-permute-start(f32[4,8192]{1,0:T(4,128)S(1)} %get-tuple-element.24), channel_id=1, source_target_pairs={{0,8},{8,0},{16,24},{24,16},{1,9},{9,1},{17,25},{25,17},{2,10},{10... | collective-permute-start | bytes 393224 | tf_op jit(solution)/shard_map/ppermute | solution.py:247
  100.7 7.5 %collective-permute-start.16 = (f32[4,8192]{1,0:T(4,128)S(1)}, f32[4,8192]{1,0:T(4,128)S(1)}, u32[]{:S(2)}, u32[]{:S(2)}) collective-permute-start(f32[4,8192]{1,0:T(4,128)S(1)} %get-tuple-element.25), channel_id=1, source_target_pairs={{0,24},{8,16},{16,8},{24,0},{1,25},{9,17},{17,9},{25,1},{2,26},{10... | collective-permute-start | bytes 393224 | tf_op jit(solution)/shard_map/ppermute | solution.py:247
  102.7 9.7 %collective-permute-start.15 = (f32[4,8192]{1,0:T(4,128)S(1)}, f32[4,8192]{1,0:T(4,128)S(1)}, u32[]{:S(2)}, u32[]{:S(2)}) collective-permute-start(f32[4,8192]{1,0:T(4,128)S(1)} %get-tuple-element.26), channel_id=1, source_target_pairs={{0,16},{8,24},{16,0},{24,8},{1,17},{9,25},{17,1},{25,9},{2,18},{10... | collective-permute-start | bytes 393224 | tf_op jit(solution)/shard_map/ppermute | solution.py:247
where the time goes:
time: 113 us
  Pallas kernels  43.7 us (39%)
  waiting for transfers between devices  31.4 us (28%)
  starting transfers between devices  26.6 us (24%)
  local copies, waits for them, and re-layouts  8.02 us (7%)
  matrix products  1.83 us (2%)
  other arithmetic  1.28 us (1%)
    ppermute x24, waiting for transfers between devices, exchange(): return lax.ppermute(value, axis, [(i, i ^ bit) for i in range(size)])  31.4 us
    ppermute x24, starting transfers between devices, exchange(): return lax.ppermute(value, axis, [(i, i ^ bit) for i in range(size)])  26.6 us
    pallas_call x2, Pallas kernels, scores_of(): pl.pallas_call(functools.partial(score_kernel, pieces, groups), grid=(cou...  18.6 us
    pallas_call x2, Pallas kernels, back_of(): pl.pallas_call(functools.partial(back_kernel, groups), grid=(count,), in_...  16 us
    pallas_call x1, Pallas kernels, relay(): pl.pallas_call(relay_kernel, grid=(per // rows,), in_specs=[pl.BlockSpec(...  7.84 us
    unnamed x7, local copies, waits for them, and re-layouts  4.18 us
  transfers between devices with their start and end apart: 24, of which 6 were waited for; matrix products, arithmetic and copies ran while one was open for 5% of the time, Pallas kernels for 22%

commit v1 on v0

--- a/solution.py
+++ b/solution.py
@@ -15,15 +15,23 @@
 LANES = 128
 PAIR = 2 * LANES
 RS_CHUNKS = 1
-WIRE = jnp.float32
+WIRE = jnp.float16
 VMEM_LIMIT = 24 << 20
 
 PARAMS = pltpu.CompilerParams(vmem_limit_bytes=VMEM_LIMIT)
 
 
-def relay_kernel(in_ref, out_ref, wide_ref):
+def relay_kernel(in_ref, out_ref, peak_ref, wide_ref):
     count, rows, _ = in_ref.shape
-    wide_ref[...] = in_ref[...].astype(jnp.float32).reshape(count * rows, LANES)
+    wide = in_ref[...].astype(jnp.float32)
+    wide_ref[...] = wide.reshape(count * rows, LANES)
+    peak = jnp.max(jnp.abs(wide), axis=0)
+
+    @pl.when(pl.program_id(0) == 0)
+    def _():
+        peak_ref[...] = jnp.zeros_like(peak_ref)
+
+    peak_ref[...] = jnp.maximum(peak_ref[...], peak)
     for r in range(rows):
         picked = wide_ref[pl.ds(r, count, stride=rows), :]
         out_ref[:, r * LANES : (r + 1) * LANES] = picked.astype(jnp.bfloat16)
@@ -39,8 +47,14 @@
         relay_kernel,
         grid=(per // rows,),
         in_specs=[pl.BlockSpec((count, rows, LANES), lambda i: (0, i, 0))],
-        out_specs=pl.BlockSpec((count, rows * LANES), lambda i: (0, i)),
-        out_shape=jax.ShapeDtypeStruct((count, per * LANES), jnp.bfloat16),
+        out_specs=(
+            pl.BlockSpec((count, rows * LANES), lambda i: (0, i)),
+            pl.BlockSpec((rows, LANES), lambda i: (0, 0)),
+        ),
+        out_shape=(
+            jax.ShapeDtypeStruct((count, per * LANES), jnp.bfloat16),
+            jax.ShapeDtypeStruct((rows, LANES), jnp.float32),
+        ),
         scratch_shapes=[pltpu.VMEM((count * rows, LANES), jnp.float32)],
         compiler_params=PARAMS,
         cost_estimate=pl.CostEstimate(
@@ -267,7 +281,7 @@
     own_set += [exchange(row_set, "col", cols, 2 * d) for d in range(1, quads)]
     other_set = [exchange(value, "col", cols, 1) for value in own_set]
 
-    x = relay(images)
+    x, peaks = relay(images)
 
     position = jnp.arange(2 * held, dtype=jnp.int32)
     at_local = position % local
@@ -303,34 +317,49 @@
         own_scores, other_scores, precision, shifts
     )
 
-    def reduce_to_owner(own, other, wire):
-        def send(value, axis, size, bit):
-            return exchange(value.astype(wire), axis, size, bit).astype(jnp.float32)
-
+    peak = math.sqrt(2.0) * jnp.max(peaks)
+
+    def send(held_rows, axis, size, bit):
+        value, total, bound = held_rows
+        power = jnp.ceil(jnp.log2(jnp.maximum(bound, 1e-30))) - 15.0
+        at = jnp.arange(LANES, dtype=jnp.int32)[None, :]
+        extra = jnp.where(at == 0, total, jnp.where(at == 1, power, 0.0))
+        payload = jnp.concatenate([value * jnp.exp2(-power), extra], axis=1)
+        got = exchange(payload.astype(WIRE), axis, size, bit).astype(jnp.float32)
+        span = value.shape[1]
+        total, power = got[:, span : span + 1], got[:, span + 1 : span + 2]
+        return got[:, :span] * jnp.exp2(power), total, jnp.exp2(power + 15.0)
+
+    def add(first, *others):
+        for other in others:
+            first = tuple(a + b for a, b in zip(first, other))
+        return first
+
+    def cut(held_rows, at, count):
+        return tuple(value[at * count : (at + 1) * count] for value in held_rows)
+
+    def reduce_to_owner(own, other):
         got = send(other, "col", cols, 1)
-        total = own + got
+        whole = add(own, got)
         per = local * rows
-        part = total[:per]
+        got = [send(cut(whole, d, per), "col", cols, 2 * d) for d in range(1, quads)]
+        whole = add(cut(whole, 0, per), *got)
         got = [
-            send(total[d * per : (d + 1) * per], "col", cols, 2 * d)
-            for d in range(1, quads)
+            send(cut(whole, d, local), "row", rows, d) for d in range(1, rows)
         ]
-        part = sum(got, part)
-        got = [
-            send(part[d * local : (d + 1) * local], "row", rows, d)
-            for d in range(1, rows)
-        ]
-        return sum(got, part[:local])
-
-    totals = reduce_to_owner(own_total, other_total, jnp.float32)
+        return add(cut(whole, 0, local), *got)
+
     results = []
     for b in range(RS_CHUNKS):
         other = back_of(other_w, x, start, steps, 1, b, RS_CHUNKS)
         own = back_of(own_w, x, start, steps, 0, b, RS_CHUNKS)
         span = width // RS_CHUNKS
-        summed = reduce_to_owner(own, other, WIRE)
+        own_sum, other_sum = own_total[:, :1], other_total[:, :1]
+        summed, totals, _ = reduce_to_owner(
+            (own, own_sum, own_sum * peak), (other, other_sum, other_sum * peak)
+        )
         prior = mine[:, b * span : (b + 1) * span].astype(jnp.float32)
-        results.append((summed + PRIOR_WEIGHT * prior) / (totals[:, :1] + PRIOR_WEIGHT))
+        results.append((summed + PRIOR_WEIGHT * prior) / (totals + PRIOR_WEIGHT))
     out = results[0] if RS_CHUNKS == 1 else jnp.concatenate(results, axis=1)
     out = out.reshape(local, groups, parts, LANES).transpose(0, 2, 1, 3)
     return out.reshape(local, parts, coeffs)

time: 113 us -> 102 us (0.903)
  waiting for transfers between devices: 31.4 us -> 16.6 us
  starting transfers between devices: 26.6 us -> 18.5 us
  local copies, waits for them, and re-layouts: 8.02 us -> 14.7 us
  other arithmetic: 1.28 us -> 4.93 us
    ppermute x24 -> x17, waiting for transfers between devices: 31.4 us -> 16.6 us  [exchange(): return lax.ppermute(value, axis, [(i, i ^ bit) for i in range(size)])]
    ppermute x24 -> x17, starting transfers between devices: 26.6 us -> 18.5 us  [exchange(): return lax.ppermute(value, axis, [(i, i ^ bit) for i in range(size)])]
    unnamed x7 -> x15, local copies, waits for them, and re-layouts: 4.18 us -> 10.8 us
  transfers between devices with their start and end apart: 24 -> 17, of which waited for: 6 -> 6; matrix products, arithmetic and copies ran while one was open for 5% -> 6% of each run, Pallas kernels for 22% -> 25%
where the time goes in v1:
time: 102 us
  Pallas kernels  44.2 us (43%)
  starting transfers between devices  18.5 us (18%)
  waiting for transfers between devices  16.6 us (16%)
  local copies, waits for them, and re-layouts  14.7 us (14%)
  other arithmetic  4.93 us (5%)
  matrix products  1.83 us (2%)
  between operations  1.06 us (1%)
    pallas_call x2, Pallas kernels, scores_of(): pl.pallas_call(functools.partial(score_kernel, pieces, groups), grid=(cou...  18.6 us
    ppermute x17, starting transfers between devices, exchange(): return lax.ppermute(value, axis, [(i, i ^ bit) for i in range(size)])  18.5 us
    ppermute x17, waiting for transfers between devices, exchange(): return lax.ppermute(value, axis, [(i, i ^ bit) for i in range(size)])  16.6 us
    pallas_call x2, Pallas kernels, back_of(): pl.pallas_call(functools.partial(back_kernel, groups), grid=(count,), in_...  15.9 us
    unnamed x15, local copies, waits for them, and re-layouts  10.8 us
    pallas_call x1, Pallas kernels, relay(): pl.pallas_call(relay_kernel, grid=(per // rows,), in_specs=[pl.BlockSpec(...  8.42 us
  transfers between devices with their start and end apart: 17, of which 6 were waited for; matrix products, arithmetic and copies ran while one was open for 6% of the time, Pallas kernels for 25%

profile of v1, /device:TPU:0, one launch (start us, length us, event | category | flops | bytes accessed | tf_op | source)
XLA Modules:
  0.0 101.9 jit_solution(14552002287664344757)
XLA Ops:
  0.0 0.9 reshape.399
  0.9 5.1 %collective-permute-start.2 = (bf16[4,8192]{1,0:T(4,128)(2,1)S(1)}, bf16[4,8192]{1,0:T(4,128)(2,1)S(1)}, u32[]{:S(2)}, u32[]{:S(2)}) collective-permute-start(bf16[4,8192]{1,0:T(4,128)(2,1)S(1)} %reshape.399), channel_id=1, source_target_pairs={{0,24},{8,16},{16,8},{24,0},{1,25},{9,17},{17,9},{25,1},{2,26},{10... | collective-permute-start | bytes 196616 | tf_op jit(solution)/shard_map/ppermute | solution.py:261
  6.0 0.6 collective-permute-start
  6.7 1.2 %gather_fusion = s32[128]{0:T(128)S(1)} fusion(s32[128]{0:T(128)S(1)} %copy-done, s32[1024]{0:T(1024)S(1)} %pad_clamp_fusion.1), kind=kCustom, calls=%fused_computation | custom fusion | bytes 1536 | tf_op jit(solution)/shard_map/gather | solution.py:292
  8.0 0.8 copy.11
  8.8 0.6 gather_fusion.1
  9.7 0.2 fusion.24
  9.9 0.5 fusion.7
  10.4 0.5 fusion.9
  10.9 0.5 fusion.8
  11.3 0.3 collective-permute-done.1
  11.8 2.5 %collective-permute-start.5 = (bf16[16,8192]{1,0:T(8,128)(2,1)S(1)}, bf16[16,8192]{1,0:T(8,128)(2,1)S(1)}, u32[]{:S(2)}, u32[]{:S(2)}) collective-permute-start(bf16[16,8192]{1,0:T(8,128)(2,1)S(1)} %pad_maximum_fusion.4.refs_0_), channel_id=1, source_target_pairs={{0,6},{1,7},{2,4},{3,5},{4,2},{5,3},{6,0},{7,1},{8,14},{9,15},{10,... | collective-permute-start | bytes 786440 | tf_op jit(solution)/shard_map/ppermute | solution.py:261
  14.3 0.5 collective-permute-start.4
  14.8 0.5 collective-permute-start.3
  15.4 3.4 %copy-done.1 = bf16[512,2,4096]{2,1,0:T(2,128)(2,1)S(1)} copy-done((bf16[512,2,4096]{2,1,0:T(2,128)(2,1)S(1)}, bf16[512,2,4096]{2,1,0:T(2,128)(2,1)}, u32[]{:S(2)}) %copy-start.1) | copy-done | bytes 8388632
  18.7 8.4 %shard_map.55 = (bf16[512,8192]{1,0:T(8,128)(2,1)S(1)}, f32[8,128]{1,0:T(8,128)S(1)}) custom-call(bf16[512,64,128]{2,1,0:T(8,128)(2,1)S(1)} %bitcast.28), custom_call_target="tpu_custom_call" | custom-call | flops 4194304 | bytes 16777216 | tf_op jit(solution)/shard_map/pallas_call | solution.py:46
  27.2 3.2 %copy-done.3 = bf16[512,8192]{1,0:T(8,128)(2,1)} copy-done((bf16[512,8192]{1,0:T(8,128)(2,1)}, bf16[512,8192]{1,0:T(8,128)(2,1)S(1)}, u32[]{:S(2)}) %copy-start.3) | copy-done | bytes 8388632
  30.4 0.6 reduce_max.9
  31.6 0.5 fusion.10
  32.2 0.5 collective-permute-start.9
  32.8 0.4 collective-permute-start.7
  33.2 3.4 %copy-done.4 = bf16[512,8192]{1,0:T(8,128)(2,1)S(1)} copy-done((bf16[512,8192]{1,0:T(8,128)(2,1)S(1)}, bf16[512,8192]{1,0:T(8,128)(2,1)}, u32[]{:S(2)}) %copy-start.4) | copy-done | bytes 8388632
  36.6 9.3 %shard_map.56 = (f32[512,512]{1,0:T(8,128)S(1)}, f32[64,128]{1,0:T(8,128)S(1)}) custom-call(bf16[16,8192]{1,0:T(8,128)(2,1)S(1)} %pad_maximum_fusion.4.refs_0_, bf16[16,8192]{1,0:T(8,128)(2,1)S(1)} %collective-permute-done.3.refs_1_, bf16[16,8192]{1,0:T(8,128)(2,1)S(1)} %collective-permute-done.4.refs_2_, ...), custom_call_target="tpu_custom_call" | custom-call | flops 4294967296 | bytes 10485760 | tf_op jit(solution)/shard_map/pallas_call | solution.py:124
  45.9 9.3 %shard_map.57 = (f32[512,512]{1,0:T(8,128)S(1)}, f32[64,128]{1,0:T(8,128)S(1)}) custom-call(bf16[16,8192]{1,0:T(8,128)(2,1)S(1)} %collective-permute-done.6.refs_0_, bf16[16,8192]{1,0:T(8,128)(2,1)S(1)} %collective-permute-done.7.refs_1_, bf16[16,8192]{1,0:T(8,128)(2,1)S(1)} %collective-permute-done.8.refs_2_, ...), custom_call_target="tpu_custom_call" | custom-call | flops 4294967296 | bytes 10485760 | tf_op jit(solution)/shard_map/pallas_call | solution.py:124
  55.2 1.3 %shard_map.58 = (bf16[8,64,512]{2,1,0:T(8,128)(2,1)S(1)}, bf16[8,64,512]{2,1,0:T(8,128)(2,1)S(1)}, f32[64,128]{1,0:T(8,128)S(1)}, f32[64,128]{1,0:T(8,128)S(1)}) custom-call(f32[8,64,512]{2,1,0:T(8,128)S(1)} %bitcast.29, f32[8,64,512]{2,1,0:T(8,128)S(1)} %bitcast.30, f32[64,128]{1,0:T(8,128)S(1)} %get-tuple-element.18.own_norm, ...), custom_call_target="tpu_custom_call" | custom-call | flops 5242880 | bytes 3145728 | tf_op jit(solution)/shard_map/pallas_call | solution.py:177
  56.6 8.0 %shard_map.60 = f32[64,8192]{1,0:T(8,128)S(1)} custom-call(bf16[512,512]{1,0:T(8,128)(2,1)S(1)} %bitcast.51, bf16[512,8192]{1,0:T(8,128)(2,1)S(1)} %bitcast.49, f32[8,128,128]{2,1,0:T(8,128)S(1)} %bitcast.45, f32[8,128,128]{2,1,0:T(8,128)S(1)} %bitcast.37, f32[8,128,128]{2,1,0:T(8,128)S(1)} %bitcast.41, f32[8,128,128]{2,1,0:T(8,128)S(1)} %bitcast.33), custom_call_target="tpu_custom_call" | custom-call | flops 4294967296 | bytes 11010048 | tf_op jit(solution)/shard_map/pallas_call | solution.py:237
  64.8 0.2 multiply_convert_fusion
  65.1 0.2 pad_maximum_fusion
  65.5 7.9 %shard_map.59 = f32[64,8192]{1,0:T(8,128)S(1)} custom-call(bf16[512,512]{1,0:T(8,128)(2,1)S(1)} %bitcast.50, bf16[512,8192]{1,0:T(8,128)(2,1)S(1)} %bitcast.49, f32[8,128,128]{2,1,0:T(8,128)S(1)} %bitcast.46, f32[8,128,128]{2,1,0:T(8,128)S(1)} %bitcast.38, f32[8,128,128]{2,1,0:T(8,128)S(1)} %bitcast.42, f32[8,128,128]{2,1,0:T(8,128)S(1)} %bitcast.34), custom_call_target="tpu_custom_call" | custom-call | flops 4294967296 | bytes 11010048 | tf_op jit(solution)/shard_map/pallas_call | solution.py:237
  73.9 0.2 exponential_reduce_fusion.7
  74.2 0.4 fusion
  74.5 0.2 fusion.6
  74.9 1.6 %collective-permute-start.12 = (f16[16,8320]{1,0:T(8,128)(2,1)S(1)}, f16[16,8320]{1,0:T(8,128)(2,1)S(1)}, u32[]{:S(2)}, u32[]{:S(2)}) collective-permute-start(f16[16,8320]{1,0:T(8,128)(2,1)S(1)} %pad_maximum_fusion.2), channel_id=1, source_target_pairs={{0,4},{1,5},{2,6},{3,7},{4,0},{5,1},{6,2},{7,3},{8,12},{9,13},{10,... | collective-permute-start | bytes 798728 | tf_op jit(solution)/shard_map/ppermute | solution.py:261
  76.5 1.5 %collective-permute-start.13 = (f16[16,8320]{1,0:T(8,128)(2,1)S(1)}, f16[16,8320]{1,0:T(8,128)(2,1)S(1)}, u32[]{:S(2)}, u32[]{:S(2)}) collective-permute-start(f16[16,8320]{1,0:T(8,128)(2,1)S(1)} %pad_maximum_fusion.3), channel_id=1, source_target_pairs={{0,6},{1,7},{2,4},{3,5},{4,2},{5,3},{6,0},{7,1},{8,14},{9,15},{10,... | collective-permute-start | bytes 798728 | tf_op jit(solution)/shard_map/ppermute | solution.py:261
  78.1 0.6 collective-permute-start.11
  78.7 10.7 %collective-permute-done.12 = f16[16,8320]{1,0:T(8,128)(2,1)S(1)} collective-permute-done((f16[16,8320]{1,0:T(8,128)(2,1)S(1)}, f16[16,8320]{1,0:T(8,128)(2,1)S(1)}, u32[]{:S(2)}, u32[]{:S(2)}) %collective-permute-start.12) | collective-permute-done | bytes 266272 | tf_op jit(solution)/shard_map/ppermute | solution.py:261
  89.5 1.3 %collective-permute-done.11 = f16[16,8320]{1,0:T(8,128)(2,1)S(1)} collective-permute-done((f16[16,8320]{1,0:T(8,128)(2,1)S(1)}, f16[16,8320]{1,0:T(8,128)(2,1)S(1)}, u32[]{:S(2)}, u32[]{:S(2)}) %collective-permute-start.11) | collective-permute-done | bytes 266272 | tf_op jit(solution)/shard_map/ppermute | solution.py:261
  90.8 0.2 slice_add_fusion.1
  91.0 0.2 exponential_reduce_fusion.10
  91.4 0.2 fusion.1
  91.9 2.1 %collective-permute-start.15 = (f16[4,8320]{1,0:T(4,128)(2,1)S(1)}, f16[4,8320]{1,0:T(4,128)(2,1)S(1)}, u32[]{:S(2)}, u32[]{:S(2)}) collective-permute-start(f16[4,8320]{1,0:T(4,128)(2,1)S(1)} %pad_maximum_fusion.6), channel_id=1, source_target_pairs={{0,16},{8,24},{16,0},{24,8},{1,17},{9,25},{17,1},{25,9},{2,18},{10... | collective-permute-start | bytes 199688 | tf_op jit(solution)/shard_map/ppermute | solution.py:261
  94.1 1.5 %collective-permute-start.16 = (f16[4,8320]{1,0:T(4,128)(2,1)S(1)}, f16[4,8320]{1,0:T(4,128)(2,1)S(1)}, u32[]{:S(2)}, u32[]{:S(2)}) collective-permute-start(f16[4,8320]{1,0:T(4,128)(2,1)S(1)} %pad_maximum_fusion.7), channel_id=1, source_target_pairs={{0,24},{8,16},{16,8},{24,0},{1,25},{9,17},{17,9},{25,1},{2,26},{10... | collective-permute-start | bytes 199688 | tf_op jit(solution)/shard_map/ppermute | solution.py:261
  95.6 0.6 collective-permute-start.14
  96.3 2.4 %collective-permute-done.15 = f16[4,8320]{1,0:T(4,128)(2,1)S(1)} collective-permute-done((f16[4,8320]{1,0:T(4,128)(2,1)S(1)}, f16[4,8320]{1,0:T(4,128)(2,1)S(1)}, u32[]{:S(2)}, u32[]{:S(2)}) %collective-permute-start.15) | collective-permute-done | bytes 66592 | tf_op jit(solution)/shard_map/ppermute | solution.py:261
  98.7 1.6 %collective-permute-done.16 = f16[4,8320]{1,0:T(4,128)(2,1)S(1)} collective-permute-done((f16[4,8320]{1,0:T(4,128)(2,1)S(1)}, f16[4,8320]{1,0:T(4,128)(2,1)S(1)}, u32[]{:S(2)}, u32[]{:S(2)}) %collective-permute-start.16) | collective-permute-done | bytes 66592 | tf_op jit(solution)/shard_map/ppermute | solution.py:261
  100.3 0.4 collective-permute-done.14
  100.7 0.2 fusion.64
  101.1 0.8 reshape.411
  (61 shorter events, 2.7 us)
Async XLA Ops:
  0.0 6.7 %copy-start = (s32[128]{0:T(128)S(1)}, s32[128]{0:T(128)}, u32[]{:S(2)}) copy-start(s32[128]{0:T(128)} %param.8) | copy-start | bytes 1540
  0.9 10.5 %collective-permute-start.2 = (bf16[4,8192]{1,0:T(4,128)(2,1)S(1)}, bf16[4,8192]{1,0:T(4,128)(2,1)S(1)}, u32[]{:S(2)}, u32[]{:S(2)}) collective-permute-start(bf16[4,8192]{1,0:T(4,128)(2,1)S(1)} %reshape.399), channel_id=1, source_target_pairs={{0,24},{8,16},{16,8},{24,0},{1,25},{9,17},{17,9},{25,1},{2,26},{10... | collective-permute-start | bytes 196616 | tf_op jit(solution)/shard_map/ppermute | solution.py:261
  6.0 5.6 %collective-permute-start.1 = (bf16[4,8192]{1,0:T(4,128)(2,1)S(1)}, bf16[4,8192]{1,0:T(4,128)(2,1)S(1)}, u32[]{:S(2)}, u32[]{:S(2)}) collective-permute-start(bf16[4,8192]{1,0:T(4,128)(2,1)S(1)} %reshape.399), channel_id=1, source_target_pairs={{0,16},{8,24},{16,0},{24,8},{1,17},{9,25},{17,1},{25,9},{2,18},{10... | collective-permute-start | bytes 196616 | tf_op jit(solution)/shard_map/ppermute | solution.py:261
  6.0 5.6 %collective-permute-start = (bf16[4,8192]{1,0:T(4,128)(2,1)S(1)}, bf16[4,8192]{1,0:T(4,128)(2,1)S(1)}, u32[]{:S(2)}, u32[]{:S(2)}) collective-permute-start(bf16[4,8192]{1,0:T(4,128)(2,1)S(1)} %reshape.399), channel_id=1, source_target_pairs={{0,8},{8,0},{16,24},{24,16},{1,9},{9,1},{17,25},{25,17},{2,10},{10... | collective-permute-start | bytes 196616 | tf_op jit(solution)/shard_map/ppermute | solution.py:261
  11.8 20.4 %collective-permute-start.5 = (bf16[16,8192]{1,0:T(8,128)(2,1)S(1)}, bf16[16,8192]{1,0:T(8,128)(2,1)S(1)}, u32[]{:S(2)}, u32[]{:S(2)}) collective-permute-start(bf16[16,8192]{1,0:T(8,128)(2,1)S(1)} %pad_maximum_fusion.4.refs_0_), channel_id=1, source_target_pairs={{0,6},{1,7},{2,4},{3,5},{4,2},{5,3},{6,0},{7,1},{8,14},{9,15},{10,... | collective-permute-start | bytes 786440 | tf_op jit(solution)/shard_map/ppermute | solution.py:261
  14.3 18.4 %collective-permute-start.4 = (bf16[16,8192]{1,0:T(8,128)(2,1)S(1)}, bf16[16,8192]{1,0:T(8,128)(2,1)S(1)}, u32[]{:S(2)}, u32[]{:S(2)}) collective-permute-start(bf16[16,8192]{1,0:T(8,128)(2,1)S(1)} %pad_maximum_fusion.4.refs_0_), channel_id=1, source_target_pairs={{0,4},{1,5},{2,6},{3,7},{4,0},{5,1},{6,2},{7,3},{8,12},{9,13},{10,... | collective-permute-start | bytes 786440 | tf_op jit(solution)/shard_map/ppermute | solution.py:261
  14.8 18.0 %collective-permute-start.3 = (bf16[16,8192]{1,0:T(8,128)(2,1)S(1)}, bf16[16,8192]{1,0:T(8,128)(2,1)S(1)}, u32[]{:S(2)}, u32[]{:S(2)}) collective-permute-start(bf16[16,8192]{1,0:T(8,128)(2,1)S(1)} %pad_maximum_fusion.4.refs_0_), channel_id=1, source_target_pairs={{0,2},{1,3},{2,0},{3,1},{4,6},{5,7},{6,4},{7,5},{8,10},{9,11},{10,... | collective-permute-start | bytes 786440 | tf_op jit(solution)/shard_map/ppermute | solution.py:261
  15.4 3.4 %copy-start.1 = (bf16[512,2,4096]{2,1,0:T(2,128)(2,1)S(1)}, bf16[512,2,4096]{2,1,0:T(2,128)(2,1)}, u32[]{:S(2)}) copy-start(bf16[512,2,4096]{2,1,0:T(2,128)(2,1)} %param.5) | copy-start | bytes 25165828
  27.2 3.2 %copy-start.3 = (bf16[512,8192]{1,0:T(8,128)(2,1)}, bf16[512,8192]{1,0:T(8,128)(2,1)S(1)}, u32[]{:S(2)}) copy-start(bf16[512,8192]{1,0:T(8,128)(2,1)S(1)} %get-tuple-element.15.refs_8_.x_ref) | copy-start | bytes 25165828
  32.1 13.8 %collective-permute-start.6 = (bf16[16,8192]{1,0:T(8,128)(2,1)S(1)}, bf16[16,8192]{1,0:T(8,128)(2,1)S(1)}, u32[]{:S(2)}, u32[]{:S(2)}) collective-permute-start(bf16[16,8192]{1,0:T(8,128)(2,1)S(1)} %pad_maximum_fusion.4.refs_0_), channel_id=1, source_target_pairs={{0,1},{1,0},{2,3},{3,2},{4,5},{5,4},{6,7},{7,6},{8,9},{9,8},{10,11... | collective-permute-start | bytes 786440 | tf_op jit(solution)/shard_map/ppermute | solution.py:261
  32.2 13.7 %collective-permute-start.9 = (bf16[16,8192]{1,0:T(8,128)(2,1)S(1)}, bf16[16,8192]{1,0:T(8,128)(2,1)S(1)}, u32[]{:S(2)}, u32[]{:S(2)}) collective-permute-start(bf16[16,8192]{1,0:T(8,128)(2,1)S(1)} %collective-permute-done.5.refs_3_), channel_id=1, source_target_pairs={{0,1},{1,0},{2,3},{3,2},{4,5},{5,4},{6,7},{7,6},{8,9},{9,8},{10,11... | collective-permute-start | bytes 786440 | tf_op jit(solution)/shard_map/ppermute | solution.py:261
  32.7 13.2 %collective-permute-start.8 = (bf16[16,8192]{1,0:T(8,128)(2,1)S(1)}, bf16[16,8192]{1,0:T(8,128)(2,1)S(1)}, u32[]{:S(2)}, u32[]{:S(2)}) collective-permute-start(bf16[16,8192]{1,0:T(8,128)(2,1)S(1)} %collective-permute-done.4.refs_2_), channel_id=1, source_target_pairs={{0,1},{1,0},{2,3},{3,2},{4,5},{5,4},{6,7},{7,6},{8,9},{9,8},{10,11... | collective-permute-start | bytes 786440 | tf_op jit(solution)/shard_map/ppermute | solution.py:261
  32.8 13.1 %collective-permute-start.7 = (bf16[16,8192]{1,0:T(8,128)(2,1)S(1)}, bf16[16,8192]{1,0:T(8,128)(2,1)S(1)}, u32[]{:S(2)}, u32[]{:S(2)}) collective-permute-start(bf16[16,8192]{1,0:T(8,128)(2,1)S(1)} %collective-permute-done.3.refs_1_), channel_id=1, source_target_pairs={{0,1},{1,0},{2,3},{3,2},{4,5},{5,4},{6,7},{7,6},{8,9},{9,8},{10,11... | collective-permute-start | bytes 786440 | tf_op jit(solution)/shard_map/ppermute | solution.py:261
  33.2 3.4 %copy-start.4 = (bf16[512,8192]{1,0:T(8,128)(2,1)S(1)}, bf16[512,8192]{1,0:T(8,128)(2,1)}, u32[]{:S(2)}) copy-start(bf16[512,8192]{1,0:T(8,128)(2,1)} %copy-done.3) | copy-start | bytes 25165828
  36.6 20.0 %slice-start = ((s8[8388608]{0:T(1024)(128)(4,1)}), s8[4194304]{0:T(1024)(128)(4,1)S(1)}, s32[]{:S(2)}) async-start(s8[8388608]{0:T(1024)(128)(4,1)} %bitcast.48), calls=%async_computation | async-start | bytes 8388608
  45.9 9.4 %copy-start.2 = (f32[512]{0:T(512)S(1)}, f32[512]{0:T(512)}, u32[]{:S(2)}) copy-start(f32[512]{0:T(512)} %param.6) | copy-start | bytes 6148
  45.9 10.7 %slice-start.1 = ((s8[8388608]{0:T(1024)(128)(4,1)}), s8[4194304]{0:T(1024)(128)(4,1)S(1)}, s32[]{:S(2)}) async-start(s8[8388608]{0:T(1024)(128)(4,1)} %bitcast.48), calls=%async_computation.1 | async-start | bytes 8388608
  65.4 8.1 %collective-permute-start.10 = (f16[64,8320]{1,0:T(8,128)(2,1)S(1)}, f16[64,8320]{1,0:T(8,128)(2,1)S(1)}, u32[]{:S(2)}, u32[]{:S(2)}) collective-permute-start(f16[64,8320]{1,0:T(8,128)(2,1)S(1)} %pad_maximum_fusion), channel_id=1, source_target_pairs={{0,1},{1,0},{2,3},{3,2},{4,5},{5,4},{6,7},{7,6},{8,9},{9,8},{10,11... | collective-permute-start | bytes 3194888 | tf_op jit(solution)/shard_map/ppermute | solution.py:261
  74.9 14.5 %collective-permute-start.12 = (f16[16,8320]{1,0:T(8,128)(2,1)S(1)}, f16[16,8320]{1,0:T(8,128)(2,1)S(1)}, u32[]{:S(2)}, u32[]{:S(2)}) collective-permute-start(f16[16,8320]{1,0:T(8,128)(2,1)S(1)} %pad_maximum_fusion.2), channel_id=1, source_target_pairs={{0,4},{1,5},{2,6},{3,7},{4,0},{5,1},{6,2},{7,3},{8,12},{9,13},{10,... | collective-permute-start | bytes 798728 | tf_op jit(solution)/shard_map/ppermute | solution.py:261
  76.5 12.9 %collective-permute-start.13 = (f16[16,8320]{1,0:T(8,128)(2,1)S(1)}, f16[16,8320]{1,0:T(8,128)(2,1)S(1)}, u32[]{:S(2)}, u32[]{:S(2)}) collective-permute-start(f16[16,8320]{1,0:T(8,128)(2,1)S(1)} %pad_maximum_fusion.3), channel_id=1, source_target_pairs={{0,6},{1,7},{2,4},{3,5},{4,2},{5,3},{6,0},{7,1},{8,14},{9,15},{10,... | collective-permute-start | bytes 798728 | tf_op jit(solution)/shard_map/ppermute | solution.py:261
  78.1 12.6 %collective-permute-start.11 = (f16[16,8320]{1,0:T(8,128)(2,1)S(1)}, f16[16,8320]{1,0:T(8,128)(2,1)S(1)}, u32[]{:S(2)}, u32[]{:S(2)}) collective-permute-start(f16[16,8320]{1,0:T(8,128)(2,1)S(1)} %pad_maximum_fusion.1), channel_id=1, source_target_pairs={{0,2},{1,3},{2,0},{3,1},{4,6},{5,7},{6,4},{7,5},{8,10},{9,11},{10,... | collective-permute-start | bytes 798728 | tf_op jit(solution)/shard_map/ppermute | solution.py:261
  91.9 6.8 %collective-permute-start.15 = (f16[4,8320]{1,0:T(4,128)(2,1)S(1)}, f16[4,8320]{1,0:T(4,128)(2,1)S(1)}, u32[]{:S(2)}, u32[]{:S(2)}) collective-permute-start(f16[4,8320]{1,0:T(4,128)(2,1)S(1)} %pad_maximum_fusion.6), channel_id=1, source_target_pairs={{0,16},{8,24},{16,0},{24,8},{1,17},{9,25},{17,1},{25,9},{2,18},{10... | collective-permute-start | bytes 199688 | tf_op jit(solution)/shard_map/ppermute | solution.py:261
  94.1 6.2 %collective-permute-start.16 = (f16[4,8320]{1,0:T(4,128)(2,1)S(1)}, f16[4,8320]{1,0:T(4,128)(2,1)S(1)}, u32[]{:S(2)}, u32[]{:S(2)}) collective-permute-start(f16[4,8320]{1,0:T(4,128)(2,1)S(1)} %pad_maximum_fusion.7), channel_id=1, source_target_pairs={{0,24},{8,16},{16,8},{24,0},{1,25},{9,17},{17,9},{25,1},{2,26},{10... | collective-permute-start | bytes 199688 | tf_op jit(solution)/shard_map/ppermute | solution.py:261
  95.6 5.1 %collective-permute-start.14 = (f16[4,8320]{1,0:T(4,128)(2,1)S(1)}, f16[4,8320]{1,0:T(4,128)(2,1)S(1)}, u32[]{:S(2)}, u32[]{:S(2)}) collective-permute-start(f16[4,8320]{1,0:T(4,128)(2,1)S(1)} %pad_maximum_fusion.5), channel_id=1, source_target_pairs={{0,8},{8,0},{16,24},{24,16},{1,9},{9,1},{17,25},{25,17},{2,10},{10... | collective-permute-start | bytes 199688 | tf_op jit(solution)/shard_map/ppermute | solution.py:261

commit v2 on v1

v2 whole, which is shorter than its diff:
```python
import functools
import math

import jax
import jax.numpy as jnp
from jax import lax
from jax.experimental import pallas as pl
from jax.experimental.pallas import tpu as pltpu
from jax.sharding import PartitionSpec as P


GRID = 64
SHIFT_SIDE = 8
PRIOR_WEIGHT = 4.0
LANES = 128
PAIR = 2 * LANES
UNROLL = 4
WIRE = jnp.float16
VMEM_LIMIT = 16 << 20

PARAMS = pltpu.CompilerParams(vmem_limit_bytes=VMEM_LIMIT)


def whole_in_vmem(count):
    return [pl.BlockSpec(memory_space=pltpu.VMEM)] * count


def relay_kernel(rows, in_ref, out_ref, taken_ref, wide_ref, peak_ref, sems):
    count, per, _ = in_ref.shape
    blocks = per // rows
    last = out_ref.shape[0]

    def fetch(block, slot):
        return pltpu.make_async_copy(
            in_ref.at[:, pl.ds(block * rows, rows), :], taken_ref.at[slot], sems.at[slot]
        )

    fetch(0, 0).start()
    peak_ref[...] = jnp.zeros_like(peak_ref)

    def step(block, carry):
        slot = lax.rem(block, 2)

        @pl.when(block + 1 < blocks)
        def _():
            fetch(block + 1, 1 - slot).start()

        fetch(block, slot).wait()
        base = pl.multiple_of(block * rows * LANES, rows * LANES)
        peak = peak_ref[...]
        for n in range(0, count, 16):
            wide = taken_ref[slot, n : n + 16].astype(jnp.float32)
            wide_ref[n * rows : (n + 16) * rows, :] = wide.reshape(16 * rows, LANES)
            peak = jnp.maximum(peak, jnp.max(jnp.abs(wide), axis=0))
            for r in range(rows):
                picked = wide_ref[pl.ds(n * rows + r, 16, stride=rows), :]
                at = pl.ds(base + r * LANES, LANES)
                out_ref[n : n + 16, at] = picked.astype(jnp.bfloat16)
        peak_ref[...] = peak
        return carry

    lax.fori_loop(0, blocks, step, 0)
    peak = jnp.max(peak_ref[...], axis=0, keepdims=True)
    out_ref[count:last, :LANES] = jnp.broadcast_to(peak, (last - count, LANES)).astype(
        jnp.bfloat16
    )


def relay(images, rows=8, spare=16):
    count, parts, coeffs = images.shape
    groups = coeffs // LANES
    per = parts * groups
    flat = images.reshape(count, parts, groups, LANES)
    flat = flat.transpose(0, 2, 1, 3).reshape(count, per, LANES)
    return pl.pallas_call(
        functools.partial(relay_kernel, rows),
        in_specs=[pl.BlockSpec(memory_space=pltpu.HBM)],
        out_specs=pl.BlockSpec(memory_space=pltpu.VMEM),
        out_shape=jax.ShapeDtypeStruct((count + spare, per * LANES), jnp.bfloat16),
        scratch_shapes=[
            pltpu.VMEM((2, count, rows, LANES), jnp.bfloat16),
            pltpu.VMEM((count * rows, LANES), jnp.float32),
            pltpu.VMEM((rows, LANES), jnp.float32),
            pltpu.SemaphoreType.DMA((2,)),
        ],
        compiler_params=pltpu.CompilerParams(vmem_limit_bytes=2 * VMEM_LIMIT),
        cost_estimate=pl.CostEstimate(
            flops=count * per * LANES,
            bytes_accessed=4 * count * per * LANES,
            transcendentals=0,
        ),
    )(flat)


def phase_kernel(shift_ref, table_ref, *refs):
    outs, first_ref = refs[:6], refs[6]
    count, rows, _ = outs[0].shape
    number = table_ref.shape[0]
    rest, parts = table_ref[...], []
    for _ in range(3):
        part = rest.astype(jnp.bfloat16)
        parts.append(part)
        rest = rest - part.astype(jnp.float32)
    parts = jnp.concatenate(parts, axis=0)
    numbers = lax.rem(lax.broadcasted_iota(jnp.int32, (rows, 3 * number), 1), number)
    for half in range(2):
        cos_ref, sin_ref, sign_ref = outs[3 * half : 3 * half + 3]
        chosen = shift_ref[half * rows : (half + 1) * rows, :] == numbers
        first_ref[...] = jnp.dot(
            jnp.where(chosen, 1.0, 0.0).astype(jnp.bfloat16),
            parts,
            preferred_element_type=jnp.float32,
        )

        def step(i, carry, cos_ref=cos_ref, sin_ref=sin_ref, sign_ref=sign_ref):
            here = pl.ds(pl.multiple_of(i * 32, 32), 32)
            c, s = first_ref[here, :LANES], first_ref[here, LANES:PAIR]
            dc, ds = first_ref[here, PAIR : PAIR + LANES], first_ref[here, PAIR + LANES :]
            cos_ref[0, here, :] = c
            sin_ref[0, here, :] = s
            for k in range(1, count):
                c, s = c * dc - s * ds, s * dc + c * ds
                cos_ref[k, here, :] = c
                sin_ref[k, here, :] = s
            c, s = c * dc - s * ds, s * dc + c * ds
            same = c * first_ref[here, :LANES] + s * first_ref[here, LANES:PAIR]
            sign_ref[here, :] = jnp.where(same > 0.0, 1.0, -1.0)
            return carry

        lax.fori_loop(0, rows // 32, step, 0)


def phases_of(shift, table, count, rows):
    held = jax.ShapeDtypeStruct((count, rows, LANES), jnp.float32)
    sign = jax.ShapeDtypeStruct((rows, LANES), jnp.float32)
    out = pl.pallas_call(
        phase_kernel,
        in_specs=whole_in_vmem(2),
        out_specs=tuple(whole_in_vmem(6)),
        out_shape=(held, held, sign) * 2,
        scratch_shapes=[pltpu.VMEM((rows, table.shape[1]), jnp.float32)],
        compiler_params=PARAMS,
        cost_estimate=pl.CostEstimate(
            flops=12 * count * rows * LANES,
            bytes_accessed=16 * count * rows * LANES,
            transcendentals=0,
        ),
    )(shift, table)
    return out[:3], out[3:]


def whole_in_vmem(count):
    return [pl.BlockSpec(memory_space=pltpu.VMEM)] * count


def score_kernel(pieces, shifts, *refs):
    piece_refs = refs[:pieces]
    cos_ref, sin_ref, sign_ref, x_ref = refs[pieces : pieces + 4]
    out_ref, norm_ref, rot_a, rot_b = refs[pieces + 4 :]
    images = out_ref.shape[1]
    piece_rows = piece_refs[0].shape[0]
    held = pieces * piece_rows
    block = rot_a.shape[1]
    per = block // PAIR
    half = cos_ref.shape[0] // per

    norm_ref[...] = jnp.zeros_like(norm_ref)
    out_ref[...] = jnp.zeros_like(out_ref)

    def rotate(index, rot_ref):
        live = index < 2 * half
        index = jnp.minimum(index, 2 * half - 1)
        base = pl.multiple_of(index * block, block)
        phase = lax.rem(index, half) * per
        for g in range(per):
            at = g * PAIR
            for i in range(pieces):
                here = slice(i * piece_rows, (i + 1) * piece_rows)
                real = piece_refs[i][:, pl.ds(base + at, LANES)].astype(jnp.float32)
                imag = piece_refs[i][:, pl.ds(base + at + LANES, LANES)].astype(jnp.float32)
                power = real * real + imag * imag
                norm_ref[here, :] += jnp.where(live, power, 0.0)
                for j in range(shifts):
                    start = j * held + i * piece_rows
                    row = slice(start, start + piece_rows)
                    c, s = cos_ref[phase + g, row, :], sin_ref[phase + g, row, :]
                    rot_ref[row, at : at + LANES] = (real * c + imag * s).astype(jnp.bfloat16)
                    rot_ref[row, at + LANES : at + PAIR] = (imag * c - real * s).astype(
                        jnp.bfloat16
                    )

    def gather_scores(index, rot_ref):
        base = pl.multiple_of(index * block, block)
        out_ref[...] += lax.dot_general(
            rot_ref[...],
            x_ref[0:images, pl.ds(base, block)],
            (((1,), (1,)), ((), ())),
            preferred_element_type=jnp.float32,
        )

    def turn_sign():
        for n in range(images // LANES):
            lanes = slice(n * LANES, (n + 1) * LANES)
            out_ref[:, lanes] = out_ref[:, lanes] * sign_ref[...]

    rotate(jnp.int32(0), rot_a)

    def step(i, carry):
        for at in range(0, UNROLL, 2):
            index = i * UNROLL + at
            gather_scores(index, rot_a)
            rotate(index + 1, rot_b)
            gather_scores(index + 1, rot_b)
            rotate(index + 2, rot_a)
        return carry

    lax.fori_loop(0, half // UNROLL, step, 0)
    turn_sign()
    lax.fori_loop(half // UNROLL, 2 * half // UNROLL, step, 0)
    turn_sign()


def scores_of(piece_list, phases, shifts, x, images, groups=2):
    pieces = len(piece_list)
    rows, width = piece_list[0].shape
    held = pieces * rows
    rotated = pltpu.VMEM((shifts * held, groups * PAIR), jnp.bfloat16)
    return pl.pallas_call(
        functools.partial(score_kernel, pieces, shifts),
        in_specs=whole_in_vmem(pieces + 4),
        out_specs=tuple(whole_in_vmem(2)),
        out_shape=(
            jax.ShapeDtypeStruct((shifts * held, images), jnp.float32),
            jax.ShapeDtypeStruct((held, LANES), jnp.float32),
        ),
        scratch_shapes=[rotated, rotated],
        compiler_params=PARAMS,
        cost_estimate=pl.CostEstimate(
            flops=2 * shifts * held * images * width,
            bytes_accessed=2 * images * width + 8 * shifts * held * images,
            transcendentals=0,
        ),
    )(*piece_list, *phases, x)


def weight_kernel(own_ref, other_ref, own_norm, other_norm, prec_ref, x_ref, *outs):
    outs, raised_refs = outs[:6], outs[6:]
    images = prec_ref.shape[1]
    peak = jnp.max(x_ref[images:, :LANES].astype(jnp.float32)) * math.sqrt(2.0)
    prec = prec_ref[...][None]
    halves = ((own_ref, own_norm), (other_ref, other_norm))
    bias, tops = [], []
    for ref, norm_ref in halves:
        norm = 0.5 * jnp.sum(norm_ref[...], axis=1, keepdims=True)
        bias.append(norm[None])
        value = prec * (ref[...] - norm[None])
        tops.append(jnp.max(jnp.max(value, axis=0), axis=0, keepdims=True))
    top = jnp.maximum(*tops)[None]
    norm = 0.0
    for (ref, _), offset, raised_ref in zip(halves, bias, raised_refs):
        raised = jnp.exp(prec * (ref[...] - offset) - top)
        raised_ref[...] = raised
        norm = norm + jnp.sum(jnp.sum(raised, axis=0), axis=0, keepdims=True)
    inverse = (1.0 / norm)[None]
    for h, ref in enumerate(raised_refs):
        weight = (ref[...] * inverse).astype(jnp.bfloat16)
        outs[h][...] = weight
        wide = weight.astype(jnp.float32)
        total = jnp.sum(jnp.sum(wide, axis=0), axis=1, keepdims=True)
        total = jnp.broadcast_to(total, outs[2 + h].shape)
        outs[2 + h][...] = total
        outs[4 + h][...] = total * peak


def weights_of(own, other, precision, x, shifts):
    rows, images = own[0].shape
    held = rows // shifts
    cube = jax.ShapeDtypeStruct((shifts, held, images), jnp.bfloat16)
    total = jax.ShapeDtypeStruct((held, LANES), jnp.float32)
    own_w, other_w, own_t, other_t, own_b, other_b = pl.pallas_call(
        weight_kernel,
        in_specs=whole_in_vmem(6),
        out_specs=tuple(whole_in_vmem(6)),
        out_shape=(cube, cube, total, total, total, total),
        scratch_shapes=[pltpu.VMEM((shifts, held, images), jnp.float32)] * 2,
        compiler_params=PARAMS,
        cost_estimate=pl.CostEstimate(
            flops=20 * rows * images,
            bytes_accessed=12 * rows * images,
            transcendentals=2 * rows * images,
        ),
    )(
        own[0].reshape(shifts, held, images),
        other[0].reshape(shifts, held, images),
        own[1],
        other[1],
        precision.reshape(1, images),
        x,
    )
    own_w, other_w = own_w.reshape(rows, images), other_w.reshape(rows, images)
    own_sum, other_sum = own_t[:, :1], other_t[:, :1]
    return (own_w, own_sum, own_b[:, :1]), (other_w, other_sum, other_b[:, :1])


def back_kernel(shifts, w_ref, cos_ref, sin_ref, sign_ref, x_ref, out_ref, *scratch):
    turned_ref, mix_a, mix_b = scratch
    rows, images = w_ref.shape
    held = rows // shifts
    count = cos_ref.shape[0]
    for n in range(images // LANES):
        lanes = slice(n * LANES, (n + 1) * LANES)
        wide = w_ref[:, lanes].astype(jnp.float32) * sign_ref[...]
        turned_ref[:, lanes] = wide.astype(jnp.bfloat16)

    def mix(index, mix_ref):
        index = jnp.minimum(index, count - 1)
        for second, ref in enumerate((w_ref, turned_ref)):
            base = pl.multiple_of((second * count + index) * PAIR, PAIR)
            mix_ref[:, second * PAIR : (second + 1) * PAIR] = jnp.dot(
                ref[...], x_ref[0:images, pl.ds(base, PAIR)], preferred_element_type=jnp.float32
            )

    def turn(index, mix_ref):
        for i in range(held // 8):
            here = slice(i * 8, (i + 1) * 8)
            total = [None] * 4
            for j in range(shifts):
                row = slice(j * held + i * 8, j * held + (i + 1) * 8)
                c, s = cos_ref[index, row, :], sin_ref[index, row, :]
                terms = []
                for second in range(2):
                    at = second * PAIR
                    real = mix_ref[row, at : at + LANES]
                    imag = mix_ref[row, at + LANES : at + PAIR]
                    terms += [real * c - imag * s, imag * c + real * s]
                total = [b if a is None else a + b for a, b in zip(total, terms)]
            for part in range(4):
                base = (part // 2 * count + index) * PAIR + part % 2 * LANES
                out_ref[here, pl.ds(pl.multiple_of(base, LANES), LANES)] = total[part]

    mix(jnp.int32(0), mix_a)

    def step(i, carry):
        for at in range(0, UNROLL, 2):
            index = i * UNROLL + at
            mix(index + 1, mix_b)
            turn(index, mix_a)
            mix(index + 2, mix_a)
            turn(index + 1, mix_b)
        return carry

    lax.fori_loop(0, count // UNROLL, step, 0)


def back_of(weight, x, phases, shifts):
    rows, images = weight.shape
    held = rows // shifts
    width = x.shape[1]
    mixed = pltpu.VMEM((rows, 2 * PAIR), jnp.float32)
    return pl.pallas_call(
        functools.partial(back_kernel, shifts),
        in_specs=whole_in_vmem(5),
        out_specs=whole_in_vmem(1)[0],
        out_shape=jax.ShapeDtypeStruct((held, width), jnp.float32),
        scratch_shapes=[pltpu.VMEM((rows, images), jnp.bfloat16), mixed, mixed],
        compiler_params=PARAMS,
        cost_estimate=pl.CostEstimate(
            flops=2 * rows * images * width,
            bytes_accessed=2 * images * width + 2 * rows * images + 4 * held * width,
            transcendentals=0,
        ),
    )(weight, *phases, x)


def exchange(value, axis, size, bit):
    return lax.ppermute(value, axis, [(i, i ^ bit) for i in range(size)])


def body(images, precision, templates, template_id, shift_table):
    image_count, parts, coeffs = images.shape
    local = templates.shape[0]
    shifts = shift_table.shape[1]
    rows, cols = lax.axis_size("row"), lax.axis_size("col")
    quads = cols // 2
    groups = coeffs // LANES
    width = parts * coeffs
    held = local * rows * quads

    mine = templates.reshape(local, parts, groups, LANES)
    mine = mine.transpose(0, 2, 1, 3).reshape(local, width)

    row_set = [mine]
    row_set += [exchange(mine, "row", rows, d) for d in range(1, rows)]
    row_set = jnp.concatenate(row_set, axis=0)
    own_set = [row_set]
    own_set += [exchange(row_set, "col", cols, 2 * d) for d in range(1, quads)]
    other_set = [exchange(value, "col", cols, 1) for value in own_set]

    x = relay(images)

    position = jnp.arange(2 * held, dtype=jnp.int32)
    at_local = position % local
    at_row = (position // local % rows) ^ lax.axis_index("row")
    at_quad = position // (local * rows) % quads
    at_col = (2 * at_quad + position // held) ^ lax.axis_index("col")
    slots = (at_row * cols + at_col) * local + at_local
    shift = shift_table[template_id[slots]].reshape(2, held, shifts)
    shift = shift.transpose(0, 2, 1).reshape(-1, 1)

    number = jnp.arange(SHIFT_SIDE * SHIFT_SIDE, dtype=jnp.int32)[:, None]
    step_x = number // SHIFT_SIDE - SHIFT_SIDE // 2
    step_y = number % SHIFT_SIDE - SHIFT_SIDE // 2
    lane = jnp.arange(LANES, dtype=jnp.int32)[None, :]
    freq_x = lane // GRID - GRID // 2
    freq_y = lane % GRID - GRID // 2
    first = (step_x * freq_x + step_y * freq_y) % GRID
    stride = jnp.broadcast_to(step_x * (LANES // GRID) % GRID, first.shape)
    angle = jnp.concatenate([first, stride], axis=1).astype(jnp.float32)
    angle = angle * (2.0 * math.pi / GRID)
    table = [jnp.cos(angle), jnp.sin(angle)]
    table = [part[:, at : at + LANES] for at in (0, LANES) for part in table]
    table = jnp.concatenate(table, axis=1)
    own_phases, other_phases = phases_of(shift, table, groups // 2, shifts * held)

    own_scores = scores_of(own_set, own_phases, shifts, x, image_count)
    other_scores = scores_of(other_set, other_phases, shifts, x, image_count)
    own, other = weights_of(own_scores, other_scores, precision, x, shifts)

    def send(held_rows, axis, size, bit):
        value, total, bound = held_rows
        power = jnp.ceil(jnp.log2(jnp.maximum(bound, 1e-30))) - 15.0
        at = jnp.arange(LANES, dtype=jnp.int32)[None, :]
        extra = jnp.where(at == 0, total, jnp.where(at == 1, power, 0.0))
        payload = jnp.concatenate([value * jnp.exp2(-power), extra], axis=1)
        got = exchange(payload.astype(WIRE), axis, size, bit).astype(jnp.float32)
        span = value.shape[1]
        total, power = got[:, span : span + 1], got[:, span + 1 : span + 2]
        return got[:, :span] * jnp.exp2(power), total, jnp.exp2(power + 15.0)

    def add(first, *others):
        for other in others:
            first = tuple(a + b for a, b in zip(first, other))
        return first

    def cut(held_rows, at, count):
        return tuple(value[at * count : (at + 1) * count] for value in held_rows)

    def reduce_to_owner(own, other):
        got = send(other, "col", cols, 1)
        whole = add(own, got)
        per = local * rows
        got = [send(cut(whole, d, per), "col", cols, 2 * d) for d in range(1, quads)]
        whole = add(cut(whole, 0, per), *got)
        got = [
            send(cut(whole, d, local), "row", rows, d) for d in range(1, rows)
        ]
        return add(cut(whole, 0, local), *got)

    other_back = back_of(other[0], x, other_phases, shifts)
    own_back = back_of(own[0], x, own_phases, shifts)
    summed, totals, _ = reduce_to_owner(
        (own_back,) + own[1:], (other_back,) + other[1:]
    )
    prior = mine.astype(jnp.float32)
    out = (summed + PRIOR_WEIGHT * prior) / (totals + PRIOR_WEIGHT)
    out = out.reshape(local, groups, parts, LANES).transpose(0, 2, 1, 3)
    return out.reshape(local, parts, coeffs)


def solution(mesh):
    return jax.shard_map(
        body,
        mesh=mesh,
        in_specs=(
            P(("row", "col"), None, None),
            P(("row", "col")),
            P(("row", "col"), None, None),
            P(),
            P(),
        ),
        out_specs=P(("row", "col"), None, None),
        check_vma=False,
    )
```

time: 102 us -> 89.7 us (0.88)
  Pallas kernels: 44.2 us -> 37 us
  local copies, waits for them, and re-layouts: 14.7 us -> 8.74 us
  waiting for transfers between devices: 16.6 us -> 20.3 us
  matrix products: 1.83 us -> 0 us
    pallas_call x6 -> x7, Pallas kernels: 44.2 us -> 37 us  [the longest x2 14.1 us: scores_of(): pl.pallas_call(functools.partial(score_kernel, pieces, shifts), in_specs=...]
    unnamed x15 -> x7, local copies, waits for them, and re-layouts: 10.8 us -> 4.17 us
    ppermute x17, waiting for transfers between devices: 16.6 us -> 20.3 us  [exchange(): return lax.ppermute(value, axis, [(i, i ^ bit) for i in range(size)])]
    dot_general x4 -> x0, matrix products: 1.83 us -> none  [body(): lax.dot(chosen, table[:, at * LANES:(at + 1) * LANES], precision=lax.Prec...]
  transfers between devices with their start and end apart: 17 -> 17, of which waited for: 6 -> 6; matrix products, arithmetic and copies ran while one was open for 6% -> 5% of each run, Pallas kernels for 25% -> 25%
where the time goes in v2:
time: 89.7 us; the launch traced here: 89.5 us
  Pallas kernels  37 us (41%)
  waiting for transfers between devices  20.3 us (23%)
  starting transfers between devices  18.7 us (21%)
  local copies, waits for them, and re-layouts  8.74 us (10%)
  other arithmetic  4.28 us (5%)
    ppermute x17, waiting for transfers between devices, exchange(): return lax.ppermute(value, axis, [(i, i ^ bit) for i in range(size)])  20.3 us
    ppermute x17, starting transfers between devices, exchange(): return lax.ppermute(value, axis, [(i, i ^ bit) for i in range(size)])  18.7 us
    pallas_call x2, Pallas kernels, scores_of(): pl.pallas_call(functools.partial(score_kernel, pieces, shifts), in_specs=...  14.1 us
    pallas_call x2, Pallas kernels, back_of(): pl.pallas_call(functools.partial(back_kernel, shifts), in_specs=whole_in_...  12.6 us
    pallas_call x1, Pallas kernels, relay(): pl.pallas_call(functools.partial(relay_kernel, rows), in_specs=[pl.BlockS...  6.24 us
    unnamed x7, local copies, waits for them, and re-layouts  4.17 us
    pallas_call x1, Pallas kernels, phases_of(): pl.pallas_call(phase_kernel, in_specs=whole_in_vmem(2), out_specs=tuple(w...  2.78 us
    gather x2, local copies, waits for them, and re-layouts, body(): shift = shift_table[template_id[slots]].reshape(2, held, shifts)  1.87 us
  transfers between devices with their start and end apart: 17, of which 6 were waited for; matrix products, arithmetic and copies ran while one was open for 5% of the time, Pallas kernels for 25%

profile of v2, /device:TPU:0, one launch (start us, length us, event | category | flops | bytes accessed | tf_op | source)
XLA Modules:
  0.0 89.5 jit_solution(13131555633999020343)
XLA Ops:
  0.0 0.9 reshape.391
  0.9 3.1 %collective-permute-start = (bf16[4,8192]{1,0:T(4,128)(2,1)S(1)}, bf16[4,8192]{1,0:T(4,128)(2,1)S(1)}, u32[]{:S(2)}, u32[]{:S(2)}) collective-permute-start(bf16[4,8192]{1,0:T(4,128)(2,1)S(1)} %reshape.391), channel_id=1, source_target_pairs={{0,8},{8,0},{16,24},{24,16},{1,9},{9,1},{17,25},{25,17},{2,10},{10... | collective-permute-start | bytes 196616 | tf_op jit(solution)/shard_map/ppermute | solution.py:376
  4.0 2.6 %collective-permute-start.1 = (bf16[4,8192]{1,0:T(4,128)(2,1)S(1)}, bf16[4,8192]{1,0:T(4,128)(2,1)S(1)}, u32[]{:S(2)}, u32[]{:S(2)}) collective-permute-start(bf16[4,8192]{1,0:T(4,128)(2,1)S(1)} %reshape.391), channel_id=1, source_target_pairs={{0,16},{8,24},{16,0},{24,8},{1,17},{9,25},{17,1},{25,9},{2,18},{10... | collective-permute-start | bytes 196616 | tf_op jit(solution)/shard_map/ppermute | solution.py:376
  6.8 0.2 fusion.17
  7.1 1.2 %gather_fusion = s32[128]{0:T(128)S(1)} fusion(s32[128]{0:T(128)S(1)} %copy-done, s32[1024]{0:T(1024)S(1)} %pad_clamp_fusion.1), kind=kCustom, calls=%fused_computation | custom fusion | bytes 1536 | tf_op jit(solution)/shard_map/gather | solution.py:407
  8.4 2.9 %collective-permute-done.1 = bf16[4,8192]{1,0:T(4,128)(2,1)S(1)} collective-permute-done((bf16[4,8192]{1,0:T(4,128)(2,1)S(1)}, bf16[4,8192]{1,0:T(4,128)(2,1)S(1)}, u32[]{:S(2)}, u32[]{:S(2)}) %collective-permute-start.1) | collective-permute-done | bytes 65568 | tf_op jit(solution)/shard_map/ppermute | solution.py:376
  11.3 1.4 %collective-permute-done.2 = bf16[4,8192]{1,0:T(4,128)(2,1)S(1)} collective-permute-done((bf16[4,8192]{1,0:T(4,128)(2,1)S(1)}, bf16[4,8192]{1,0:T(4,128)(2,1)S(1)}, u32[]{:S(2)}, u32[]{:S(2)}) %collective-permute-start.2) | collective-permute-done | bytes 65568 | tf_op jit(solution)/shard_map/ppermute | solution.py:376
  12.7 0.2 pad_maximum_fusion.4.refs_0_
  12.8 1.6 %collective-permute-start.3 = (bf16[16,8192]{1,0:T(8,128)(2,1)S(1)}, bf16[16,8192]{1,0:T(8,128)(2,1)S(1)}, u32[]{:S(2)}, u32[]{:S(2)}) collective-permute-start(bf16[16,8192]{1,0:T(8,128)(2,1)S(1)} %pad_maximum_fusion.4.refs_0_), channel_id=1, source_target_pairs={{0,2},{1,3},{2,0},{3,1},{4,6},{5,7},{6,4},{7,5},{8,10},{9,11},{10,... | collective-permute-start | bytes 786440 | tf_op jit(solution)/shard_map/ppermute | solution.py:376
  14.4 1.5 %collective-permute-start.4 = (bf16[16,8192]{1,0:T(8,128)(2,1)S(1)}, bf16[16,8192]{1,0:T(8,128)(2,1)S(1)}, u32[]{:S(2)}, u32[]{:S(2)}) collective-permute-start(bf16[16,8192]{1,0:T(8,128)(2,1)S(1)} %pad_maximum_fusion.4.refs_0_), channel_id=1, source_target_pairs={{0,4},{1,5},{2,6},{3,7},{4,0},{5,1},{6,2},{7,3},{8,12},{9,13},{10,... | collective-permute-start | bytes 786440 | tf_op jit(solution)/shard_map/ppermute | solution.py:376
  15.9 0.5 collective-permute-start.5
  16.4 0.8 copy.18
  17.2 0.6 gather_fusion.1
  17.9 0.5 reshape.419.shift_ref
  18.4 3.4 %copy-done.1 = bf16[512,2,4096]{2,1,0:T(2,128)(2,1)S(1)} copy-done((bf16[512,2,4096]{2,1,0:T(2,128)(2,1)S(1)}, bf16[512,2,4096]{2,1,0:T(2,128)(2,1)}, u32[]{:S(2)}) %copy-start.1) | copy-done | bytes 8388632
  21.7 6.2 %shard_map.56.refs_7_.x_ref = bf16[528,8192]{1,0:T(8,128)(2,1)S(1)} custom-call(bf16[512,64,128]{2,1,0:T(8,128)(2,1)S(1)} %bitcast.24), custom_call_target="tpu_custom_call" | custom-call | flops 4194304 | bytes 16777216 | tf_op jit(solution)/shard_map/pallas_call | solution.py:75
  28.0 2.8 %shard_map.55 = (f32[16,512,128]{2,1,0:T(8,128)S(1)}, f32[16,512,128]{2,1,0:T(8,128)S(1)}, f32[512,128]{1,0:T(8,128)S(1)}, f32[16,512,128]{2,1,0:T(8,128)S(1)}, ...) custom-call(s32[1024,1]{1,0:T(8,128)S(1)} %reshape.419.shift_ref, f32[64,512]{1,0:T(8,128)S(1)} %pad_maximum_fusion.5.table_ref), custom_call_target="tpu_custom_call" | custom-call | flops 12582912 | bytes 16777216 | tf_op jit(solution)/shard_map/pallas_call | solution.py:136
  30.9 0.5 collective-permute-start.7
  31.5 0.4 collective-permute-start.9
  31.9 7.0 %shard_map.57 = (f32[512,512]{1,0:T(8,128)S(1)}, f32[64,128]{1,0:T(8,128)S(1)}) custom-call(bf16[16,8192]{1,0:T(8,128)(2,1)S(1)} %pad_maximum_fusion.4.refs_0_, bf16[16,8192]{1,0:T(8,128)(2,1)S(1)} %collective-permute-done.3.refs_1_, bf16[16,8192]{1,0:T(8,128)(2,1)S(1)} %collective-permute-done.4.refs_2_, ...), custom_call_target="tpu_custom_call" | custom-call | flops 4294967296 | bytes 10485760 | tf_op jit(solution)/shard_map/pallas_call | solution.py:228
  39.0 7.0 %shard_map.58 = (f32[512,512]{1,0:T(8,128)S(1)}, f32[64,128]{1,0:T(8,128)S(1)}) custom-call(bf16[16,8192]{1,0:T(8,128)(2,1)S(1)} %collective-permute-done.6.refs_0_, bf16[16,8192]{1,0:T(8,128)(2,1)S(1)} %collective-permute-done.7.refs_1_, bf16[16,8192]{1,0:T(8,128)(2,1)S(1)} %collective-permute-done.8.refs_2_, ...), custom_call_target="tpu_custom_call" | custom-call | flops 4294967296 | bytes 10485760 | tf_op jit(solution)/shard_map/pallas_call | solution.py:228
  46.1 1.3 %shard_map.59 = (bf16[8,64,512]{2,1,0:T(8,128)(2,1)S(1)}, bf16[8,64,512]{2,1,0:T(8,128)(2,1)S(1)}, f32[64,128]{1,0:T(8,128)S(1)}, f32[64,128]{1,0:T(8,128)S(1)},...) custom-call(f32[8,64,512]{2,1,0:T(8,128)S(1)} %bitcast.25, f32[8,64,512]{2,1,0:T(8,128)S(1)} %bitcast.26, ...), custom_call_target="tpu_custom_call" | custom-call | flops 5242880 | bytes 3145728 | tf_op jit(solution)/shard_map/pallas_call | solution.py:280
  47.4 6.4 %shard_map.61 = f32[64,8192]{1,0:T(8,128)S(1)} custom-call(bf16[512,512]{1,0:T(8,128)(2,1)S(1)} %bitcast.28, f32[16,512,128]{2,1,0:T(8,128)S(1)} %get-tuple-element.25.refs_4_.cos_ref, f32[16,512,128]{2,1,0:T(8,128)S(1)} %get-tuple-element.26.refs_5_.sin_ref, f32[512,128]{1,0:T(8,128)S(1)} %get-tuple-element.27.refs_6_.sign_ref, ...), custom_call_target="tpu_custom_call" | custom-call | flops 4294967296 | bytes 11010048 | tf_op jit(solution)/shard_map/pallas_call | solution.py:360
  54.0 0.2 multiply_convert_fusion
  54.4 0.2 pad_maximum_fusion
  54.6 0.2 collective-permute-start.10
  54.8 6.2 %shard_map.60 = f32[64,8192]{1,0:T(8,128)S(1)} custom-call(bf16[512,512]{1,0:T(8,128)(2,1)S(1)} %bitcast.27, f32[16,512,128]{2,1,0:T(8,128)S(1)} %get-tuple-element.21.refs_4_.cos_ref, f32[16,512,128]{2,1,0:T(8,128)S(1)} %get-tuple-element.22.refs_5_.sin_ref, f32[512,128]{1,0:T(8,128)S(1)} %get-tuple-element.23.refs_6_.sign_ref, ...), custom_call_target="tpu_custom_call" | custom-call | flops 4294967296 | bytes 11010048 | tf_op jit(solution)/shard_map/pallas_call | solution.py:360
  61.1 0.2 exponential_reduce_fusion
  61.3 0.2 exponential_reduce_fusion.7
  61.5 0.1 slice_reduce_fusion.3
  61.7 0.4 fusion
  62.1 0.2 fusion.6
  62.4 1.6 %collective-permute-start.11 = (f16[16,8320]{1,0:T(8,128)(2,1)S(1)}, f16[16,8320]{1,0:T(8,128)(2,1)S(1)}, u32[]{:S(2)}, u32[]{:S(2)}) collective-permute-start(f16[16,8320]{1,0:T(8,128)(2,1)S(1)} %pad_maximum_fusion.1), channel_id=1, source_target_pairs={{0,2},{1,3},{2,0},{3,1},{4,6},{5,7},{6,4},{7,5},{8,10},{9,11},{10,... | collective-permute-start | bytes 798728 | tf_op jit(solution)/shard_map/ppermute | solution.py:376
  64.1 1.6 %collective-permute-start.12 = (f16[16,8320]{1,0:T(8,128)(2,1)S(1)}, f16[16,8320]{1,0:T(8,128)(2,1)S(1)}, u32[]{:S(2)}, u32[]{:S(2)}) collective-permute-start(f16[16,8320]{1,0:T(8,128)(2,1)S(1)} %pad_maximum_fusion.2), channel_id=1, source_target_pairs={{0,4},{1,5},{2,6},{3,7},{4,0},{5,1},{6,2},{7,3},{8,12},{9,13},{10,... | collective-permute-start | bytes 798728 | tf_op jit(solution)/shard_map/ppermute | solution.py:376
  65.7 0.5 collective-permute-start.13
  66.3 5.5 %collective-permute-done.11 = f16[16,8320]{1,0:T(8,128)(2,1)S(1)} collective-permute-done((f16[16,8320]{1,0:T(8,128)(2,1)S(1)}, f16[16,8320]{1,0:T(8,128)(2,1)S(1)}, u32[]{:S(2)}, u32[]{:S(2)}) %collective-permute-start.11) | collective-permute-done | bytes 266272 | tf_op jit(solution)/shard_map/ppermute | solution.py:376
  71.8 6.4 %collective-permute-done.12 = f16[16,8320]{1,0:T(8,128)(2,1)S(1)} collective-permute-done((f16[16,8320]{1,0:T(8,128)(2,1)S(1)}, f16[16,8320]{1,0:T(8,128)(2,1)S(1)}, u32[]{:S(2)}, u32[]{:S(2)}) %collective-permute-start.12) | collective-permute-done | bytes 266272 | tf_op jit(solution)/shard_map/ppermute | solution.py:376
  78.4 0.2 slice_add_fusion.1
  78.6 0.2 exponential_reduce_fusion.10
  78.9 0.2 fusion.1
  79.2 0.2 fusion.14
  79.6 2.4 %collective-permute-start.15 = (f16[4,8320]{1,0:T(4,128)(2,1)S(1)}, f16[4,8320]{1,0:T(4,128)(2,1)S(1)}, u32[]{:S(2)}, u32[]{:S(2)}) collective-permute-start(f16[4,8320]{1,0:T(4,128)(2,1)S(1)} %pad_maximum_fusion.7), channel_id=1, source_target_pairs={{0,16},{8,24},{16,0},{24,8},{1,17},{9,25},{17,1},{25,9},{2,18},{10... | collective-permute-start | bytes 199688 | tf_op jit(solution)/shard_map/ppermute | solution.py:376
  82.1 2.1 %collective-permute-start.16 = (f16[4,8320]{1,0:T(4,128)(2,1)S(1)}, f16[4,8320]{1,0:T(4,128)(2,1)S(1)}, u32[]{:S(2)}, u32[]{:S(2)}) collective-permute-start(f16[4,8320]{1,0:T(4,128)(2,1)S(1)} %pad_maximum_fusion.8), channel_id=1, source_target_pairs={{0,24},{8,16},{16,8},{24,0},{1,25},{9,17},{17,9},{25,1},{2,26},{10... | collective-permute-start | bytes 199688 | tf_op jit(solution)/shard_map/ppermute | solution.py:376
  84.2 2.9 %collective-permute-done.15 = f16[4,8320]{1,0:T(4,128)(2,1)S(1)} collective-permute-done((f16[4,8320]{1,0:T(4,128)(2,1)S(1)}, f16[4,8320]{1,0:T(4,128)(2,1)S(1)}, u32[]{:S(2)}, u32[]{:S(2)}) %collective-permute-start.15) | collective-permute-done | bytes 66592 | tf_op jit(solution)/shard_map/ppermute | solution.py:376
  87.1 1.2 %collective-permute-done.16 = f16[4,8320]{1,0:T(4,128)(2,1)S(1)} collective-permute-done((f16[4,8320]{1,0:T(4,128)(2,1)S(1)}, f16[4,8320]{1,0:T(4,128)(2,1)S(1)}, u32[]{:S(2)}, u32[]{:S(2)}) %collective-permute-start.16) | collective-permute-done | bytes 66592 | tf_op jit(solution)/shard_map/ppermute | solution.py:376
  88.3 0.2 fusion.52
  88.5 0.2 fusion.9
  88.7 0.8 reshape.401
  (53 shorter events, 1.9 us)
Async XLA Ops:
  0.0 7.1 %copy-start = (s32[128]{0:T(128)S(1)}, s32[128]{0:T(128)}, u32[]{:S(2)}) copy-start(s32[128]{0:T(128)} %param.8) | copy-start | bytes 1540
  0.9 7.5 %collective-permute-start = (bf16[4,8192]{1,0:T(4,128)(2,1)S(1)}, bf16[4,8192]{1,0:T(4,128)(2,1)S(1)}, u32[]{:S(2)}, u32[]{:S(2)}) collective-permute-start(bf16[4,8192]{1,0:T(4,128)(2,1)S(1)} %reshape.391), channel_id=1, source_target_pairs={{0,8},{8,0},{16,24},{24,16},{1,9},{9,1},{17,25},{25,17},{2,10},{10... | collective-permute-start | bytes 196616 | tf_op jit(solution)/shard_map/ppermute | solution.py:376
  4.0 7.3 %collective-permute-start.1 = (bf16[4,8192]{1,0:T(4,128)(2,1)S(1)}, bf16[4,8192]{1,0:T(4,128)(2,1)S(1)}, u32[]{:S(2)}, u32[]{:S(2)}) collective-permute-start(bf16[4,8192]{1,0:T(4,128)(2,1)S(1)} %reshape.391), channel_id=1, source_target_pairs={{0,16},{8,24},{16,0},{24,8},{1,17},{9,25},{17,1},{25,9},{2,18},{10... | collective-permute-start | bytes 196616 | tf_op jit(solution)/shard_map/ppermute | solution.py:376
  6.6 6.1 %collective-permute-start.2 = (bf16[4,8192]{1,0:T(4,128)(2,1)S(1)}, bf16[4,8192]{1,0:T(4,128)(2,1)S(1)}, u32[]{:S(2)}, u32[]{:S(2)}) collective-permute-start(bf16[4,8192]{1,0:T(4,128)(2,1)S(1)} %reshape.391), channel_id=1, source_target_pairs={{0,24},{8,16},{16,8},{24,0},{1,25},{9,17},{17,9},{25,1},{2,26},{10... | collective-permute-start | bytes 196616 | tf_op jit(solution)/shard_map/ppermute | solution.py:376
  12.8 18.1 %collective-permute-start.3 = (bf16[16,8192]{1,0:T(8,128)(2,1)S(1)}, bf16[16,8192]{1,0:T(8,128)(2,1)S(1)}, u32[]{:S(2)}, u32[]{:S(2)}) collective-permute-start(bf16[16,8192]{1,0:T(8,128)(2,1)S(1)} %pad_maximum_fusion.4.refs_0_), channel_id=1, source_target_pairs={{0,2},{1,3},{2,0},{3,1},{4,6},{5,7},{6,4},{7,5},{8,10},{9,11},{10,... | collective-permute-start | bytes 786440 | tf_op jit(solution)/shard_map/ppermute | solution.py:376
  14.4 17.0 %collective-permute-start.4 = (bf16[16,8192]{1,0:T(8,128)(2,1)S(1)}, bf16[16,8192]{1,0:T(8,128)(2,1)S(1)}, u32[]{:S(2)}, u32[]{:S(2)}) collective-permute-start(bf16[16,8192]{1,0:T(8,128)(2,1)S(1)} %pad_maximum_fusion.4.refs_0_), channel_id=1, source_target_pairs={{0,4},{1,5},{2,6},{3,7},{4,0},{5,1},{6,2},{7,3},{8,12},{9,13},{10,... | collective-permute-start | bytes 786440 | tf_op jit(solution)/shard_map/ppermute | solution.py:376
  15.9 15.6 %collective-permute-start.5 = (bf16[16,8192]{1,0:T(8,128)(2,1)S(1)}, bf16[16,8192]{1,0:T(8,128)(2,1)S(1)}, u32[]{:S(2)}, u32[]{:S(2)}) collective-permute-start(bf16[16,8192]{1,0:T(8,128)(2,1)S(1)} %pad_maximum_fusion.4.refs_0_), channel_id=1, source_target_pairs={{0,6},{1,7},{2,4},{3,5},{4,2},{5,3},{6,0},{7,1},{8,14},{9,15},{10,... | collective-permute-start | bytes 786440 | tf_op jit(solution)/shard_map/ppermute | solution.py:376
  18.4 3.4 %copy-start.1 = (bf16[512,2,4096]{2,1,0:T(2,128)(2,1)S(1)}, bf16[512,2,4096]{2,1,0:T(2,128)(2,1)}, u32[]{:S(2)}) copy-start(bf16[512,2,4096]{2,1,0:T(2,128)(2,1)} %param.5) | copy-start | bytes 25165828
  30.8 8.1 %collective-permute-start.6 = (bf16[16,8192]{1,0:T(8,128)(2,1)S(1)}, bf16[16,8192]{1,0:T(8,128)(2,1)S(1)}, u32[]{:S(2)}, u32[]{:S(2)}) collective-permute-start(bf16[16,8192]{1,0:T(8,128)(2,1)S(1)} %pad_maximum_fusion.4.refs_0_), channel_id=1, source_target_pairs={{0,1},{1,0},{2,3},{3,2},{4,5},{5,4},{6,7},{7,6},{8,9},{9,8},{10,11... | collective-permute-start | bytes 786440 | tf_op jit(solution)/shard_map/ppermute | solution.py:376
  30.9 8.1 %collective-permute-start.7 = (bf16[16,8192]{1,0:T(8,128)(2,1)S(1)}, bf16[16,8192]{1,0:T(8,128)(2,1)S(1)}, u32[]{:S(2)}, u32[]{:S(2)}) collective-permute-start(bf16[16,8192]{1,0:T(8,128)(2,1)S(1)} %collective-permute-done.3.refs_1_), channel_id=1, source_target_pairs={{0,1},{1,0},{2,3},{3,2},{4,5},{5,4},{6,7},{7,6},{8,9},{9,8},{10,11... | collective-permute-start | bytes 786440 | tf_op jit(solution)/shard_map/ppermute | solution.py:376
  31.4 7.6 %collective-permute-start.8 = (bf16[16,8192]{1,0:T(8,128)(2,1)S(1)}, bf16[16,8192]{1,0:T(8,128)(2,1)S(1)}, u32[]{:S(2)}, u32[]{:S(2)}) collective-permute-start(bf16[16,8192]{1,0:T(8,128)(2,1)S(1)} %collective-permute-done.4.refs_2_), channel_id=1, source_target_pairs={{0,1},{1,0},{2,3},{3,2},{4,5},{5,4},{6,7},{7,6},{8,9},{9,8},{10,11... | collective-permute-start | bytes 786440 | tf_op jit(solution)/shard_map/ppermute | solution.py:376
  31.5 7.5 %collective-permute-start.9 = (bf16[16,8192]{1,0:T(8,128)(2,1)S(1)}, bf16[16,8192]{1,0:T(8,128)(2,1)S(1)}, u32[]{:S(2)}, u32[]{:S(2)}) collective-permute-start(bf16[16,8192]{1,0:T(8,128)(2,1)S(1)} %collective-permute-done.5.refs_3_), channel_id=1, source_target_pairs={{0,1},{1,0},{2,3},{3,2},{4,5},{5,4},{6,7},{7,6},{8,9},{9,8},{10,11... | collective-permute-start | bytes 786440 | tf_op jit(solution)/shard_map/ppermute | solution.py:376
  39.0 7.1 %copy-start.2 = (f32[512]{0:T(512)S(1)}, f32[512]{0:T(512)}, u32[]{:S(2)}) copy-start(f32[512]{0:T(512)} %param.6) | copy-start | bytes 6148
  54.6 6.4 %collective-permute-start.10 = (f16[64,8320]{1,0:T(8,128)(2,1)S(1)}, f16[64,8320]{1,0:T(8,128)(2,1)S(1)}, u32[]{:S(2)}, u32[]{:S(2)}) collective-permute-start(f16[64,8320]{1,0:T(8,128)(2,1)S(1)} %pad_maximum_fusion), channel_id=1, source_target_pairs={{0,1},{1,0},{2,3},{3,2},{4,5},{5,4},{6,7},{7,6},{8,9},{9,8},{10,11... | collective-permute-start | bytes 3194888 | tf_op jit(solution)/shard_map/ppermute | solution.py:376
  62.4 9.3 %collective-permute-start.11 = (f16[16,8320]{1,0:T(8,128)(2,1)S(1)}, f16[16,8320]{1,0:T(8,128)(2,1)S(1)}, u32[]{:S(2)}, u32[]{:S(2)}) collective-permute-start(f16[16,8320]{1,0:T(8,128)(2,1)S(1)} %pad_maximum_fusion.1), channel_id=1, source_target_pairs={{0,2},{1,3},{2,0},{3,1},{4,6},{5,7},{6,4},{7,5},{8,10},{9,11},{10,... | collective-permute-start | bytes 798728 | tf_op jit(solution)/shard_map/ppermute | solution.py:376
  64.1 14.2 %collective-permute-start.12 = (f16[16,8320]{1,0:T(8,128)(2,1)S(1)}, f16[16,8320]{1,0:T(8,128)(2,1)S(1)}, u32[]{:S(2)}, u32[]{:S(2)}) collective-permute-start(f16[16,8320]{1,0:T(8,128)(2,1)S(1)} %pad_maximum_fusion.2), channel_id=1, source_target_pairs={{0,4},{1,5},{2,6},{3,7},{4,0},{5,1},{6,2},{7,3},{8,12},{9,13},{10,... | collective-permute-start | bytes 798728 | tf_op jit(solution)/shard_map/ppermute | solution.py:376
  65.7 12.6 %collective-permute-start.13 = (f16[16,8320]{1,0:T(8,128)(2,1)S(1)}, f16[16,8320]{1,0:T(8,128)(2,1)S(1)}, u32[]{:S(2)}, u32[]{:S(2)}) collective-permute-start(f16[16,8320]{1,0:T(8,128)(2,1)S(1)} %pad_maximum_fusion.3), channel_id=1, source_target_pairs={{0,6},{1,7},{2,4},{3,5},{4,2},{5,3},{6,0},{7,1},{8,14},{9,15},{10,... | collective-permute-start | bytes 798728 | tf_op jit(solution)/shard_map/ppermute | solution.py:376
  79.5 4.7 %collective-permute-start.14 = (f16[4,8320]{1,0:T(4,128)(2,1)S(1)}, f16[4,8320]{1,0:T(4,128)(2,1)S(1)}, u32[]{:S(2)}, u32[]{:S(2)}) collective-permute-start(f16[4,8320]{1,0:T(4,128)(2,1)S(1)} %pad_maximum_fusion.6), channel_id=1, source_target_pairs={{0,8},{8,0},{16,24},{24,16},{1,9},{9,1},{17,25},{25,17},{2,10},{10... | collective-permute-start | bytes 199688 | tf_op jit(solution)/shard_map/ppermute | solution.py:376
  79.6 7.5 %collective-permute-start.15 = (f16[4,8320]{1,0:T(4,128)(2,1)S(1)}, f16[4,8320]{1,0:T(4,128)(2,1)S(1)}, u32[]{:S(2)}, u32[]{:S(2)}) collective-permute-start(f16[4,8320]{1,0:T(4,128)(2,1)S(1)} %pad_maximum_fusion.7), channel_id=1, source_target_pairs={{0,16},{8,24},{16,0},{24,8},{1,17},{9,25},{17,1},{25,9},{2,18},{10... | collective-permute-start | bytes 199688 | tf_op jit(solution)/shard_map/ppermute | solution.py:376
  82.1 6.2 %collective-permute-start.16 = (f16[4,8320]{1,0:T(4,128)(2,1)S(1)}, f16[4,8320]{1,0:T(4,128)(2,1)S(1)}, u32[]{:S(2)}, u32[]{:S(2)}) collective-permute-start(f16[4,8320]{1,0:T(4,128)(2,1)S(1)} %pad_maximum_fusion.8), channel_id=1, source_target_pairs={{0,24},{8,16},{16,8},{24,0},{1,25},{9,17},{17,9},{25,1},{2,26},{10... | collective-permute-start | bytes 199688 | tf_op jit(solution)/shard_map/ppermute | solution.py:376

commit v3 on v2

--- a/solution.py
+++ b/solution.py
@@ -16,7 +16,8 @@
 PAIR = 2 * LANES
 UNROLL = 4
 WIRE = jnp.float16
-VMEM_LIMIT = 16 << 20
+VMEM_LIMIT = 8 << 20
+RELAY_LIMIT = 12 << 20
 
 PARAMS = pltpu.CompilerParams(vmem_limit_bytes=VMEM_LIMIT)
 
@@ -72,6 +73,7 @@
     per = parts * groups
     flat = images.reshape(count, parts, groups, LANES)
     flat = flat.transpose(0, 2, 1, 3).reshape(count, per, LANES)
+    flat = pltpu.with_memory_space_constraint(flat, pltpu.HBM)
     return pl.pallas_call(
         functools.partial(relay_kernel, rows),
         in_specs=[pl.BlockSpec(memory_space=pltpu.HBM)],
@@ -83,7 +85,7 @@
             pltpu.VMEM((rows, LANES), jnp.float32),
             pltpu.SemaphoreType.DMA((2,)),
         ],
-        compiler_params=pltpu.CompilerParams(vmem_limit_bytes=2 * VMEM_LIMIT),
+        compiler_params=pltpu.CompilerParams(vmem_limit_bytes=RELAY_LIMIT),
         cost_estimate=pl.CostEstimate(
             flops=count * per * LANES,
             bytes_accessed=4 * count * per * LANES,
@@ -153,16 +155,17 @@
     return [pl.BlockSpec(memory_space=pltpu.VMEM)] * count
 
 
-def score_kernel(pieces, shifts, *refs):
+def score_kernel(places, shifts, *refs):
+    pieces = len(places)
     piece_refs = refs[:pieces]
-    cos_ref, sin_ref, sign_ref, x_ref = refs[pieces : pieces + 4]
-    out_ref, norm_ref, rot_a, rot_b = refs[pieces + 4 :]
+    tables = (refs[pieces : pieces + 3], refs[pieces + 3 : pieces + 6])
+    x_ref, out_ref, norm_ref, rot_a, rot_b = refs[pieces + 6 :]
     images = out_ref.shape[1]
     piece_rows = piece_refs[0].shape[0]
-    held = pieces * piece_rows
+    span = shifts * piece_rows
     block = rot_a.shape[1]
     per = block // PAIR
-    half = cos_ref.shape[0] // per
+    half = tables[0][0].shape[0] // per
 
     norm_ref[...] = jnp.zeros_like(norm_ref)
     out_ref[...] = jnp.zeros_like(out_ref)
@@ -174,16 +177,19 @@
         phase = lax.rem(index, half) * per
         for g in range(per):
             at = g * PAIR
-            for i in range(pieces):
+            for i, (side, place) in enumerate(places):
+                cos_ref, sin_ref, _ = tables[side]
                 here = slice(i * piece_rows, (i + 1) * piece_rows)
                 real = piece_refs[i][:, pl.ds(base + at, LANES)].astype(jnp.float32)
                 imag = piece_refs[i][:, pl.ds(base + at + LANES, LANES)].astype(jnp.float32)
                 power = real * real + imag * imag
                 norm_ref[here, :] += jnp.where(live, power, 0.0)
                 for j in range(shifts):
-                    start = j * held + i * piece_rows
+                    start = place * span + j * piece_rows
                     row = slice(start, start + piece_rows)
                     c, s = cos_ref[phase + g, row, :], sin_ref[phase + g, row, :]
+                    start = i * span + j * piece_rows
+                    row = slice(start, start + piece_rows)
                     rot_ref[row, at : at + LANES] = (real * c + imag * s).astype(jnp.bfloat16)
                     rot_ref[row, at + LANES : at + PAIR] = (imag * c - real * s).astype(
                         jnp.bfloat16
@@ -201,7 +207,10 @@
     def turn_sign():
         for n in range(images // LANES):
             lanes = slice(n * LANES, (n + 1) * LANES)
-            out_ref[:, lanes] = out_ref[:, lanes] * sign_ref[...]
+            for i, (side, place) in enumerate(places):
+                sign = tables[side][2][place * span : (place + 1) * span, :]
+                row = slice(i * span, (i + 1) * span)
+                out_ref[row, lanes] = out_ref[row, lanes] * sign
 
     rotate(jnp.int32(0), rot_a)
 
@@ -220,14 +229,14 @@
     turn_sign()
 
 
-def scores_of(piece_list, phases, shifts, x, images, groups=2):
+def scores_of(piece_list, places, tables, shifts, x, images, groups=2):
     pieces = len(piece_list)
     rows, width = piece_list[0].shape
     held = pieces * rows
     rotated = pltpu.VMEM((shifts * held, groups * PAIR), jnp.bfloat16)
     return pl.pallas_call(
-        functools.partial(score_kernel, pieces, shifts),
-        in_specs=whole_in_vmem(pieces + 4),
+        functools.partial(score_kernel, places, shifts),
+        in_specs=whole_in_vmem(pieces + 7),
         out_specs=tuple(whole_in_vmem(2)),
         out_shape=(
             jax.ShapeDtypeStruct((shifts * held, images), jnp.float32),
@@ -240,49 +249,66 @@
             bytes_accessed=2 * images * width + 8 * shifts * held * images,
             transcendentals=0,
         ),
-    )(*piece_list, *phases, x)
-
-
-def weight_kernel(own_ref, other_ref, own_norm, other_norm, prec_ref, x_ref, *outs):
-    outs, raised_refs = outs[:6], outs[6:]
+    )(*piece_list, *tables[0], *tables[1], x)
+
+
+def weight_kernel(layout, shifts, piece_rows, *refs):
+    blocks = len(layout)
+    score_refs, norm_refs = refs[:blocks], refs[blocks : 2 * blocks]
+    prec_ref, x_ref = refs[2 * blocks : 2 * blocks + 2]
+    outs, raised_refs = refs[2 * blocks + 2 : 2 * blocks + 8], refs[2 * blocks + 8 :]
     images = prec_ref.shape[1]
+    span = shifts * piece_rows
     peak = jnp.max(x_ref[images:, :LANES].astype(jnp.float32)) * math.sqrt(2.0)
     prec = prec_ref[...][None]
-    halves = ((own_ref, own_norm), (other_ref, other_norm))
-    bias, tops = [], []
-    for ref, norm_ref in halves:
+
+    def cube(value):
+        return value.reshape(-1, piece_rows, value.shape[-1])
+
+    top = None
+    for places, score_ref, norm_ref, raised_ref in zip(
+        layout, score_refs, norm_refs, raised_refs
+    ):
         norm = 0.5 * jnp.sum(norm_ref[...], axis=1, keepdims=True)
-        bias.append(norm[None])
-        value = prec * (ref[...] - norm[None])
-        tops.append(jnp.max(jnp.max(value, axis=0), axis=0, keepdims=True))
-    top = jnp.maximum(*tops)[None]
-    norm = 0.0
-    for (ref, _), offset, raised_ref in zip(halves, bias, raised_refs):
-        raised = jnp.exp(prec * (ref[...] - offset) - top)
-        raised_ref[...] = raised
-        norm = norm + jnp.sum(jnp.sum(raised, axis=0), axis=0, keepdims=True)
-    inverse = (1.0 / norm)[None]
-    for h, ref in enumerate(raised_refs):
-        weight = (ref[...] * inverse).astype(jnp.bfloat16)
-        outs[h][...] = weight
-        wide = weight.astype(jnp.float32)
-        total = jnp.sum(jnp.sum(wide, axis=0), axis=1, keepdims=True)
-        total = jnp.broadcast_to(total, outs[2 + h].shape)
-        outs[2 + h][...] = total
-        outs[4 + h][...] = total * peak
-
-
-def weights_of(own, other, precision, x, shifts):
-    rows, images = own[0].shape
-    held = rows // shifts
-    cube = jax.ShapeDtypeStruct((shifts, held, images), jnp.bfloat16)
+        for i in range(len(places)):
+            row = slice(i * span, (i + 1) * span)
+            bias = norm[i * piece_rows : (i + 1) * piece_rows][None]
+            value = prec * (cube(score_ref[row, :]) - bias)
+            raised_ref[row, :] = value.reshape(span, images)
+            best = jnp.max(jnp.max(value, axis=0), axis=0, keepdims=True)
+            top = best if top is None else jnp.maximum(top, best)
+    norm = None
+    for places, raised_ref in zip(layout, raised_refs):
+        for i in range(len(places)):
+            row = slice(i * span, (i + 1) * span)
+            raised = jnp.exp(raised_ref[row, :] - top)
+            raised_ref[row, :] = raised
+            part = jnp.sum(jnp.sum(cube(raised), axis=0), axis=0, keepdims=True)
+            norm = part if norm is None else norm + part
+    inverse = 1.0 / norm
+    for places, raised_ref in zip(layout, raised_refs):
+        for i, (side, place) in enumerate(places):
+            weight = (raised_ref[i * span : (i + 1) * span, :] * inverse).astype(jnp.bfloat16)
+            outs[side][place * span : (place + 1) * span, :] = weight
+            total = jnp.sum(cube(weight.astype(jnp.float32)), axis=0)
+            total = jnp.sum(total, axis=1, keepdims=True)
+            total = jnp.broadcast_to(total, (piece_rows, LANES))
+            here = slice(place * piece_rows, (place + 1) * piece_rows)
+            outs[2 + side][here, :] = total
+            outs[4 + side][here, :] = total * peak
+
+
+def weights_of(scores, layout, precision, x, shifts, held, piece_rows):
+    images = precision.shape[0]
+    weight = jax.ShapeDtypeStruct((shifts * held, images), jnp.bfloat16)
     total = jax.ShapeDtypeStruct((held, LANES), jnp.float32)
+    rows = 2 * shifts * held
     own_w, other_w, own_t, other_t, own_b, other_b = pl.pallas_call(
-        weight_kernel,
-        in_specs=whole_in_vmem(6),
+        functools.partial(weight_kernel, layout, shifts, piece_rows),
+        in_specs=whole_in_vmem(2 * len(layout) + 2),
         out_specs=tuple(whole_in_vmem(6)),
-        out_shape=(cube, cube, total, total, total, total),
-        scratch_shapes=[pltpu.VMEM((shifts, held, images), jnp.float32)] * 2,
+        out_shape=(weight, weight, total, total, total, total),
+        scratch_shapes=[pltpu.VMEM(value.shape, jnp.float32) for value, _ in scores],
         compiler_params=PARAMS,
         cost_estimate=pl.CostEstimate(
             flops=20 * rows * images,
@@ -290,53 +316,56 @@
             transcendentals=2 * rows * images,
         ),
     )(
-        own[0].reshape(shifts, held, images),
-        other[0].reshape(shifts, held, images),
-        own[1],
-        other[1],
+        *[value for value, _ in scores],
+        *[value for _, value in scores],
         precision.reshape(1, images),
         x,
     )
-    own_w, other_w = own_w.reshape(rows, images), other_w.reshape(rows, images)
-    own_sum, other_sum = own_t[:, :1], other_t[:, :1]
-    return (own_w, own_sum, own_b[:, :1]), (other_w, other_sum, other_b[:, :1])
-
-
-def back_kernel(shifts, w_ref, cos_ref, sin_ref, sign_ref, x_ref, out_ref, *scratch):
-    turned_ref, mix_a, mix_b = scratch
-    rows, images = w_ref.shape
-    held = rows // shifts
+    return (own_w, own_t[:, :1], own_b[:, :1]), (other_w, other_t[:, :1], other_b[:, :1])
+
+
+def back_kernel(first, pieces, shifts, w_ref, cos_ref, sin_ref, sign_ref, x_ref, *refs):
+    out_ref, turned_ref, mix_a, mix_b = refs
+    rows, images = turned_ref.shape
+    span = rows // pieces
+    piece_rows = span // shifts
     count = cos_ref.shape[0]
+    first = first * span
+    used = slice(first, first + rows)
     for n in range(images // LANES):
         lanes = slice(n * LANES, (n + 1) * LANES)
-        wide = w_ref[:, lanes].astype(jnp.float32) * sign_ref[...]
+        wide = w_ref[used, lanes].astype(jnp.float32) * sign_ref[used, :]
         turned_ref[:, lanes] = wide.astype(jnp.bfloat16)
 
     def mix(index, mix_ref):
         index = jnp.minimum(index, count - 1)
-        for second, ref in enumerate((w_ref, turned_ref)):
+        for second in range(2):
+            weight = turned_ref[...] if second else w_ref[used, :]
             base = pl.multiple_of((second * count + index) * PAIR, PAIR)
             mix_ref[:, second * PAIR : (second + 1) * PAIR] = jnp.dot(
-                ref[...], x_ref[0:images, pl.ds(base, PAIR)], preferred_element_type=jnp.float32
+                weight, x_ref[0:images, pl.ds(base, PAIR)], preferred_element_type=jnp.float32
             )
 
     def turn(index, mix_ref):
-        for i in range(held // 8):
-            here = slice(i * 8, (i + 1) * 8)
-            total = [None] * 4
-            for j in range(shifts):
-                row = slice(j * held + i * 8, j * held + (i + 1) * 8)
-                c, s = cos_ref[index, row, :], sin_ref[index, row, :]
-                terms = []
-                for second in range(2):
-                    at = second * PAIR
-                    real = mix_ref[row, at : at + LANES]
-                    imag = mix_ref[row, at + LANES : at + PAIR]
-                    terms += [real * c - imag * s, imag * c + real * s]
-                total = [b if a is None else a + b for a, b in zip(total, terms)]
-            for part in range(4):
-                base = (part // 2 * count + index) * PAIR + part % 2 * LANES
-                out_ref[here, pl.ds(pl.multiple_of(base, LANES), LANES)] = total[part]
+        for i in range(pieces):
+            for t in range(0, piece_rows, 8):
+                total = [None] * 4
+                for j in range(shifts):
+                    start = i * span + j * piece_rows + t
+                    row = slice(start, start + 8)
+                    at_row = slice(first + start, first + start + 8)
+                    c, s = cos_ref[index, at_row, :], sin_ref[index, at_row, :]
+                    terms = []
+                    for second in range(2):
+                        at = second * PAIR
+                        real = mix_ref[row, at : at + LANES]
+                        imag = mix_ref[row, at + LANES : at + PAIR]
+                        terms += [real * c - imag * s, imag * c + real * s]
+                    total = [b if a is None else a + b for a, b in zip(total, terms)]
+                here = slice(i * piece_rows + t, i * piece_rows + t + 8)
+                for part in range(4):
+                    base = (part // 2 * count + index) * PAIR + part % 2 * LANES
+                    out_ref[here, pl.ds(pl.multiple_of(base, LANES), LANES)] = total[part]
 
     mix(jnp.int32(0), mix_a)
 
@@ -352,21 +381,21 @@
     lax.fori_loop(0, count // UNROLL, step, 0)
 
 
-def back_of(weight, x, phases, shifts):
-    rows, images = weight.shape
-    held = rows // shifts
+def back_of(weight, x, phases, shifts, first, pieces, piece_rows):
+    images = weight.shape[1]
+    rows = pieces * shifts * piece_rows
     width = x.shape[1]
     mixed = pltpu.VMEM((rows, 2 * PAIR), jnp.float32)
     return pl.pallas_call(
-        functools.partial(back_kernel, shifts),
+        functools.partial(back_kernel, first, pieces, shifts),
         in_specs=whole_in_vmem(5),
         out_specs=whole_in_vmem(1)[0],
-        out_shape=jax.ShapeDtypeStruct((held, width), jnp.float32),
+        out_shape=jax.ShapeDtypeStruct((pieces * piece_rows, width), jnp.float32),
         scratch_shapes=[pltpu.VMEM((rows, images), jnp.bfloat16), mixed, mixed],
         compiler_params=PARAMS,
         cost_estimate=pl.CostEstimate(
             flops=2 * rows * images * width,
-            bytes_accessed=2 * images * width + 2 * rows * images + 4 * held * width,
+            bytes_accessed=2 * images * width + 2 * rows * images + 4 * pieces * width,
             transcendentals=0,
         ),
     )(weight, *phases, x)
@@ -391,20 +420,23 @@
 
     row_set = [mine]
     row_set += [exchange(mine, "row", rows, d) for d in range(1, rows)]
-    row_set = jnp.concatenate(row_set, axis=0)
-    own_set = [row_set]
-    own_set += [exchange(row_set, "col", cols, 2 * d) for d in range(1, quads)]
-    other_set = [exchange(value, "col", cols, 1) for value in own_set]
+    own_set = [jnp.concatenate(row_set, axis=0)]
+    for d in range(1, quads):
+        own_set.append(exchange(own_set[0], "col", cols, 2 * d))
+    other_set = []
+    for d in range(quads):
+        other_set.append(exchange(own_set[d], "col", cols, 1))
 
     x = relay(images)
 
+    piece_rows = local * rows
     position = jnp.arange(2 * held, dtype=jnp.int32)
     at_local = position % local
     at_row = (position // local % rows) ^ lax.axis_index("row")
-    at_quad = position // (local * rows) % quads
+    at_quad = (position // piece_rows + 1) % quads
     at_col = (2 * at_quad + position // held) ^ lax.axis_index("col")
     slots = (at_row * cols + at_col) * local + at_local
-    shift = shift_table[template_id[slots]].reshape(2, held, shifts)
+    shift = shift_table[template_id[slots]].reshape(2 * quads, piece_rows, shifts)
     shift = shift.transpose(0, 2, 1).reshape(-1, 1)
 
     number = jnp.arange(SHIFT_SIDE * SHIFT_SIDE, dtype=jnp.int32)[:, None]
@@ -420,22 +452,33 @@
     table = [jnp.cos(angle), jnp.sin(angle)]
     table = [part[:, at : at + LANES] for at in (0, LANES) for part in table]
     table = jnp.concatenate(table, axis=1)
-    own_phases, other_phases = phases_of(shift, table, groups // 2, shifts * held)
-
-    own_scores = scores_of(own_set, own_phases, shifts, x, image_count)
-    other_scores = scores_of(other_set, other_phases, shifts, x, image_count)
-    own, other = weights_of(own_scores, other_scores, precision, x, shifts)
-
-    def send(held_rows, axis, size, bit):
+    tables = phases_of(shift, table, groups // 2, shifts * held)
+
+    layout = [
+        tuple((0, (d - 1) % quads) for d in range(quads - 1)),
+        tuple((1, (d - 1) % quads) for d in range(quads - 1)),
+        ((0, quads - 2), (1, quads - 2)),
+    ]
+    piece_lists = [own_set[:-1], other_set[:-1], [own_set[-1], other_set[-1]]]
+    scores = []
+    for number, (piece_list, places) in enumerate(zip(piece_lists, layout)):
+        scores.append(scores_of(piece_list, places, tables, shifts, x, image_count))
+    own, other = weights_of(scores, layout, precision, x, shifts, held, piece_rows)
+
+    def pack(held_rows):
         value, total, bound = held_rows
         power = jnp.ceil(jnp.log2(jnp.maximum(bound, 1e-30))) - 15.0
         at = jnp.arange(LANES, dtype=jnp.int32)[None, :]
         extra = jnp.where(at == 0, total, jnp.where(at == 1, power, 0.0))
-        payload = jnp.concatenate([value * jnp.exp2(-power), extra], axis=1)
-        got = exchange(payload.astype(WIRE), axis, size, bit).astype(jnp.float32)
-        span = value.shape[1]
-        total, power = got[:, span : span + 1], got[:, span + 1 : span + 2]
-        return got[:, :span] * jnp.exp2(power), total, jnp.exp2(power + 15.0)
+        return jnp.concatenate([value * jnp.exp2(-power), extra], axis=1).astype(WIRE)
+
+    def unpack(payload):
+        got = payload.astype(jnp.float32)
+        total, power = got[:, width : width + 1], got[:, width + 1 : width + 2]
+        return got[:, :width] * jnp.exp2(power), total, jnp.exp2(power + 15.0)
+
+    def send(held_rows, axis, size, bit):
+        return unpack(exchange(pack(held_rows), axis, size, bit))
 
     def add(first, *others):
         for other in others:
@@ -445,22 +488,29 @@
     def cut(held_rows, at, count):
         return tuple(value[at * count : (at + 1) * count] for value in held_rows)
 
-    def reduce_to_owner(own, other):
-        got = send(other, "col", cols, 1)
-        whole = add(own, got)
-        per = local * rows
-        got = [send(cut(whole, d, per), "col", cols, 2 * d) for d in range(1, quads)]
-        whole = add(cut(whole, 0, per), *got)
-        got = [
-            send(cut(whole, d, local), "row", rows, d) for d in range(1, rows)
-        ]
-        return add(cut(whole, 0, local), *got)
-
-    other_back = back_of(other[0], x, other_phases, shifts)
-    own_back = back_of(own[0], x, own_phases, shifts)
-    summed, totals, _ = reduce_to_owner(
-        (own_back,) + own[1:], (other_back,) + other[1:]
-    )
+    other_back = back_of(other[0], x, tables[1], shifts, 0, quads, piece_rows)
+    got = send((other_back,) + other[1:], "col", cols, 1)
+    per_set = quads // 2
+    set_rows = per_set * piece_rows
+    own_weight = own[0]
+    sums, received = [], []
+    for number in range(2):
+        back = back_of(
+            own_weight, x, tables[0], shifts, number * per_set, per_set, piece_rows
+        )
+        whole = add((back,) + cut(own[1:], number, set_rows), cut(got, number, set_rows))
+        pieces = [cut(whole, place, piece_rows) for place in range(per_set)]
+        if number:
+            sums.append(pieces.pop())
+        pieces = [pack(piece) for piece in pieces]
+        if not number:
+            *pieces, own_weight = lax.optimization_barrier((*pieces, own_weight))
+        for place, piece in enumerate(pieces):
+            d = number * per_set + place + 1
+            received.append(unpack(exchange(piece, "col", cols, 2 * d)))
+    whole = add(sums[0], *received)
+    got = [send(cut(whole, d, local), "row", rows, d) for d in range(1, rows)]
+    summed, totals, _ = add(cut(whole, 0, local), *got)
     prior = mine.astype(jnp.float32)
     out = (summed + PRIOR_WEIGHT * prior) / (totals + PRIOR_WEIGHT)
     out = out.reshape(local, groups, parts, LANES).transpose(0, 2, 1, 3)

time: 89.7 us -> 90 us (level)
  Pallas kernels: 37 us -> 40.5 us
  local copies, waits for them, and re-layouts: 8.74 us -> 5.28 us
    unnamed x7 -> x5, local copies, waits for them, and re-layouts: 4.17 us -> 0.8 us
    pallas_call x5 -> x7, Pallas kernels: 28 us -> 30.1 us  [the longest x3 15 us: scores_of(): pl.pallas_call(functools.partial(score_kernel, places, shifts), in_specs=...]
    pallas_call x1, Pallas kernels: 6.24 us -> 7.67 us  [relay(): pl.pallas_call(functools.partial(relay_kernel, rows), in_specs=[pl.BlockS...]
  transfers between devices with their start and end apart: 17 -> 17, of which waited for: 6 -> 7; matrix products, arithmetic and copies ran while one was open for 5% -> 4% of each run, Pallas kernels for 25% -> 26%
where the time goes in v3:
time: 90 us; the launch traced here: 89.7 us
  Pallas kernels  40.5 us (45%)
  waiting for transfers between devices  20.2 us (22%)
  starting transfers between devices  18.6 us (21%)
  local copies, waits for them, and re-layouts  5.28 us (6%)
  other arithmetic  4.63 us (5%)
    ppermute x17, waiting for transfers between devices, exchange(): return lax.ppermute(value, axis, [(i, i ^ bit) for i in range(size)])  20.2 us
    ppermute x17, starting transfers between devices, exchange(): return lax.ppermute(value, axis, [(i, i ^ bit) for i in range(size)])  18.6 us
    pallas_call x3, Pallas kernels, scores_of(): pl.pallas_call(functools.partial(score_kernel, places, shifts), in_specs=...  15 us
    pallas_call x3, Pallas kernels, back_of(): pl.pallas_call(functools.partial(back_kernel, first, pieces, shifts), in_...  13.9 us
    pallas_call x1, Pallas kernels, relay(): pl.pallas_call(functools.partial(relay_kernel, rows), in_specs=[pl.BlockS...  7.67 us
    pallas_call x1, Pallas kernels, phases_of(): pl.pallas_call(phase_kernel, in_specs=whole_in_vmem(2), out_specs=tuple(w...  2.78 us
  transfers between devices with their start and end apart: 17, of which 7 were waited for; matrix products, arithmetic and copies ran while one was open for 4% of the time, Pallas kernels for 26%

profile of v3, /device:TPU:0, one launch (start us, length us, event | category | flops | bytes accessed | tf_op | source)
XLA Modules:
  0.0 89.7 jit_solution(14233621013921123261)
XLA Ops:
  0.0 0.9 reshape.382
  0.9 3.1 %collective-permute-start = (bf16[4,8192]{1,0:T(4,128)(2,1)S(1)}, bf16[4,8192]{1,0:T(4,128)(2,1)S(1)}, u32[]{:S(2)}, u32[]{:S(2)}) collective-permute-start(bf16[4,8192]{1,0:T(4,128)(2,1)S(1)} %reshape.382), channel_id=1, source_target_pairs={{0,8},{8,0},{16,24},{24,16},{1,9},{9,1},{17,25},{25,17},{2,10},{10... | collective-permute-start | bytes 196616 | tf_op jit(solution)/shard_map/ppermute | solution.py:405
  4.0 2.6 %collective-permute-start.1 = (bf16[4,8192]{1,0:T(4,128)(2,1)S(1)}, bf16[4,8192]{1,0:T(4,128)(2,1)S(1)}, u32[]{:S(2)}, u32[]{:S(2)}) collective-permute-start(bf16[4,8192]{1,0:T(4,128)(2,1)S(1)} %reshape.382), channel_id=1, source_target_pairs={{0,16},{8,24},{16,0},{24,8},{1,17},{9,25},{17,1},{25,9},{2,18},{10... | collective-permute-start | bytes 196616 | tf_op jit(solution)/shard_map/ppermute | solution.py:405
  6.8 0.2 fusion.16
  7.1 1.2 %gather_fusion = s32[128]{0:T(128)S(1)} fusion(s32[128]{0:T(128)S(1)} %copy-done, s32[1024]{0:T(1024)S(1)} %pad_clamp_fusion.1), kind=kCustom, calls=%fused_computation | custom fusion | bytes 1536 | tf_op jit(solution)/shard_map/gather | solution.py:439
  8.4 2.9 %collective-permute-done.1 = bf16[4,8192]{1,0:T(4,128)(2,1)S(1)} collective-permute-done((bf16[4,8192]{1,0:T(4,128)(2,1)S(1)}, bf16[4,8192]{1,0:T(4,128)(2,1)S(1)}, u32[]{:S(2)}, u32[]{:S(2)}) %collective-permute-start.1) | collective-permute-done | bytes 65568 | tf_op jit(solution)/shard_map/ppermute | solution.py:405
  11.3 1.4 %collective-permute-done.2 = bf16[4,8192]{1,0:T(4,128)(2,1)S(1)} collective-permute-done((bf16[4,8192]{1,0:T(4,128)(2,1)S(1)}, bf16[4,8192]{1,0:T(4,128)(2,1)S(1)}, u32[]{:S(2)}, u32[]{:S(2)}) %collective-permute-start.2) | collective-permute-done | bytes 65568 | tf_op jit(solution)/shard_map/ppermute | solution.py:405
  12.8 2.5 %collective-permute-start.8 = (bf16[16,8192]{1,0:T(8,128)(2,1)S(1)}, bf16[16,8192]{1,0:T(8,128)(2,1)S(1)}, u32[]{:S(2)}, u32[]{:S(2)}) collective-permute-start(bf16[16,8192]{1,0:T(8,128)(2,1)S(1)} %pad_maximum_fusion.4.refs_0_), channel_id=1, source_target_pairs={{0,6},{1,7},{2,4},{3,5},{4,2},{5,3},{6,0},{7,1},{8,14},{9,15},{10,... | collective-permute-start | bytes 786440 | tf_op jit(solution)/shard_map/ppermute | solution.py:405
  15.3 0.5 collective-permute-start.3
  15.9 0.5 collective-permute-start.4
  16.4 0.8 copy.18
  17.2 0.6 gather_fusion.1
  17.9 0.3 reshape.406.shift_ref
  18.2 7.7 %shard_map.56.refs_9_.refs_8_.refs_7_.x_ref = bf16[528,8192]{1,0:T(8,128)(2,1)S(1)} custom-call(bf16[512,64,128]{2,1,0:T(8,128)(2,1)} %bitcast.21), custom_call_target="tpu_custom_call" | custom-call | flops 4194304 | bytes 16777216 | tf_op jit(solution)/shard_map/pallas_call | solution.py:77
  25.9 2.8 %shard_map.55 = (f32[16,512,128]{2,1,0:T(8,128)S(1)}, f32[16,512,128]{2,1,0:T(8,128)S(1)}, f32[512,128]{1,0:T(8,128)S(1)}, f32[16,512,128]{2,1,0:T(8,128)S(1)}, ...) custom-call(s32[1024,1]{1,0:T(8,128)S(1)} %reshape.406.shift_ref, f32[64,512]{1,0:T(8,128)S(1)} %pad_maximum_fusion.5.table_ref), custom_call_target="tpu_custom_call" | custom-call | flops 12582912 | bytes 16777216 | tf_op jit(solution)/shard_map/pallas_call | solution.py:138
  28.8 0.5 collective-permute-start.9
  29.4 0.4 collective-permute-start.7
  29.8 5.5 %shard_map.57 = (f32[384,512]{1,0:T(8,128)S(1)}, f32[48,128]{1,0:T(8,128)S(1)}) custom-call(bf16[16,8192]{1,0:T(8,128)(2,1)S(1)} %pad_maximum_fusion.4.refs_0_, bf16[16,8192]{1,0:T(8,128)(2,1)S(1)} %collective-permute-done.3.refs_1_, bf16[16,8192]{1,0:T(8,128)(2,1)S(1)} %collective-permute-done.4.refs_2_, ...), custom_call_target="tpu_custom_call" | custom-call | flops 3221225472 | bytes 9961472 | tf_op jit(solution)/shard_map/pallas_call | solution.py:237
  35.3 3.9 %shard_map.59 = (f32[256,512]{1,0:T(8,128)S(1)}, f32[32,128]{1,0:T(8,128)S(1)}) custom-call(bf16[16,8192]{1,0:T(8,128)(2,1)S(1)} %collective-permute-done.8.refs_0_, bf16[16,8192]{1,0:T(8,128)(2,1)S(1)} %collective-permute-done.9.refs_1_, f32[16,512,128]{2,1,0:T(8,128)S(1)} %get-tuple-element.26.refs_3_.refs_2_.cos_ref, ...), custom_call_target="tpu_custom_call" | custom-call | flops 2147483648 | bytes 9437184 | tf_op jit(solution)/shard_map/pallas_call | solution.py:237
  39.3 5.5 %shard_map.58 = (f32[384,512]{1,0:T(8,128)S(1)}, f32[48,128]{1,0:T(8,128)S(1)}) custom-call(bf16[16,8192]{1,0:T(8,128)(2,1)S(1)} %collective-permute-done.5.refs_0_, bf16[16,8192]{1,0:T(8,128)(2,1)S(1)} %collective-permute-done.6.refs_1_, bf16[16,8192]{1,0:T(8,128)(2,1)S(1)} %collective-permute-done.7.refs_2_, ...), custom_call_target="tpu_custom_call" | custom-call | flops 3221225472 | bytes 9961472 | tf_op jit(solution)/shard_map/pallas_call | solution.py:237
  44.9 1.2 %shard_map.60 = (bf16[512,512]{1,0:T(8,128)(2,1)S(1)}, bf16[512,512]{1,0:T(8,128)(2,1)S(1)}, f32[64,128]{1,0:T(8,128)S(1)}, f32[64,128]{1,0:T(8,128)S(1)}, f32[64,128]{1,0:T(8,128)S(1)}, /*index=5*/f32[64,128]{1,0:T(8,128)S(1)}) custom-call(f32[384,512]{1,0:T(8,128)S(1)} %get-tuple-element.32.refs_0_, f32[384,512]{1,0:T(8,128)S(1)} %get-tuple-element.33.refs_1_, ...), custom_call_target="tpu_custom_call" | custom-call | flops 10485760 | bytes 6291456 | tf_op jit(solution)/shard_map/pallas_call | solution.py:306
  46.1 6.3 %shard_map.62 = f32[64,8192]{1,0:T(8,128)S(1)} custom-call(bf16[512,512]{1,0:T(8,128)(2,1)S(1)} %get-tuple-element.39.w_ref, f32[16,512,128]{2,1,0:T(8,128)S(1)} %get-tuple-element.29.refs_6_.refs_5_.cos_ref, f32[16,512,128]{2,1,0:T(8,128)S(1)} %get-tuple-element.30.refs_7_.refs_6_.sin_ref, f32[512,128]{1,0:T(8,128)S(1)} %get-tuple-element.31.refs_8_.refs_7_.sign_ref, ...), custom_call_target="tpu_custom_call" | custom-call | flops 4294967296 | bytes 9043968 | tf_op jit(solution)/shard_map/pallas_call | solution.py:389
  52.7 0.2 multiply_convert_fusion
  53.0 0.2 pad_maximum_fusion
  53.4 3.8 %shard_map.61 = f32[32,8192]{1,0:T(8,128)S(1)} custom-call(bf16[512,512]{1,0:T(8,128)(2,1)S(1)} %get-tuple-element.44.w_ref, f32[16,512,128]{2,1,0:T(8,128)S(1)} %get-tuple-element.26.refs_3_.refs_2_.cos_ref, f32[16,512,128]{2,1,0:T(8,128)S(1)} %get-tuple-element.27.refs_4_.refs_3_.sin_ref, f32[512,128]{1,0:T(8,128)S(1)} %get-tuple-element.28.refs_5_.refs_4_.sign_ref, ...), custom_call_target="tpu_custom_call" | custom-call | flops 2147483648 | bytes 8716288 | tf_op jit(solution)/shard_map/pallas_call | solution.py:389
  57.4 0.2 exponential_reduce_fusion
  57.5 0.2 slice_multiply_fusion
  57.8 0.2 exponential_reduce_fusion.6
  58.3 0.2 slice_add_fusion.1
  58.9 3.8 %shard_map.63 = f32[32,8192]{1,0:T(8,128)S(1)} custom-call(bf16[512,512]{1,0:T(8,128)(2,1)S(1)} %get-tuple-element.44.w_ref, f32[16,512,128]{2,1,0:T(8,128)S(1)} %get-tuple-element.26.refs_3_.refs_2_.cos_ref, f32[16,512,128]{2,1,0:T(8,128)S(1)} %get-tuple-element.27.refs_4_.refs_3_.sin_ref, f32[512,128]{1,0:T(8,128)S(1)} %get-tuple-element.28.refs_5_.refs_4_.sign_ref, ...), custom_call_target="tpu_custom_call" | custom-call | flops 2147483648 | bytes 8716288 | tf_op jit(solution)/shard_map/pallas_call | solution.py:389
  62.7 0.2 slice_add_fusion
  63.0 2.5 %collective-permute-start.13 = (f16[16,8320]{1,0:T(8,128)(2,1)S(1)}, f16[16,8320]{1,0:T(8,128)(2,1)S(1)}, u32[]{:S(2)}, u32[]{:S(2)}) collective-permute-start(f16[16,8320]{1,0:T(8,128)(2,1)S(1)} %pad_maximum_fusion.3), channel_id=1, source_target_pairs={{0,6},{1,7},{2,4},{3,5},{4,2},{5,3},{6,0},{7,1},{8,14},{9,15},{10,... | collective-permute-start | bytes 798728 | tf_op jit(solution)/shard_map/ppermute | solution.py:405
  65.5 0.6 collective-permute-start.11
  66.1 0.5 collective-permute-start.12
  66.6 6.7 %collective-permute-done.13 = f16[16,8320]{1,0:T(8,128)(2,1)S(1)} collective-permute-done((f16[16,8320]{1,0:T(8,128)(2,1)S(1)}, f16[16,8320]{1,0:T(8,128)(2,1)S(1)}, u32[]{:S(2)}, u32[]{:S(2)}) %collective-permute-start.13) | collective-permute-done | bytes 266272 | tf_op jit(solution)/shard_map/ppermute | solution.py:405
  73.3 5.2 %collective-permute-done.11 = f16[16,8320]{1,0:T(8,128)(2,1)S(1)} collective-permute-done((f16[16,8320]{1,0:T(8,128)(2,1)S(1)}, f16[16,8320]{1,0:T(8,128)(2,1)S(1)}, u32[]{:S(2)}, u32[]{:S(2)}) %collective-permute-start.11) | collective-permute-done | bytes 266272 | tf_op jit(solution)/shard_map/ppermute | solution.py:405
  78.6 0.2 slice_add_fusion.6
  78.9 0.2 exponential_reduce_fusion.10
  79.2 0.2 fusion
  79.5 0.2 fusion.13
  79.9 2.4 %collective-permute-start.15 = (f16[4,8320]{1,0:T(4,128)(2,1)S(1)}, f16[4,8320]{1,0:T(4,128)(2,1)S(1)}, u32[]{:S(2)}, u32[]{:S(2)}) collective-permute-start(f16[4,8320]{1,0:T(4,128)(2,1)S(1)} %pad_maximum_fusion.7), channel_id=1, source_target_pairs={{0,16},{8,24},{16,0},{24,8},{1,17},{9,25},{17,1},{25,9},{2,18},{10... | collective-permute-start | bytes 199688 | tf_op jit(solution)/shard_map/ppermute | solution.py:405
  82.3 2.1 %collective-permute-start.16 = (f16[4,8320]{1,0:T(4,128)(2,1)S(1)}, f16[4,8320]{1,0:T(4,128)(2,1)S(1)}, u32[]{:S(2)}, u32[]{:S(2)}) collective-permute-start(f16[4,8320]{1,0:T(4,128)(2,1)S(1)} %pad_maximum_fusion.8), channel_id=1, source_target_pairs={{0,24},{8,16},{16,8},{24,0},{1,25},{9,17},{17,9},{25,1},{2,26},{10... | collective-permute-start | bytes 199688 | tf_op jit(solution)/shard_map/ppermute | solution.py:405
  84.5 0.6 collective-permute-done.14
  85.1 2.6 %collective-permute-done.15 = f16[4,8320]{1,0:T(4,128)(2,1)S(1)} collective-permute-done((f16[4,8320]{1,0:T(4,128)(2,1)S(1)}, f16[4,8320]{1,0:T(4,128)(2,1)S(1)}, u32[]{:S(2)}, u32[]{:S(2)}) %collective-permute-start.15) | collective-permute-done | bytes 66592 | tf_op jit(solution)/shard_map/ppermute | solution.py:405
  87.7 0.8 collective-permute-done.16
  88.5 0.2 fusion.51
  88.7 0.2 fusion.8
  88.9 0.8 reshape.388
  (60 shorter events, 2.8 us)
Async XLA Ops:
  0.0 7.1 %copy-start = (s32[128]{0:T(128)S(1)}, s32[128]{0:T(128)}, u32[]{:S(2)}) copy-start(s32[128]{0:T(128)} %param.8) | copy-start | bytes 1540
  0.9 7.5 %collective-permute-start = (bf16[4,8192]{1,0:T(4,128)(2,1)S(1)}, bf16[4,8192]{1,0:T(4,128)(2,1)S(1)}, u32[]{:S(2)}, u32[]{:S(2)}) collective-permute-start(bf16[4,8192]{1,0:T(4,128)(2,1)S(1)} %reshape.382), channel_id=1, source_target_pairs={{0,8},{8,0},{16,24},{24,16},{1,9},{9,1},{17,25},{25,17},{2,10},{10... | collective-permute-start | bytes 196616 | tf_op jit(solution)/shard_map/ppermute | solution.py:405
  4.0 7.3 %collective-permute-start.1 = (bf16[4,8192]{1,0:T(4,128)(2,1)S(1)}, bf16[4,8192]{1,0:T(4,128)(2,1)S(1)}, u32[]{:S(2)}, u32[]{:S(2)}) collective-permute-start(bf16[4,8192]{1,0:T(4,128)(2,1)S(1)} %reshape.382), channel_id=1, source_target_pairs={{0,16},{8,24},{16,0},{24,8},{1,17},{9,25},{17,1},{25,9},{2,18},{10... | collective-permute-start | bytes 196616 | tf_op jit(solution)/shard_map/ppermute | solution.py:405
  6.6 6.1 %collective-permute-start.2 = (bf16[4,8192]{1,0:T(4,128)(2,1)S(1)}, bf16[4,8192]{1,0:T(4,128)(2,1)S(1)}, u32[]{:S(2)}, u32[]{:S(2)}) collective-permute-start(bf16[4,8192]{1,0:T(4,128)(2,1)S(1)} %reshape.382), channel_id=1, source_target_pairs={{0,24},{8,16},{16,8},{24,0},{1,25},{9,17},{17,9},{25,1},{2,26},{10... | collective-permute-start | bytes 196616 | tf_op jit(solution)/shard_map/ppermute | solution.py:405
  12.8 16.0 %collective-permute-start.8 = (bf16[16,8192]{1,0:T(8,128)(2,1)S(1)}, bf16[16,8192]{1,0:T(8,128)(2,1)S(1)}, u32[]{:S(2)}, u32[]{:S(2)}) collective-permute-start(bf16[16,8192]{1,0:T(8,128)(2,1)S(1)} %pad_maximum_fusion.4.refs_0_), channel_id=1, source_target_pairs={{0,6},{1,7},{2,4},{3,5},{4,2},{5,3},{6,0},{7,1},{8,14},{9,15},{10,... | collective-permute-start | bytes 786440 | tf_op jit(solution)/shard_map/ppermute | solution.py:405
  15.3 13.9 %collective-permute-start.3 = (bf16[16,8192]{1,0:T(8,128)(2,1)S(1)}, bf16[16,8192]{1,0:T(8,128)(2,1)S(1)}, u32[]{:S(2)}, u32[]{:S(2)}) collective-permute-start(bf16[16,8192]{1,0:T(8,128)(2,1)S(1)} %pad_maximum_fusion.4.refs_0_), channel_id=1, source_target_pairs={{0,2},{1,3},{2,0},{3,1},{4,6},{5,7},{6,4},{7,5},{8,10},{9,11},{10,... | collective-permute-start | bytes 786440 | tf_op jit(solution)/shard_map/ppermute | solution.py:405
  15.9 13.5 %collective-permute-start.4 = (bf16[16,8192]{1,0:T(8,128)(2,1)S(1)}, bf16[16,8192]{1,0:T(8,128)(2,1)S(1)}, u32[]{:S(2)}, u32[]{:S(2)}) collective-permute-start(bf16[16,8192]{1,0:T(8,128)(2,1)S(1)} %pad_maximum_fusion.4.refs_0_), channel_id=1, source_target_pairs={{0,4},{1,5},{2,6},{3,7},{4,0},{5,1},{6,2},{7,3},{8,12},{9,13},{10,... | collective-permute-start | bytes 786440 | tf_op jit(solution)/shard_map/ppermute | solution.py:405
  28.7 10.6 %collective-permute-start.5 = (bf16[16,8192]{1,0:T(8,128)(2,1)S(1)}, bf16[16,8192]{1,0:T(8,128)(2,1)S(1)}, u32[]{:S(2)}, u32[]{:S(2)}) collective-permute-start(bf16[16,8192]{1,0:T(8,128)(2,1)S(1)} %pad_maximum_fusion.4.refs_0_), channel_id=1, source_target_pairs={{0,1},{1,0},{2,3},{3,2},{4,5},{5,4},{6,7},{7,6},{8,9},{9,8},{10,11... | collective-permute-start | bytes 786440 | tf_op jit(solution)/shard_map/ppermute | solution.py:405
  28.8 6.5 %collective-permute-start.9 = (bf16[16,8192]{1,0:T(8,128)(2,1)S(1)}, bf16[16,8192]{1,0:T(8,128)(2,1)S(1)}, u32[]{:S(2)}, u32[]{:S(2)}) collective-permute-start(bf16[16,8192]{1,0:T(8,128)(2,1)S(1)} %collective-permute-done.8.refs_0_), channel_id=1, source_target_pairs={{0,1},{1,0},{2,3},{3,2},{4,5},{5,4},{6,7},{7,6},{8,9},{9,8},{10,11... | collective-permute-start | bytes 786440 | tf_op jit(solution)/shard_map/ppermute | solution.py:405
  29.3 10.0 %collective-permute-start.6 = (bf16[16,8192]{1,0:T(8,128)(2,1)S(1)}, bf16[16,8192]{1,0:T(8,128)(2,1)S(1)}, u32[]{:S(2)}, u32[]{:S(2)}) collective-permute-start(bf16[16,8192]{1,0:T(8,128)(2,1)S(1)} %collective-permute-done.3.refs_1_), channel_id=1, source_target_pairs={{0,1},{1,0},{2,3},{3,2},{4,5},{5,4},{6,7},{7,6},{8,9},{9,8},{10,11... | collective-permute-start | bytes 786440 | tf_op jit(solution)/shard_map/ppermute | solution.py:405
  29.4 9.9 %collective-permute-start.7 = (bf16[16,8192]{1,0:T(8,128)(2,1)S(1)}, bf16[16,8192]{1,0:T(8,128)(2,1)S(1)}, u32[]{:S(2)}, u32[]{:S(2)}) collective-permute-start(bf16[16,8192]{1,0:T(8,128)(2,1)S(1)} %collective-permute-done.4.refs_2_), channel_id=1, source_target_pairs={{0,1},{1,0},{2,3},{3,2},{4,5},{5,4},{6,7},{7,6},{8,9},{9,8},{10,11... | collective-permute-start | bytes 786440 | tf_op jit(solution)/shard_map/ppermute | solution.py:405
  39.3 5.6 %copy-start.1 = (f32[512]{0:T(512)S(1)}, f32[512]{0:T(512)}, u32[]{:S(2)}) copy-start(f32[512]{0:T(512)} %param.6) | copy-start | bytes 6148
  53.3 3.9 %collective-permute-start.10 = (f16[64,8320]{1,0:T(8,128)(2,1)S(1)}, f16[64,8320]{1,0:T(8,128)(2,1)S(1)}, u32[]{:S(2)}, u32[]{:S(2)}) collective-permute-start(f16[64,8320]{1,0:T(8,128)(2,1)S(1)} %pad_maximum_fusion), channel_id=1, source_target_pairs={{0,1},{1,0},{2,3},{3,2},{4,5},{5,4},{6,7},{7,6},{8,9},{9,8},{10,11... | collective-permute-start | bytes 3194888 | tf_op jit(solution)/shard_map/ppermute | solution.py:405
  63.0 10.3 %collective-permute-start.13 = (f16[16,8320]{1,0:T(8,128)(2,1)S(1)}, f16[16,8320]{1,0:T(8,128)(2,1)S(1)}, u32[]{:S(2)}, u32[]{:S(2)}) collective-permute-start(f16[16,8320]{1,0:T(8,128)(2,1)S(1)} %pad_maximum_fusion.3), channel_id=1, source_target_pairs={{0,6},{1,7},{2,4},{3,5},{4,2},{5,3},{6,0},{7,1},{8,14},{9,15},{10,... | collective-permute-start | bytes 798728 | tf_op jit(solution)/shard_map/ppermute | solution.py:405
  65.5 13.0 %collective-permute-start.11 = (f16[16,8320]{1,0:T(8,128)(2,1)S(1)}, f16[16,8320]{1,0:T(8,128)(2,1)S(1)}, u32[]{:S(2)}, u32[]{:S(2)}) collective-permute-start(f16[16,8320]{1,0:T(8,128)(2,1)S(1)} %pad_maximum_fusion.1), channel_id=1, source_target_pairs={{0,2},{1,3},{2,0},{3,1},{4,6},{5,7},{6,4},{7,5},{8,10},{9,11},{10,... | collective-permute-start | bytes 798728 | tf_op jit(solution)/shard_map/ppermute | solution.py:405
  66.1 12.5 %collective-permute-start.12 = (f16[16,8320]{1,0:T(8,128)(2,1)S(1)}, f16[16,8320]{1,0:T(8,128)(2,1)S(1)}, u32[]{:S(2)}, u32[]{:S(2)}) collective-permute-start(f16[16,8320]{1,0:T(8,128)(2,1)S(1)} %pad_maximum_fusion.2), channel_id=1, source_target_pairs={{0,4},{1,5},{2,6},{3,7},{4,0},{5,1},{6,2},{7,3},{8,12},{9,13},{10,... | collective-permute-start | bytes 798728 | tf_op jit(solution)/shard_map/ppermute | solution.py:405
  79.8 5.3 %collective-permute-start.14 = (f16[4,8320]{1,0:T(4,128)(2,1)S(1)}, f16[4,8320]{1,0:T(4,128)(2,1)S(1)}, u32[]{:S(2)}, u32[]{:S(2)}) collective-permute-start(f16[4,8320]{1,0:T(4,128)(2,1)S(1)} %pad_maximum_fusion.6), channel_id=1, source_target_pairs={{0,8},{8,0},{16,24},{24,16},{1,9},{9,1},{17,25},{25,17},{2,10},{10... | collective-permute-start | bytes 199688 | tf_op jit(solution)/shard_map/ppermute | solution.py:405
  79.9 7.8 %collective-permute-start.15 = (f16[4,8320]{1,0:T(4,128)(2,1)S(1)}, f16[4,8320]{1,0:T(4,128)(2,1)S(1)}, u32[]{:S(2)}, u32[]{:S(2)}) collective-permute-start(f16[4,8320]{1,0:T(4,128)(2,1)S(1)} %pad_maximum_fusion.7), channel_id=1, source_target_pairs={{0,16},{8,24},{16,0},{24,8},{1,17},{9,25},{17,1},{25,9},{2,18},{10... | collective-permute-start | bytes 199688 | tf_op jit(solution)/shard_map/ppermute | solution.py:405
  82.3 6.1 %collective-permute-start.16 = (f16[4,8320]{1,0:T(4,128)(2,1)S(1)}, f16[4,8320]{1,0:T(4,128)(2,1)S(1)}, u32[]{:S(2)}, u32[]{:S(2)}) collective-permute-start(f16[4,8320]{1,0:T(4,128)(2,1)S(1)} %pad_maximum_fusion.8), channel_id=1, source_target_pairs={{0,24},{8,16},{16,8},{24,0},{1,25},{9,17},{17,9},{25,1},{2,26},{10... | collective-permute-start | bytes 199688 | tf_op jit(solution)/shard_map/ppermute | solution.py:405

commit v4 on v3

--- a/solution.py
+++ b/solution.py
@@ -26,14 +26,16 @@
     return [pl.BlockSpec(memory_space=pltpu.VMEM)] * count
 
 
-def relay_kernel(rows, in_ref, out_ref, taken_ref, wide_ref, peak_ref, sems):
+def relay_kernel(in_ref, out_ref, taken_ref, wide_ref, peak_ref, sems):
     count, per, _ = in_ref.shape
-    blocks = per // rows
+    some = taken_ref.shape[1]
+    rows = peak_ref.shape[0]
+    blocks = count // some
     last = out_ref.shape[0]
 
     def fetch(block, slot):
         return pltpu.make_async_copy(
-            in_ref.at[:, pl.ds(block * rows, rows), :], taken_ref.at[slot], sems.at[slot]
+            in_ref.at[pl.ds(block * some, some)], taken_ref.at[slot], sems.at[slot]
         )
 
     fetch(0, 0).start()
@@ -47,16 +49,18 @@
             fetch(block + 1, 1 - slot).start()
 
         fetch(block, slot).wait()
-        base = pl.multiple_of(block * rows * LANES, rows * LANES)
+        base = pl.multiple_of(block * some, some)
         peak = peak_ref[...]
-        for n in range(0, count, 16):
-            wide = taken_ref[slot, n : n + 16].astype(jnp.float32)
-            wide_ref[n * rows : (n + 16) * rows, :] = wide.reshape(16 * rows, LANES)
-            peak = jnp.maximum(peak, jnp.max(jnp.abs(wide), axis=0))
-            for r in range(rows):
-                picked = wide_ref[pl.ds(n * rows + r, 16, stride=rows), :]
-                at = pl.ds(base + r * LANES, LANES)
-                out_ref[n : n + 16, at] = picked.astype(jnp.bfloat16)
+        for n in range(0, some, 16):
+            for r in range(0, per, rows):
+                wide = taken_ref[slot, n : n + 16, r : r + rows, :].astype(jnp.float32)
+                start = (n * per) + 16 * r
+                wide_ref[start : start + 16 * rows, :] = wide.reshape(16 * rows, LANES)
+                peak = jnp.maximum(peak, jnp.max(jnp.abs(wide), axis=0))
+                for k in range(rows):
+                    picked = wide_ref[pl.ds(start + k, 16, stride=rows), :]
+                    at = (r + k) * LANES
+                    out_ref[pl.ds(base + n, 16), at : at + LANES] = picked.astype(jnp.bfloat16)
         peak_ref[...] = peak
         return carry
 
@@ -71,17 +75,18 @@
     count, parts, coeffs = images.shape
     groups = coeffs // LANES
     per = parts * groups
+    some = min(count, 64)
     flat = images.reshape(count, parts, groups, LANES)
     flat = flat.transpose(0, 2, 1, 3).reshape(count, per, LANES)
     flat = pltpu.with_memory_space_constraint(flat, pltpu.HBM)
     return pl.pallas_call(
-        functools.partial(relay_kernel, rows),
+        relay_kernel,
         in_specs=[pl.BlockSpec(memory_space=pltpu.HBM)],
         out_specs=pl.BlockSpec(memory_space=pltpu.VMEM),
         out_shape=jax.ShapeDtypeStruct((count + spare, per * LANES), jnp.bfloat16),
         scratch_shapes=[
-            pltpu.VMEM((2, count, rows, LANES), jnp.bfloat16),
-            pltpu.VMEM((count * rows, LANES), jnp.float32),
+            pltpu.VMEM((2, some, per, LANES), jnp.bfloat16),
+            pltpu.VMEM((some * per, LANES), jnp.float32),
             pltpu.VMEM((rows, LANES), jnp.float32),
             pltpu.SemaphoreType.DMA((2,)),
         ],

time: 90 us -> 90.2 us (level)
  transfers between devices with their start and end apart: 17 -> 17, of which waited for: 7 -> 7; matrix products, arithmetic and copies ran while one was open for 4% -> 4% of each run, Pallas kernels for 26% -> 27%
where the time goes in v4:
time: 90.2 us; the launch traced here: 89.9 us
  Pallas kernels  40.7 us (45%)
  waiting for transfers between devices  20.2 us (22%)
  starting transfers between devices  18.6 us (21%)
  local copies, waits for them, and re-layouts  5.28 us (6%)
  other arithmetic  4.63 us (5%)
    ppermute x17, waiting for transfers between devices, exchange(): return lax.ppermute(value, axis, [(i, i ^ bit) for i in range(size)])  20.2 us
    ppermute x17, starting transfers between devices, exchange(): return lax.ppermute(value, axis, [(i, i ^ bit) for i in range(size)])  18.6 us
    pallas_call x3, Pallas kernels, scores_of(): pl.pallas_call(functools.partial(score_kernel, places, shifts), in_specs=...  15 us
    pallas_call x3, Pallas kernels, back_of(): pl.pallas_call(functools.partial(back_kernel, first, pieces, shifts), in_...  13.9 us
    pallas_call x1, Pallas kernels, relay(): pl.pallas_call(relay_kernel, in_specs=[pl.BlockSpec(memory_space=pltpu.HB...  7.86 us
    pallas_call x1, Pallas kernels, phases_of(): pl.pallas_call(phase_kernel, in_specs=whole_in_vmem(2), out_specs=tuple(w...  2.78 us
  transfers between devices with their start and end apart: 17, of which 7 were waited for; matrix products, arithmetic and copies ran while one was open for 4% of the time, Pallas kernels for 27%

profile of v4, /device:TPU:0, one launch (start us, length us, event | category | flops | bytes accessed | tf_op | source)
XLA Modules:
  0.0 89.9 jit_solution(2717296767898127053)
XLA Ops:
  0.0 0.9 reshape.382
  0.9 3.1 %collective-permute-start = (bf16[4,8192]{1,0:T(4,128)(2,1)S(1)}, bf16[4,8192]{1,0:T(4,128)(2,1)S(1)}, u32[]{:S(2)}, u32[]{:S(2)}) collective-permute-start(bf16[4,8192]{1,0:T(4,128)(2,1)S(1)} %reshape.382), channel_id=1, source_target_pairs={{0,8},{8,0},{16,24},{24,16},{1,9},{9,1},{17,25},{25,17},{2,10},{10... | collective-permute-start | bytes 196616 | tf_op jit(solution)/shard_map/ppermute | solution.py:410
  4.0 2.6 %collective-permute-start.1 = (bf16[4,8192]{1,0:T(4,128)(2,1)S(1)}, bf16[4,8192]{1,0:T(4,128)(2,1)S(1)}, u32[]{:S(2)}, u32[]{:S(2)}) collective-permute-start(bf16[4,8192]{1,0:T(4,128)(2,1)S(1)} %reshape.382), channel_id=1, source_target_pairs={{0,16},{8,24},{16,0},{24,8},{1,17},{9,25},{17,1},{25,9},{2,18},{10... | collective-permute-start | bytes 196616 | tf_op jit(solution)/shard_map/ppermute | solution.py:410
  6.8 0.2 fusion.16
  7.1 1.2 %gather_fusion = s32[128]{0:T(128)S(1)} fusion(s32[128]{0:T(128)S(1)} %copy-done, s32[1024]{0:T(1024)S(1)} %pad_clamp_fusion.1), kind=kCustom, calls=%fused_computation | custom fusion | bytes 1536 | tf_op jit(solution)/shard_map/gather | solution.py:444
  8.4 2.9 %collective-permute-done.1 = bf16[4,8192]{1,0:T(4,128)(2,1)S(1)} collective-permute-done((bf16[4,8192]{1,0:T(4,128)(2,1)S(1)}, bf16[4,8192]{1,0:T(4,128)(2,1)S(1)}, u32[]{:S(2)}, u32[]{:S(2)}) %collective-permute-start.1) | collective-permute-done | bytes 65568 | tf_op jit(solution)/shard_map/ppermute | solution.py:410
  11.3 1.4 %collective-permute-done.2 = bf16[4,8192]{1,0:T(4,128)(2,1)S(1)} collective-permute-done((bf16[4,8192]{1,0:T(4,128)(2,1)S(1)}, bf16[4,8192]{1,0:T(4,128)(2,1)S(1)}, u32[]{:S(2)}, u32[]{:S(2)}) %collective-permute-start.2) | collective-permute-done | bytes 65568 | tf_op jit(solution)/shard_map/ppermute | solution.py:410
  12.8 2.5 %collective-permute-start.8 = (bf16[16,8192]{1,0:T(8,128)(2,1)S(1)}, bf16[16,8192]{1,0:T(8,128)(2,1)S(1)}, u32[]{:S(2)}, u32[]{:S(2)}) collective-permute-start(bf16[16,8192]{1,0:T(8,128)(2,1)S(1)} %pad_maximum_fusion.4.refs_0_), channel_id=1, source_target_pairs={{0,6},{1,7},{2,4},{3,5},{4,2},{5,3},{6,0},{7,1},{8,14},{9,15},{10,... | collective-permute-start | bytes 786440 | tf_op jit(solution)/shard_map/ppermute | solution.py:410
  15.3 0.5 collective-permute-start.3
  15.9 0.5 collective-permute-start.4
  16.4 0.8 copy.18
  17.2 0.6 gather_fusion.1
  17.9 0.3 reshape.406.shift_ref
  18.2 7.9 %shard_map.56.refs_9_.refs_8_.refs_7_.x_ref = bf16[528,8192]{1,0:T(8,128)(2,1)S(1)} custom-call(bf16[512,64,128]{2,1,0:T(8,128)(2,1)} %bitcast.21), custom_call_target="tpu_custom_call" | custom-call | flops 4194304 | bytes 16777216 | tf_op jit(solution)/shard_map/pallas_call | solution.py:82
  26.1 2.8 %shard_map.55 = (f32[16,512,128]{2,1,0:T(8,128)S(1)}, f32[16,512,128]{2,1,0:T(8,128)S(1)}, f32[512,128]{1,0:T(8,128)S(1)}, f32[16,512,128]{2,1,0:T(8,128)S(1)}, ...) custom-call(s32[1024,1]{1,0:T(8,128)S(1)} %reshape.406.shift_ref, f32[64,512]{1,0:T(8,128)S(1)} %pad_maximum_fusion.5.table_ref), custom_call_target="tpu_custom_call" | custom-call | flops 12582912 | bytes 16777216 | tf_op jit(solution)/shard_map/pallas_call | solution.py:143
  29.0 0.5 collective-permute-start.9
  29.6 0.4 collective-permute-start.7
  30.0 5.5 %shard_map.57 = (f32[384,512]{1,0:T(8,128)S(1)}, f32[48,128]{1,0:T(8,128)S(1)}) custom-call(bf16[16,8192]{1,0:T(8,128)(2,1)S(1)} %pad_maximum_fusion.4.refs_0_, bf16[16,8192]{1,0:T(8,128)(2,1)S(1)} %collective-permute-done.3.refs_1_, bf16[16,8192]{1,0:T(8,128)(2,1)S(1)} %collective-permute-done.4.refs_2_, ...), custom_call_target="tpu_custom_call" | custom-call | flops 3221225472 | bytes 9961472 | tf_op jit(solution)/shard_map/pallas_call | solution.py:242
  35.5 3.9 %shard_map.59 = (f32[256,512]{1,0:T(8,128)S(1)}, f32[32,128]{1,0:T(8,128)S(1)}) custom-call(bf16[16,8192]{1,0:T(8,128)(2,1)S(1)} %collective-permute-done.8.refs_0_, bf16[16,8192]{1,0:T(8,128)(2,1)S(1)} %collective-permute-done.9.refs_1_, f32[16,512,128]{2,1,0:T(8,128)S(1)} %get-tuple-element.26.refs_3_.refs_2_.cos_ref, ...), custom_call_target="tpu_custom_call" | custom-call | flops 2147483648 | bytes 9437184 | tf_op jit(solution)/shard_map/pallas_call | solution.py:242
  39.5 5.6 %shard_map.58 = (f32[384,512]{1,0:T(8,128)S(1)}, f32[48,128]{1,0:T(8,128)S(1)}) custom-call(bf16[16,8192]{1,0:T(8,128)(2,1)S(1)} %collective-permute-done.5.refs_0_, bf16[16,8192]{1,0:T(8,128)(2,1)S(1)} %collective-permute-done.6.refs_1_, bf16[16,8192]{1,0:T(8,128)(2,1)S(1)} %collective-permute-done.7.refs_2_, ...), custom_call_target="tpu_custom_call" | custom-call | flops 3221225472 | bytes 9961472 | tf_op jit(solution)/shard_map/pallas_call | solution.py:242
  45.1 1.2 %shard_map.60 = (bf16[512,512]{1,0:T(8,128)(2,1)S(1)}, bf16[512,512]{1,0:T(8,128)(2,1)S(1)}, f32[64,128]{1,0:T(8,128)S(1)}, f32[64,128]{1,0:T(8,128)S(1)}, f32[64,128]{1,0:T(8,128)S(1)}, /*index=5*/f32[64,128]{1,0:T(8,128)S(1)}) custom-call(f32[384,512]{1,0:T(8,128)S(1)} %get-tuple-element.32.refs_0_, f32[384,512]{1,0:T(8,128)S(1)} %get-tuple-element.33.refs_1_, ...), custom_call_target="tpu_custom_call" | custom-call | flops 10485760 | bytes 6291456 | tf_op jit(solution)/shard_map/pallas_call | solution.py:311
  46.3 6.3 %shard_map.62 = f32[64,8192]{1,0:T(8,128)S(1)} custom-call(bf16[512,512]{1,0:T(8,128)(2,1)S(1)} %get-tuple-element.39.w_ref, f32[16,512,128]{2,1,0:T(8,128)S(1)} %get-tuple-element.29.refs_6_.refs_5_.cos_ref, f32[16,512,128]{2,1,0:T(8,128)S(1)} %get-tuple-element.30.refs_7_.refs_6_.sin_ref, f32[512,128]{1,0:T(8,128)S(1)} %get-tuple-element.31.refs_8_.refs_7_.sign_ref, ...), custom_call_target="tpu_custom_call" | custom-call | flops 4294967296 | bytes 9043968 | tf_op jit(solution)/shard_map/pallas_call | solution.py:394
  52.9 0.2 multiply_convert_fusion
  53.2 0.2 pad_maximum_fusion
  53.6 3.8 %shard_map.61 = f32[32,8192]{1,0:T(8,128)S(1)} custom-call(bf16[512,512]{1,0:T(8,128)(2,1)S(1)} %get-tuple-element.44.w_ref, f32[16,512,128]{2,1,0:T(8,128)S(1)} %get-tuple-element.26.refs_3_.refs_2_.cos_ref, f32[16,512,128]{2,1,0:T(8,128)S(1)} %get-tuple-element.27.refs_4_.refs_3_.sin_ref, f32[512,128]{1,0:T(8,128)S(1)} %get-tuple-element.28.refs_5_.refs_4_.sign_ref, ...), custom_call_target="tpu_custom_call" | custom-call | flops 2147483648 | bytes 8716288 | tf_op jit(solution)/shard_map/pallas_call | solution.py:394
  57.5 0.2 exponential_reduce_fusion
  57.7 0.2 slice_multiply_fusion
  58.0 0.2 exponential_reduce_fusion.6
  58.5 0.2 slice_add_fusion.1
  59.1 3.8 %shard_map.63 = f32[32,8192]{1,0:T(8,128)S(1)} custom-call(bf16[512,512]{1,0:T(8,128)(2,1)S(1)} %get-tuple-element.44.w_ref, f32[16,512,128]{2,1,0:T(8,128)S(1)} %get-tuple-element.26.refs_3_.refs_2_.cos_ref, f32[16,512,128]{2,1,0:T(8,128)S(1)} %get-tuple-element.27.refs_4_.refs_3_.sin_ref, f32[512,128]{1,0:T(8,128)S(1)} %get-tuple-element.28.refs_5_.refs_4_.sign_ref, ...), custom_call_target="tpu_custom_call" | custom-call | flops 2147483648 | bytes 8716288 | tf_op jit(solution)/shard_map/pallas_call | solution.py:394
  62.9 0.2 slice_add_fusion
  63.2 2.5 %collective-permute-start.13 = (f16[16,8320]{1,0:T(8,128)(2,1)S(1)}, f16[16,8320]{1,0:T(8,128)(2,1)S(1)}, u32[]{:S(2)}, u32[]{:S(2)}) collective-permute-start(f16[16,8320]{1,0:T(8,128)(2,1)S(1)} %pad_maximum_fusion.3), channel_id=1, source_target_pairs={{0,6},{1,7},{2,4},{3,5},{4,2},{5,3},{6,0},{7,1},{8,14},{9,15},{10,... | collective-permute-start | bytes 798728 | tf_op jit(solution)/shard_map/ppermute | solution.py:410
  65.7 0.5 collective-permute-start.11
  66.3 0.5 collective-permute-start.12
  66.8 6.7 %collective-permute-done.13 = f16[16,8320]{1,0:T(8,128)(2,1)S(1)} collective-permute-done((f16[16,8320]{1,0:T(8,128)(2,1)S(1)}, f16[16,8320]{1,0:T(8,128)(2,1)S(1)}, u32[]{:S(2)}, u32[]{:S(2)}) %collective-permute-start.13) | collective-permute-done | bytes 266272 | tf_op jit(solution)/shard_map/ppermute | solution.py:410
  73.5 5.2 %collective-permute-done.11 = f16[16,8320]{1,0:T(8,128)(2,1)S(1)} collective-permute-done((f16[16,8320]{1,0:T(8,128)(2,1)S(1)}, f16[16,8320]{1,0:T(8,128)(2,1)S(1)}, u32[]{:S(2)}, u32[]{:S(2)}) %collective-permute-start.11) | collective-permute-done | bytes 266272 | tf_op jit(solution)/shard_map/ppermute | solution.py:410
  78.8 0.2 slice_add_fusion.6
  79.0 0.2 exponential_reduce_fusion.10
  79.4 0.2 fusion
  79.6 0.2 fusion.13
  80.1 2.4 %collective-permute-start.15 = (f16[4,8320]{1,0:T(4,128)(2,1)S(1)}, f16[4,8320]{1,0:T(4,128)(2,1)S(1)}, u32[]{:S(2)}, u32[]{:S(2)}) collective-permute-start(f16[4,8320]{1,0:T(4,128)(2,1)S(1)} %pad_maximum_fusion.7), channel_id=1, source_target_pairs={{0,16},{8,24},{16,0},{24,8},{1,17},{9,25},{17,1},{25,9},{2,18},{10... | collective-permute-start | bytes 199688 | tf_op jit(solution)/shard_map/ppermute | solution.py:410
  82.5 2.1 %collective-permute-start.16 = (f16[4,8320]{1,0:T(4,128)(2,1)S(1)}, f16[4,8320]{1,0:T(4,128)(2,1)S(1)}, u32[]{:S(2)}, u32[]{:S(2)}) collective-permute-start(f16[4,8320]{1,0:T(4,128)(2,1)S(1)} %pad_maximum_fusion.8), channel_id=1, source_target_pairs={{0,24},{8,16},{16,8},{24,0},{1,25},{9,17},{17,9},{25,1},{2,26},{10... | collective-permute-start | bytes 199688 | tf_op jit(solution)/shard_map/ppermute | solution.py:410
  84.6 0.7 collective-permute-done.14
  85.3 2.5 %collective-permute-done.15 = f16[4,8320]{1,0:T(4,128)(2,1)S(1)} collective-permute-done((f16[4,8320]{1,0:T(4,128)(2,1)S(1)}, f16[4,8320]{1,0:T(4,128)(2,1)S(1)}, u32[]{:S(2)}, u32[]{:S(2)}) %collective-permute-start.15) | collective-permute-done | bytes 66592 | tf_op jit(solution)/shard_map/ppermute | solution.py:410
  87.9 0.8 collective-permute-done.16
  88.7 0.2 fusion.51
  88.9 0.2 fusion.8
  89.1 0.8 reshape.388
  (60 shorter events, 2.8 us)
Async XLA Ops:
  0.0 7.1 %copy-start = (s32[128]{0:T(128)S(1)}, s32[128]{0:T(128)}, u32[]{:S(2)}) copy-start(s32[128]{0:T(128)} %param.8) | copy-start | bytes 1540
  0.9 7.5 %collective-permute-start = (bf16[4,8192]{1,0:T(4,128)(2,1)S(1)}, bf16[4,8192]{1,0:T(4,128)(2,1)S(1)}, u32[]{:S(2)}, u32[]{:S(2)}) collective-permute-start(bf16[4,8192]{1,0:T(4,128)(2,1)S(1)} %reshape.382), channel_id=1, source_target_pairs={{0,8},{8,0},{16,24},{24,16},{1,9},{9,1},{17,25},{25,17},{2,10},{10... | collective-permute-start | bytes 196616 | tf_op jit(solution)/shard_map/ppermute | solution.py:410
  4.0 7.3 %collective-permute-start.1 = (bf16[4,8192]{1,0:T(4,128)(2,1)S(1)}, bf16[4,8192]{1,0:T(4,128)(2,1)S(1)}, u32[]{:S(2)}, u32[]{:S(2)}) collective-permute-start(bf16[4,8192]{1,0:T(4,128)(2,1)S(1)} %reshape.382), channel_id=1, source_target_pairs={{0,16},{8,24},{16,0},{24,8},{1,17},{9,25},{17,1},{25,9},{2,18},{10... | collective-permute-start | bytes 196616 | tf_op jit(solution)/shard_map/ppermute | solution.py:410
  6.6 6.1 %collective-permute-start.2 = (bf16[4,8192]{1,0:T(4,128)(2,1)S(1)}, bf16[4,8192]{1,0:T(4,128)(2,1)S(1)}, u32[]{:S(2)}, u32[]{:S(2)}) collective-permute-start(bf16[4,8192]{1,0:T(4,128)(2,1)S(1)} %reshape.382), channel_id=1, source_target_pairs={{0,24},{8,16},{16,8},{24,0},{1,25},{9,17},{17,9},{25,1},{2,26},{10... | collective-permute-start | bytes 196616 | tf_op jit(solution)/shard_map/ppermute | solution.py:410
  12.8 16.1 %collective-permute-start.8 = (bf16[16,8192]{1,0:T(8,128)(2,1)S(1)}, bf16[16,8192]{1,0:T(8,128)(2,1)S(1)}, u32[]{:S(2)}, u32[]{:S(2)}) collective-permute-start(bf16[16,8192]{1,0:T(8,128)(2,1)S(1)} %pad_maximum_fusion.4.refs_0_), channel_id=1, source_target_pairs={{0,6},{1,7},{2,4},{3,5},{4,2},{5,3},{6,0},{7,1},{8,14},{9,15},{10,... | collective-permute-start | bytes 786440 | tf_op jit(solution)/shard_map/ppermute | solution.py:410
  15.3 14.1 %collective-permute-start.3 = (bf16[16,8192]{1,0:T(8,128)(2,1)S(1)}, bf16[16,8192]{1,0:T(8,128)(2,1)S(1)}, u32[]{:S(2)}, u32[]{:S(2)}) collective-permute-start(bf16[16,8192]{1,0:T(8,128)(2,1)S(1)} %pad_maximum_fusion.4.refs_0_), channel_id=1, source_target_pairs={{0,2},{1,3},{2,0},{3,1},{4,6},{5,7},{6,4},{7,5},{8,10},{9,11},{10,... | collective-permute-start | bytes 786440 | tf_op jit(solution)/shard_map/ppermute | solution.py:410
  15.9 13.7 %collective-permute-start.4 = (bf16[16,8192]{1,0:T(8,128)(2,1)S(1)}, bf16[16,8192]{1,0:T(8,128)(2,1)S(1)}, u32[]{:S(2)}, u32[]{:S(2)}) collective-permute-start(bf16[16,8192]{1,0:T(8,128)(2,1)S(1)} %pad_maximum_fusion.4.refs_0_), channel_id=1, source_target_pairs={{0,4},{1,5},{2,6},{3,7},{4,0},{5,1},{6,2},{7,3},{8,12},{9,13},{10,... | collective-permute-start | bytes 786440 | tf_op jit(solution)/shard_map/ppermute | solution.py:410
  28.9 10.6 %collective-permute-start.5 = (bf16[16,8192]{1,0:T(8,128)(2,1)S(1)}, bf16[16,8192]{1,0:T(8,128)(2,1)S(1)}, u32[]{:S(2)}, u32[]{:S(2)}) collective-permute-start(bf16[16,8192]{1,0:T(8,128)(2,1)S(1)} %pad_maximum_fusion.4.refs_0_), channel_id=1, source_target_pairs={{0,1},{1,0},{2,3},{3,2},{4,5},{5,4},{6,7},{7,6},{8,9},{9,8},{10,11... | collective-permute-start | bytes 786440 | tf_op jit(solution)/shard_map/ppermute | solution.py:410
  29.0 6.5 %collective-permute-start.9 = (bf16[16,8192]{1,0:T(8,128)(2,1)S(1)}, bf16[16,8192]{1,0:T(8,128)(2,1)S(1)}, u32[]{:S(2)}, u32[]{:S(2)}) collective-permute-start(bf16[16,8192]{1,0:T(8,128)(2,1)S(1)} %collective-permute-done.8.refs_0_), channel_id=1, source_target_pairs={{0,1},{1,0},{2,3},{3,2},{4,5},{5,4},{6,7},{7,6},{8,9},{9,8},{10,11... | collective-permute-start | bytes 786440 | tf_op jit(solution)/shard_map/ppermute | solution.py:410
  29.5 10.0 %collective-permute-start.6 = (bf16[16,8192]{1,0:T(8,128)(2,1)S(1)}, bf16[16,8192]{1,0:T(8,128)(2,1)S(1)}, u32[]{:S(2)}, u32[]{:S(2)}) collective-permute-start(bf16[16,8192]{1,0:T(8,128)(2,1)S(1)} %collective-permute-done.3.refs_1_), channel_id=1, source_target_pairs={{0,1},{1,0},{2,3},{3,2},{4,5},{5,4},{6,7},{7,6},{8,9},{9,8},{10,11... | collective-permute-start | bytes 786440 | tf_op jit(solution)/shard_map/ppermute | solution.py:410
  29.6 9.9 %collective-permute-start.7 = (bf16[16,8192]{1,0:T(8,128)(2,1)S(1)}, bf16[16,8192]{1,0:T(8,128)(2,1)S(1)}, u32[]{:S(2)}, u32[]{:S(2)}) collective-permute-start(bf16[16,8192]{1,0:T(8,128)(2,1)S(1)} %collective-permute-done.4.refs_2_), channel_id=1, source_target_pairs={{0,1},{1,0},{2,3},{3,2},{4,5},{5,4},{6,7},{7,6},{8,9},{9,8},{10,11... | collective-permute-start | bytes 786440 | tf_op jit(solution)/shard_map/ppermute | solution.py:410
  39.5 5.6 %copy-start.1 = (f32[512]{0:T(512)S(1)}, f32[512]{0:T(512)}, u32[]{:S(2)}) copy-start(f32[512]{0:T(512)} %param.6) | copy-start | bytes 6148
  53.5 3.9 %collective-permute-start.10 = (f16[64,8320]{1,0:T(8,128)(2,1)S(1)}, f16[64,8320]{1,0:T(8,128)(2,1)S(1)}, u32[]{:S(2)}, u32[]{:S(2)}) collective-permute-start(f16[64,8320]{1,0:T(8,128)(2,1)S(1)} %pad_maximum_fusion), channel_id=1, source_target_pairs={{0,1},{1,0},{2,3},{3,2},{4,5},{5,4},{6,7},{7,6},{8,9},{9,8},{10,11... | collective-permute-start | bytes 3194888 | tf_op jit(solution)/shard_map/ppermute | solution.py:410
  63.2 10.3 %collective-permute-start.13 = (f16[16,8320]{1,0:T(8,128)(2,1)S(1)}, f16[16,8320]{1,0:T(8,128)(2,1)S(1)}, u32[]{:S(2)}, u32[]{:S(2)}) collective-permute-start(f16[16,8320]{1,0:T(8,128)(2,1)S(1)} %pad_maximum_fusion.3), channel_id=1, source_target_pairs={{0,6},{1,7},{2,4},{3,5},{4,2},{5,3},{6,0},{7,1},{8,14},{9,15},{10,... | collective-permute-start | bytes 798728 | tf_op jit(solution)/shard_map/ppermute | solution.py:410
  65.7 13.0 %collective-permute-start.11 = (f16[16,8320]{1,0:T(8,128)(2,1)S(1)}, f16[16,8320]{1,0:T(8,128)(2,1)S(1)}, u32[]{:S(2)}, u32[]{:S(2)}) collective-permute-start(f16[16,8320]{1,0:T(8,128)(2,1)S(1)} %pad_maximum_fusion.1), channel_id=1, source_target_pairs={{0,2},{1,3},{2,0},{3,1},{4,6},{5,7},{6,4},{7,5},{8,10},{9,11},{10,... | collective-permute-start | bytes 798728 | tf_op jit(solution)/shard_map/ppermute | solution.py:410
  66.3 12.5 %collective-permute-start.12 = (f16[16,8320]{1,0:T(8,128)(2,1)S(1)}, f16[16,8320]{1,0:T(8,128)(2,1)S(1)}, u32[]{:S(2)}, u32[]{:S(2)}) collective-permute-start(f16[16,8320]{1,0:T(8,128)(2,1)S(1)} %pad_maximum_fusion.2), channel_id=1, source_target_pairs={{0,4},{1,5},{2,6},{3,7},{4,0},{5,1},{6,2},{7,3},{8,12},{9,13},{10,... | collective-permute-start | bytes 798728 | tf_op jit(solution)/shard_map/ppermute | solution.py:410
  80.0 5.4 %collective-permute-start.14 = (f16[4,8320]{1,0:T(4,128)(2,1)S(1)}, f16[4,8320]{1,0:T(4,128)(2,1)S(1)}, u32[]{:S(2)}, u32[]{:S(2)}) collective-permute-start(f16[4,8320]{1,0:T(4,128)(2,1)S(1)} %pad_maximum_fusion.6), channel_id=1, source_target_pairs={{0,8},{8,0},{16,24},{24,16},{1,9},{9,1},{17,25},{25,17},{2,10},{10... | collective-permute-start | bytes 199688 | tf_op jit(solution)/shard_map/ppermute | solution.py:410
  80.1 7.8 %collective-permute-start.15 = (f16[4,8320]{1,0:T(4,128)(2,1)S(1)}, f16[4,8320]{1,0:T(4,128)(2,1)S(1)}, u32[]{:S(2)}, u32[]{:S(2)}) collective-permute-start(f16[4,8320]{1,0:T(4,128)(2,1)S(1)} %pad_maximum_fusion.7), channel_id=1, source_target_pairs={{0,16},{8,24},{16,0},{24,8},{1,17},{9,25},{17,1},{25,9},{2,18},{10... | collective-permute-start | bytes 199688 | tf_op jit(solution)/shard_map/ppermute | solution.py:410
  82.5 6.1 %collective-permute-start.16 = (f16[4,8320]{1,0:T(4,128)(2,1)S(1)}, f16[4,8320]{1,0:T(4,128)(2,1)S(1)}, u32[]{:S(2)}, u32[]{:S(2)}) collective-permute-start(f16[4,8320]{1,0:T(4,128)(2,1)S(1)} %pad_maximum_fusion.8), channel_id=1, source_target_pairs={{0,24},{8,16},{16,8},{24,0},{1,25},{9,17},{17,9},{25,1},{2,26},{10... | collective-permute-start | bytes 199688 | tf_op jit(solution)/shard_map/ppermute | solution.py:410

commit v5 on v4

--- a/solution.py
+++ b/solution.py
@@ -14,7 +14,7 @@
 PRIOR_WEIGHT = 4.0
 LANES = 128
 PAIR = 2 * LANES
-UNROLL = 4
+UNROLL = 8
 WIRE = jnp.float16
 VMEM_LIMIT = 8 << 20
 RELAY_LIMIT = 12 << 20
@@ -99,24 +99,52 @@
     )(flat)
 
 
-def phase_kernel(shift_ref, table_ref, *refs):
-    outs, first_ref = refs[:6], refs[6]
+def phase_kernel(local, quads, id_ref, shifts_ref, table_ref, *refs):
+    outs, first_ref, chosen_ref = refs[:6], refs[6], refs[7]
     count, rows, _ = outs[0].shape
     number = table_ref.shape[0]
+    shifts, templates = shifts_ref.shape
+    held = templates // 2
+    piece_rows = held // quads
+    in_row = piece_rows // local
+
+    position = lax.broadcasted_iota(jnp.int32, (templates, templates), 0)
+    lane = lax.broadcasted_iota(jnp.int32, (templates, templates), 1)
+    at_local = lax.rem(position, local)
+    at_row = lax.rem(lax.div(position, local), in_row) ^ lax.axis_index("row")
+    at_quad = lax.rem(lax.div(position, piece_rows) + 1, quads)
+    at_col = (2 * at_quad + lax.div(position, held)) ^ lax.axis_index("col")
+    slots = (at_row * (2 * quads) + at_col) * local + at_local
+    names = jnp.where(slots == lane, id_ref[...].astype(jnp.float32), 0.0)
+    names = jnp.sum(names, axis=1, keepdims=True)
+    named = jnp.where(names == lane.astype(jnp.float32), 1.0, 0.0).astype(jnp.bfloat16)
+    shift = lax.dot_general(
+        named,
+        shifts_ref[...].astype(jnp.float32).astype(jnp.bfloat16),
+        (((1,), (1,)), ((), ())),
+        preferred_element_type=jnp.float32,
+    )
+
     rest, parts = table_ref[...], []
     for _ in range(3):
         part = rest.astype(jnp.bfloat16)
         parts.append(part)
         rest = rest - part.astype(jnp.float32)
     parts = jnp.concatenate(parts, axis=0)
-    numbers = lax.rem(lax.broadcasted_iota(jnp.int32, (rows, 3 * number), 1), number)
+    numbers = lax.broadcasted_iota(jnp.int32, (piece_rows, 3 * number), 1)
+    numbers = lax.rem(numbers, number).astype(jnp.float32)
     for half in range(2):
         cos_ref, sin_ref, sign_ref = outs[3 * half : 3 * half + 3]
-        chosen = shift_ref[half * rows : (half + 1) * rows, :] == numbers
+        for place in range(quads):
+            at = half * held + place * piece_rows
+            for j in range(shifts):
+                hit = shift[at : at + piece_rows, j : j + 1] == numbers
+                to = (place * shifts + j) * piece_rows
+                chosen_ref[to : to + piece_rows, :] = jnp.where(hit, 1.0, 0.0).astype(
+                    jnp.bfloat16
+                )
         first_ref[...] = jnp.dot(
-            jnp.where(chosen, 1.0, 0.0).astype(jnp.bfloat16),
-            parts,
-            preferred_element_type=jnp.float32,
+            chosen_ref[...], parts, preferred_element_type=jnp.float32
         )
 
         def step(i, carry, cos_ref=cos_ref, sin_ref=sin_ref, sign_ref=sign_ref):
@@ -137,27 +165,28 @@
         lax.fori_loop(0, rows // 32, step, 0)
 
 
-def phases_of(shift, table, count, rows):
+def phases_of(template_id, shift_table, table, count, local, quads):
+    templates, shifts = shift_table.shape
+    rows = templates // 2 * shifts
     held = jax.ShapeDtypeStruct((count, rows, LANES), jnp.float32)
     sign = jax.ShapeDtypeStruct((rows, LANES), jnp.float32)
     out = pl.pallas_call(
-        phase_kernel,
-        in_specs=whole_in_vmem(2),
+        functools.partial(phase_kernel, local, quads),
+        in_specs=whole_in_vmem(3),
         out_specs=tuple(whole_in_vmem(6)),
         out_shape=(held, held, sign) * 2,
-        scratch_shapes=[pltpu.VMEM((rows, table.shape[1]), jnp.float32)],
+        scratch_shapes=[
+            pltpu.VMEM((rows, table.shape[1]), jnp.float32),
+            pltpu.VMEM((rows, 3 * table.shape[0]), jnp.bfloat16),
+        ],
         compiler_params=PARAMS,
         cost_estimate=pl.CostEstimate(
             flops=12 * count * rows * LANES,
             bytes_accessed=16 * count * rows * LANES,
             transcendentals=0,
         ),
-    )(shift, table)
+    )(template_id.reshape(1, templates), shift_table.T, table)
     return out[:3], out[3:]
-
-
-def whole_in_vmem(count):
-    return [pl.BlockSpec(memory_space=pltpu.VMEM)] * count
 
 
 def score_kernel(places, shifts, *refs):
@@ -435,14 +464,6 @@
     x = relay(images)
 
     piece_rows = local * rows
-    position = jnp.arange(2 * held, dtype=jnp.int32)
-    at_local = position % local
-    at_row = (position // local % rows) ^ lax.axis_index("row")
-    at_quad = (position // piece_rows + 1) % quads
-    at_col = (2 * at_quad + position // held) ^ lax.axis_index("col")
-    slots = (at_row * cols + at_col) * local + at_local
-    shift = shift_table[template_id[slots]].reshape(2 * quads, piece_rows, shifts)
-    shift = shift.transpose(0, 2, 1).reshape(-1, 1)
 
     number = jnp.arange(SHIFT_SIDE * SHIFT_SIDE, dtype=jnp.int32)[:, None]
     step_x = number // SHIFT_SIDE - SHIFT_SIDE // 2
@@ -457,7 +478,7 @@
     table = [jnp.cos(angle), jnp.sin(angle)]
     table = [part[:, at : at + LANES] for at in (0, LANES) for part in table]
     table = jnp.concatenate(table, axis=1)
-    tables = phases_of(shift, table, groups // 2, shifts * held)
+    tables = phases_of(template_id, shift_table, table, groups // 2, local, quads)
 
     layout = [
         tuple((0, (d - 1) % quads) for d in range(quads - 1)),

time: 90.2 us -> 83 us (0.920)
  Pallas kernels: 40.7 us -> 35.4 us
  local copies, waits for them, and re-layouts: 5.28 us -> 2.24 us
  waiting for transfers between devices: 20.2 us -> 21.5 us
    pallas_call x3, Pallas kernels: 15 us -> 10.4 us  [scores_of(): pl.pallas_call(functools.partial(score_kernel, places, shifts), in_specs=...]
    gather x2 -> x0, local copies, waits for them, and re-layouts: 1.87 us -> none  [the longest x1 1.23 us: body(): template_id[slots]]
    ppermute x17, waiting for transfers between devices: 20.2 us -> 21.5 us  [exchange(): return lax.ppermute(value, axis, [(i, i ^ bit) for i in range(size)])]
    pallas_call x3, Pallas kernels: 13.9 us -> 12.7 us  [back_of(): pl.pallas_call(functools.partial(back_kernel, first, pieces, shifts), in_...]
  transfers between devices with their start and end apart: 17 -> 17, of which waited for: 7 -> 7; matrix products, arithmetic and copies ran while one was open for 4% -> 1% of each run, Pallas kernels for 27% -> 25%
where the time goes in v5:
time: 83 us; the launch traced here: 82.7 us
  Pallas kernels  35.4 us (43%)
  waiting for transfers between devices  21.5 us (26%)
  starting transfers between devices  18.6 us (22%)
  other arithmetic  4.59 us (6%)
  local copies, waits for them, and re-layouts  2.24 us (3%)
    ppermute x17, waiting for transfers between devices, exchange(): return lax.ppermute(value, axis, [(i, i ^ bit) for i in range(size)])  21.5 us
    ppermute x17, starting transfers between devices, exchange(): return lax.ppermute(value, axis, [(i, i ^ bit) for i in range(size)])  18.6 us
    pallas_call x3, Pallas kernels, back_of(): pl.pallas_call(functools.partial(back_kernel, first, pieces, shifts), in_...  12.7 us
    pallas_call x3, Pallas kernels, scores_of(): pl.pallas_call(functools.partial(score_kernel, places, shifts), in_specs=...  10.4 us
    pallas_call x1, Pallas kernels, relay(): pl.pallas_call(relay_kernel, in_specs=[pl.BlockSpec(memory_space=pltpu.HB...  7.87 us
    pallas_call x1, Pallas kernels, phases_of(): pl.pallas_call(functools.partial(phase_kernel, local, quads), in_specs=wh...  3.2 us
  transfers between devices with their start and end apart: 17, of which 7 were waited for; matrix products, arithmetic and copies ran while one was open for 1% of the time, Pallas kernels for 25%

profile of v5, /device:TPU:0, one launch (start us, length us, event | category | flops | bytes accessed | tf_op | source)
XLA Modules:
  0.0 82.7 jit_solution(2391910131414992368)
XLA Ops:
  0.0 0.9 %reshape.167 = bf16[4,8192]{1,0:T(4,128)(2,1)S(1)} reshape(bf16[4,32,2,128]{3,2,1,0:T(2,128)(2,1)} %bitcast.18) | data formatting | bytes 131072 | tf_op jit(solution)/shard_map/reshape | solution.py:453
  0.9 3.1 %collective-permute-start = (bf16[4,8192]{1,0:T(4,128)(2,1)S(1)}, bf16[4,8192]{1,0:T(4,128)(2,1)S(1)}, u32[]{:S(2)}, u32[]{:S(2)}) collective-permute-start(bf16[4,8192]{1,0:T(4,128)(2,1)S(1)} %reshape.167), channel_id=1, source_target_pairs={{0,8},{8,0},{16,24},{24,16},{1,9},{9,1},{17,25},{25,17},{2,10},{10... | collective-permute-start | bytes 196616 | tf_op jit(solution)/shard_map/ppermute | solution.py:439
  4.0 2.6 %collective-permute-start.1 = (bf16[4,8192]{1,0:T(4,128)(2,1)S(1)}, bf16[4,8192]{1,0:T(4,128)(2,1)S(1)}, u32[]{:S(2)}, u32[]{:S(2)}) collective-permute-start(bf16[4,8192]{1,0:T(4,128)(2,1)S(1)} %reshape.167), channel_id=1, source_target_pairs={{0,16},{8,24},{16,0},{24,8},{1,17},{9,25},{17,1},{25,9},{2,18},{10... | collective-permute-start | bytes 196616 | tf_op jit(solution)/shard_map/ppermute | solution.py:439
  6.8 0.2 fusion.16
  7.0 4.2 %collective-permute-done.1 = bf16[4,8192]{1,0:T(4,128)(2,1)S(1)} collective-permute-done((bf16[4,8192]{1,0:T(4,128)(2,1)S(1)}, bf16[4,8192]{1,0:T(4,128)(2,1)S(1)}, u32[]{:S(2)}, u32[]{:S(2)}) %collective-permute-start.1) | collective-permute-done | bytes 65568 | tf_op jit(solution)/shard_map/ppermute | solution.py:439
  11.2 1.4 %collective-permute-done.2 = bf16[4,8192]{1,0:T(4,128)(2,1)S(1)} collective-permute-done((bf16[4,8192]{1,0:T(4,128)(2,1)S(1)}, bf16[4,8192]{1,0:T(4,128)(2,1)S(1)}, u32[]{:S(2)}, u32[]{:S(2)}) %collective-permute-start.2) | collective-permute-done | bytes 65568 | tf_op jit(solution)/shard_map/ppermute | solution.py:439
  12.6 0.2 pad_maximum_fusion.4.refs_0_
  12.8 2.5 %collective-permute-start.8 = (bf16[16,8192]{1,0:T(8,128)(2,1)S(1)}, bf16[16,8192]{1,0:T(8,128)(2,1)S(1)}, u32[]{:S(2)}, u32[]{:S(2)}) collective-permute-start(bf16[16,8192]{1,0:T(8,128)(2,1)S(1)} %pad_maximum_fusion.4.refs_0_), channel_id=1, source_target_pairs={{0,6},{1,7},{2,4},{3,5},{4,2},{5,3},{6,0},{7,1},{8,14},{9,15},{10,... | collective-permute-start | bytes 786440 | tf_op jit(solution)/shard_map/ppermute | solution.py:439
  15.3 0.5 collective-permute-start.3
  15.9 0.5 collective-permute-start.4
  16.4 7.9 %shard_map.56.refs_9_.refs_8_.refs_7_.x_ref = bf16[528,8192]{1,0:T(8,128)(2,1)S(1)} custom-call(bf16[512,64,128]{2,1,0:T(8,128)(2,1)} %bitcast.17), custom_call_target="tpu_custom_call" | custom-call | flops 4194304 | bytes 16777216 | tf_op jit(solution)/shard_map/pallas_call | solution.py:82
  24.3 3.2 %shard_map.55 = (f32[16,512,128]{2,1,0:T(8,128)S(1)}, f32[16,512,128]{2,1,0:T(8,128)S(1)}, f32[512,128]{1,0:T(8,128)S(1)}, f32[16,512,128]{2,1,0:T(8,128)S(1)}, ...) custom-call(s32[1,128]{1,0:T(1,128)S(1)} %bitcast.16, s32[8,128]{1,0:T(8,128)S(1)} %bitcast.14, ...), custom_call_target="tpu_custom_call" | custom-call | flops 12582912 | bytes 16777216 | tf_op jit(solution)/shard_map/pallas_call | solution.py:173
  27.6 0.5 collective-permute-start.9
  28.2 0.4 collective-permute-start.7
  28.6 3.9 %shard_map.57 = (f32[384,512]{1,0:T(8,128)S(1)}, f32[48,128]{1,0:T(8,128)S(1)}) custom-call(bf16[16,8192]{1,0:T(8,128)(2,1)S(1)} %pad_maximum_fusion.4.refs_0_, bf16[16,8192]{1,0:T(8,128)(2,1)S(1)} %collective-permute-done.3.refs_1_, bf16[16,8192]{1,0:T(8,128)(2,1)S(1)} %collective-permute-done.4.refs_2_, ...), custom_call_target="tpu_custom_call" | custom-call | flops 3221225472 | bytes 9961472 | tf_op jit(solution)/shard_map/pallas_call | solution.py:271
  32.5 2.7 %shard_map.59 = (f32[256,512]{1,0:T(8,128)S(1)}, f32[32,128]{1,0:T(8,128)S(1)}) custom-call(bf16[16,8192]{1,0:T(8,128)(2,1)S(1)} %collective-permute-done.8.refs_0_, bf16[16,8192]{1,0:T(8,128)(2,1)S(1)} %collective-permute-done.9.refs_1_, f32[16,512,128]{2,1,0:T(8,128)S(1)} %get-tuple-element.26.refs_3_.refs_2_.cos_ref, ...), custom_call_target="tpu_custom_call" | custom-call | flops 2147483648 | bytes 9437184 | tf_op jit(solution)/shard_map/pallas_call | solution.py:271
  35.3 3.8 %shard_map.58 = (f32[384,512]{1,0:T(8,128)S(1)}, f32[48,128]{1,0:T(8,128)S(1)}) custom-call(bf16[16,8192]{1,0:T(8,128)(2,1)S(1)} %collective-permute-done.5.refs_0_, bf16[16,8192]{1,0:T(8,128)(2,1)S(1)} %collective-permute-done.6.refs_1_, bf16[16,8192]{1,0:T(8,128)(2,1)S(1)} %collective-permute-done.7.refs_2_, ...), custom_call_target="tpu_custom_call" | custom-call | flops 3221225472 | bytes 9961472 | tf_op jit(solution)/shard_map/pallas_call | solution.py:271
  39.1 1.2 %shard_map.60 = (bf16[512,512]{1,0:T(8,128)(2,1)S(1)}, bf16[512,512]{1,0:T(8,128)(2,1)S(1)}, f32[64,128]{1,0:T(8,128)S(1)}, f32[64,128]{1,0:T(8,128)S(1)}, f32[64,128]{1,0:T(8,128)S(1)}, /*index=5*/f32[64,128]{1,0:T(8,128)S(1)}) custom-call(f32[384,512]{1,0:T(8,128)S(1)} %get-tuple-element.32.refs_0_, f32[384,512]{1,0:T(8,128)S(1)} %get-tuple-element.33.refs_1_, ...), custom_call_target="tpu_custom_call" | custom-call | flops 10485760 | bytes 6291456 | tf_op jit(solution)/shard_map/pallas_call | solution.py:340
  40.3 6.0 %shard_map.62 = f32[64,8192]{1,0:T(8,128)S(1)} custom-call(bf16[512,512]{1,0:T(8,128)(2,1)S(1)} %get-tuple-element.39.w_ref, f32[16,512,128]{2,1,0:T(8,128)S(1)} %get-tuple-element.29.refs_6_.refs_5_.cos_ref, f32[16,512,128]{2,1,0:T(8,128)S(1)} %get-tuple-element.30.refs_7_.refs_6_.sin_ref, f32[512,128]{1,0:T(8,128)S(1)} %get-tuple-element.31.refs_8_.refs_7_.sign_ref, ...), custom_call_target="tpu_custom_call" | custom-call | flops 4294967296 | bytes 9043968 | tf_op jit(solution)/shard_map/pallas_call | solution.py:423
  46.6 0.2 multiply_convert_fusion
  46.9 0.2 pad_maximum_fusion
  47.2 0.1 collective-permute-start.10
  47.3 3.3 %shard_map.61 = f32[32,8192]{1,0:T(8,128)S(1)} custom-call(bf16[512,512]{1,0:T(8,128)(2,1)S(1)} %get-tuple-element.44.w_ref, f32[16,512,128]{2,1,0:T(8,128)S(1)} %get-tuple-element.26.refs_3_.refs_2_.cos_ref, f32[16,512,128]{2,1,0:T(8,128)S(1)} %get-tuple-element.27.refs_4_.refs_3_.sin_ref, f32[512,128]{1,0:T(8,128)S(1)} %get-tuple-element.28.refs_5_.refs_4_.sign_ref, ...), custom_call_target="tpu_custom_call" | custom-call | flops 2147483648 | bytes 8716288 | tf_op jit(solution)/shard_map/pallas_call | solution.py:423
  50.8 0.2 exponential_reduce_fusion
  51.0 0.2 slice_multiply_fusion
  51.3 0.2 exponential_reduce_fusion.6
  51.8 0.2 slice_add_fusion.1
  52.0 0.2 fusion.4
  52.4 3.3 %shard_map.63 = f32[32,8192]{1,0:T(8,128)S(1)} custom-call(bf16[512,512]{1,0:T(8,128)(2,1)S(1)} %get-tuple-element.44.w_ref, f32[16,512,128]{2,1,0:T(8,128)S(1)} %get-tuple-element.26.refs_3_.refs_2_.cos_ref, f32[16,512,128]{2,1,0:T(8,128)S(1)} %get-tuple-element.27.refs_4_.refs_3_.sin_ref, f32[512,128]{1,0:T(8,128)S(1)} %get-tuple-element.28.refs_5_.refs_4_.sign_ref, ...), custom_call_target="tpu_custom_call" | custom-call | flops 2147483648 | bytes 8716288 | tf_op jit(solution)/shard_map/pallas_call | solution.py:423
  55.7 0.2 slice_add_fusion
  56.1 2.5 %collective-permute-start.13 = (f16[16,8320]{1,0:T(8,128)(2,1)S(1)}, f16[16,8320]{1,0:T(8,128)(2,1)S(1)}, u32[]{:S(2)}, u32[]{:S(2)}) collective-permute-start(f16[16,8320]{1,0:T(8,128)(2,1)S(1)} %pad_maximum_fusion.3), channel_id=1, source_target_pairs={{0,6},{1,7},{2,4},{3,5},{4,2},{5,3},{6,0},{7,1},{8,14},{9,15},{10,... | collective-permute-start | bytes 798728 | tf_op jit(solution)/shard_map/ppermute | solution.py:439
  58.6 0.5 collective-permute-start.11
  59.1 0.5 collective-permute-start.12
  59.6 6.7 %collective-permute-done.13 = f16[16,8320]{1,0:T(8,128)(2,1)S(1)} collective-permute-done((f16[16,8320]{1,0:T(8,128)(2,1)S(1)}, f16[16,8320]{1,0:T(8,128)(2,1)S(1)}, u32[]{:S(2)}, u32[]{:S(2)}) %collective-permute-start.13) | collective-permute-done | bytes 266272 | tf_op jit(solution)/shard_map/ppermute | solution.py:439
  66.4 5.2 %collective-permute-done.11 = f16[16,8320]{1,0:T(8,128)(2,1)S(1)} collective-permute-done((f16[16,8320]{1,0:T(8,128)(2,1)S(1)}, f16[16,8320]{1,0:T(8,128)(2,1)S(1)}, u32[]{:S(2)}, u32[]{:S(2)}) %collective-permute-start.11) | collective-permute-done | bytes 266272 | tf_op jit(solution)/shard_map/ppermute | solution.py:439
  71.7 0.2 slice_add_fusion.6
  71.9 0.2 exponential_reduce_fusion.10
  72.1 0.1 slice_reduce_fusion.6
  72.3 0.2 fusion
  72.5 0.2 fusion.13
  72.9 2.4 %collective-permute-start.15 = (f16[4,8320]{1,0:T(4,128)(2,1)S(1)}, f16[4,8320]{1,0:T(4,128)(2,1)S(1)}, u32[]{:S(2)}, u32[]{:S(2)}) collective-permute-start(f16[4,8320]{1,0:T(4,128)(2,1)S(1)} %pad_maximum_fusion.7), channel_id=1, source_target_pairs={{0,16},{8,24},{16,0},{24,8},{1,17},{9,25},{17,1},{25,9},{2,18},{10... | collective-permute-start | bytes 199688 | tf_op jit(solution)/shard_map/ppermute | solution.py:439
  75.4 2.1 %collective-permute-start.16 = (f16[4,8320]{1,0:T(4,128)(2,1)S(1)}, f16[4,8320]{1,0:T(4,128)(2,1)S(1)}, u32[]{:S(2)}, u32[]{:S(2)}) collective-permute-start(f16[4,8320]{1,0:T(4,128)(2,1)S(1)} %pad_maximum_fusion.8), channel_id=1, source_target_pairs={{0,24},{8,16},{16,8},{24,0},{1,25},{9,17},{17,9},{25,1},{2,26},{10... | collective-permute-start | bytes 199688 | tf_op jit(solution)/shard_map/ppermute | solution.py:439
  77.5 0.6 collective-permute-done.14
  78.1 2.6 %collective-permute-done.15 = f16[4,8320]{1,0:T(4,128)(2,1)S(1)} collective-permute-done((f16[4,8320]{1,0:T(4,128)(2,1)S(1)}, f16[4,8320]{1,0:T(4,128)(2,1)S(1)}, u32[]{:S(2)}, u32[]{:S(2)}) %collective-permute-start.15) | collective-permute-done | bytes 66592 | tf_op jit(solution)/shard_map/ppermute | solution.py:439
  80.7 0.8 collective-permute-done.16
  81.5 0.2 fusion.51
  81.8 0.2 fusion.8
  81.9 0.8 reshape.172
  (53 shorter events, 2.1 us)
Async XLA Ops:
  0.9 6.2 %collective-permute-start = (bf16[4,8192]{1,0:T(4,128)(2,1)S(1)}, bf16[4,8192]{1,0:T(4,128)(2,1)S(1)}, u32[]{:S(2)}, u32[]{:S(2)}) collective-permute-start(bf16[4,8192]{1,0:T(4,128)(2,1)S(1)} %reshape.167), channel_id=1, source_target_pairs={{0,8},{8,0},{16,24},{24,16},{1,9},{9,1},{17,25},{25,17},{2,10},{10... | collective-permute-start | bytes 196616 | tf_op jit(solution)/shard_map/ppermute | solution.py:439
  4.0 7.3 %collective-permute-start.1 = (bf16[4,8192]{1,0:T(4,128)(2,1)S(1)}, bf16[4,8192]{1,0:T(4,128)(2,1)S(1)}, u32[]{:S(2)}, u32[]{:S(2)}) collective-permute-start(bf16[4,8192]{1,0:T(4,128)(2,1)S(1)} %reshape.167), channel_id=1, source_target_pairs={{0,16},{8,24},{16,0},{24,8},{1,17},{9,25},{17,1},{25,9},{2,18},{10... | collective-permute-start | bytes 196616 | tf_op jit(solution)/shard_map/ppermute | solution.py:439
  6.6 6.1 %collective-permute-start.2 = (bf16[4,8192]{1,0:T(4,128)(2,1)S(1)}, bf16[4,8192]{1,0:T(4,128)(2,1)S(1)}, u32[]{:S(2)}, u32[]{:S(2)}) collective-permute-start(bf16[4,8192]{1,0:T(4,128)(2,1)S(1)} %reshape.167), channel_id=1, source_target_pairs={{0,24},{8,16},{16,8},{24,0},{1,25},{9,17},{17,9},{25,1},{2,26},{10... | collective-permute-start | bytes 196616 | tf_op jit(solution)/shard_map/ppermute | solution.py:439
  12.8 14.8 %collective-permute-start.8 = (bf16[16,8192]{1,0:T(8,128)(2,1)S(1)}, bf16[16,8192]{1,0:T(8,128)(2,1)S(1)}, u32[]{:S(2)}, u32[]{:S(2)}) collective-permute-start(bf16[16,8192]{1,0:T(8,128)(2,1)S(1)} %pad_maximum_fusion.4.refs_0_), channel_id=1, source_target_pairs={{0,6},{1,7},{2,4},{3,5},{4,2},{5,3},{6,0},{7,1},{8,14},{9,15},{10,... | collective-permute-start | bytes 786440 | tf_op jit(solution)/shard_map/ppermute | solution.py:439
  15.3 12.8 %collective-permute-start.3 = (bf16[16,8192]{1,0:T(8,128)(2,1)S(1)}, bf16[16,8192]{1,0:T(8,128)(2,1)S(1)}, u32[]{:S(2)}, u32[]{:S(2)}) collective-permute-start(bf16[16,8192]{1,0:T(8,128)(2,1)S(1)} %pad_maximum_fusion.4.refs_0_), channel_id=1, source_target_pairs={{0,2},{1,3},{2,0},{3,1},{4,6},{5,7},{6,4},{7,5},{8,10},{9,11},{10,... | collective-permute-start | bytes 786440 | tf_op jit(solution)/shard_map/ppermute | solution.py:439
  15.9 12.3 %collective-permute-start.4 = (bf16[16,8192]{1,0:T(8,128)(2,1)S(1)}, bf16[16,8192]{1,0:T(8,128)(2,1)S(1)}, u32[]{:S(2)}, u32[]{:S(2)}) collective-permute-start(bf16[16,8192]{1,0:T(8,128)(2,1)S(1)} %pad_maximum_fusion.4.refs_0_), channel_id=1, source_target_pairs={{0,4},{1,5},{2,6},{3,7},{4,0},{5,1},{6,2},{7,3},{8,12},{9,13},{10,... | collective-permute-start | bytes 786440 | tf_op jit(solution)/shard_map/ppermute | solution.py:439
  16.4 7.9 %copy-start = (s32[128,8]{0,1:T(8,128)S(1)}, s32[128,8]{0,1:T(8,128)}, u32[]{:S(2)}) copy-start(s32[128,8]{0,1:T(8,128)} %param.9) | copy-start | bytes 12292
  16.4 7.9 %copy-start.2 = (s32[128]{0:T(128)S(1)}, s32[128]{0:T(128)}, u32[]{:S(2)}) copy-start(s32[128]{0:T(128)} %param.8) | copy-start | bytes 1540
  27.5 7.7 %collective-permute-start.5 = (bf16[16,8192]{1,0:T(8,128)(2,1)S(1)}, bf16[16,8192]{1,0:T(8,128)(2,1)S(1)}, u32[]{:S(2)}, u32[]{:S(2)}) collective-permute-start(bf16[16,8192]{1,0:T(8,128)(2,1)S(1)} %pad_maximum_fusion.4.refs_0_), channel_id=1, source_target_pairs={{0,1},{1,0},{2,3},{3,2},{4,5},{5,4},{6,7},{7,6},{8,9},{9,8},{10,11... | collective-permute-start | bytes 786440 | tf_op jit(solution)/shard_map/ppermute | solution.py:439
  27.6 4.9 %collective-permute-start.9 = (bf16[16,8192]{1,0:T(8,128)(2,1)S(1)}, bf16[16,8192]{1,0:T(8,128)(2,1)S(1)}, u32[]{:S(2)}, u32[]{:S(2)}) collective-permute-start(bf16[16,8192]{1,0:T(8,128)(2,1)S(1)} %collective-permute-done.8.refs_0_), channel_id=1, source_target_pairs={{0,1},{1,0},{2,3},{3,2},{4,5},{5,4},{6,7},{7,6},{8,9},{9,8},{10,11... | collective-permute-start | bytes 786440 | tf_op jit(solution)/shard_map/ppermute | solution.py:439
  28.1 7.2 %collective-permute-start.6 = (bf16[16,8192]{1,0:T(8,128)(2,1)S(1)}, bf16[16,8192]{1,0:T(8,128)(2,1)S(1)}, u32[]{:S(2)}, u32[]{:S(2)}) collective-permute-start(bf16[16,8192]{1,0:T(8,128)(2,1)S(1)} %collective-permute-done.3.refs_1_), channel_id=1, source_target_pairs={{0,1},{1,0},{2,3},{3,2},{4,5},{5,4},{6,7},{7,6},{8,9},{9,8},{10,11... | collective-permute-start | bytes 786440 | tf_op jit(solution)/shard_map/ppermute | solution.py:439
  28.2 7.1 %collective-permute-start.7 = (bf16[16,8192]{1,0:T(8,128)(2,1)S(1)}, bf16[16,8192]{1,0:T(8,128)(2,1)S(1)}, u32[]{:S(2)}, u32[]{:S(2)}) collective-permute-start(bf16[16,8192]{1,0:T(8,128)(2,1)S(1)} %collective-permute-done.4.refs_2_), channel_id=1, source_target_pairs={{0,1},{1,0},{2,3},{3,2},{4,5},{5,4},{6,7},{7,6},{8,9},{9,8},{10,11... | collective-permute-start | bytes 786440 | tf_op jit(solution)/shard_map/ppermute | solution.py:439
  35.2 3.9 %copy-start.1 = (f32[512]{0:T(512)S(1)}, f32[512]{0:T(512)}, u32[]{:S(2)}) copy-start(f32[512]{0:T(512)} %param.6) | copy-start | bytes 6148
  47.2 3.5 %collective-permute-start.10 = (f16[64,8320]{1,0:T(8,128)(2,1)S(1)}, f16[64,8320]{1,0:T(8,128)(2,1)S(1)}, u32[]{:S(2)}, u32[]{:S(2)}) collective-permute-start(f16[64,8320]{1,0:T(8,128)(2,1)S(1)} %pad_maximum_fusion), channel_id=1, source_target_pairs={{0,1},{1,0},{2,3},{3,2},{4,5},{5,4},{6,7},{7,6},{8,9},{9,8},{10,11... | collective-permute-start | bytes 3194888 | tf_op jit(solution)/shard_map/ppermute | solution.py:439
  56.1 10.3 %collective-permute-start.13 = (f16[16,8320]{1,0:T(8,128)(2,1)S(1)}, f16[16,8320]{1,0:T(8,128)(2,1)S(1)}, u32[]{:S(2)}, u32[]{:S(2)}) collective-permute-start(f16[16,8320]{1,0:T(8,128)(2,1)S(1)} %pad_maximum_fusion.3), channel_id=1, source_target_pairs={{0,6},{1,7},{2,4},{3,5},{4,2},{5,3},{6,0},{7,1},{8,14},{9,15},{10,... | collective-permute-start | bytes 798728 | tf_op jit(solution)/shard_map/ppermute | solution.py:439
  58.6 13.0 %collective-permute-start.11 = (f16[16,8320]{1,0:T(8,128)(2,1)S(1)}, f16[16,8320]{1,0:T(8,128)(2,1)S(1)}, u32[]{:S(2)}, u32[]{:S(2)}) collective-permute-start(f16[16,8320]{1,0:T(8,128)(2,1)S(1)} %pad_maximum_fusion.1), channel_id=1, source_target_pairs={{0,2},{1,3},{2,0},{3,1},{4,6},{5,7},{6,4},{7,5},{8,10},{9,11},{10,... | collective-permute-start | bytes 798728 | tf_op jit(solution)/shard_map/ppermute | solution.py:439
  59.1 12.5 %collective-permute-start.12 = (f16[16,8320]{1,0:T(8,128)(2,1)S(1)}, f16[16,8320]{1,0:T(8,128)(2,1)S(1)}, u32[]{:S(2)}, u32[]{:S(2)}) collective-permute-start(f16[16,8320]{1,0:T(8,128)(2,1)S(1)} %pad_maximum_fusion.2), channel_id=1, source_target_pairs={{0,4},{1,5},{2,6},{3,7},{4,0},{5,1},{6,2},{7,3},{8,12},{9,13},{10,... | collective-permute-start | bytes 798728 | tf_op jit(solution)/shard_map/ppermute | solution.py:439
  72.8 5.3 %collective-permute-start.14 = (f16[4,8320]{1,0:T(4,128)(2,1)S(1)}, f16[4,8320]{1,0:T(4,128)(2,1)S(1)}, u32[]{:S(2)}, u32[]{:S(2)}) collective-permute-start(f16[4,8320]{1,0:T(4,128)(2,1)S(1)} %pad_maximum_fusion.6), channel_id=1, source_target_pairs={{0,8},{8,0},{16,24},{24,16},{1,9},{9,1},{17,25},{25,17},{2,10},{10... | collective-permute-start | bytes 199688 | tf_op jit(solution)/shard_map/ppermute | solution.py:439
  72.9 7.8 %collective-permute-start.15 = (f16[4,8320]{1,0:T(4,128)(2,1)S(1)}, f16[4,8320]{1,0:T(4,128)(2,1)S(1)}, u32[]{:S(2)}, u32[]{:S(2)}) collective-permute-start(f16[4,8320]{1,0:T(4,128)(2,1)S(1)} %pad_maximum_fusion.7), channel_id=1, source_target_pairs={{0,16},{8,24},{16,0},{24,8},{1,17},{9,25},{17,1},{25,9},{2,18},{10... | collective-permute-start | bytes 199688 | tf_op jit(solution)/shard_map/ppermute | solution.py:439
  75.4 6.1 %collective-permute-start.16 = (f16[4,8320]{1,0:T(4,128)(2,1)S(1)}, f16[4,8320]{1,0:T(4,128)(2,1)S(1)}, u32[]{:S(2)}, u32[]{:S(2)}) collective-permute-start(f16[4,8320]{1,0:T(4,128)(2,1)S(1)} %pad_maximum_fusion.8), channel_id=1, source_target_pairs={{0,24},{8,16},{16,8},{24,0},{1,25},{9,17},{17,9},{25,1},{2,26},{10... | collective-permute-start | bytes 199688 | tf_op jit(solution)/shard_map/ppermute | solution.py:439

commit v6 on v5

--- a/solution.py
+++ b/solution.py
@@ -17,7 +17,7 @@
 UNROLL = 8
 WIRE = jnp.float16
 VMEM_LIMIT = 8 << 20
-RELAY_LIMIT = 12 << 20
+RELAY_LIMIT = 14 << 20
 
 PARAMS = pltpu.CompilerParams(vmem_limit_bytes=VMEM_LIMIT)
 
@@ -27,38 +27,35 @@
 
 
 def relay_kernel(in_ref, out_ref, taken_ref, wide_ref, peak_ref, sems):
-    count, per, _ = in_ref.shape
-    some = taken_ref.shape[1]
+    blocks, some, per, _ = taken_ref.shape
     rows = peak_ref.shape[0]
-    blocks = count // some
+    count = blocks * some
     last = out_ref.shape[0]
-
-    def fetch(block, slot):
+    pitch = rows + 1
+
+    def fetch(block):
         return pltpu.make_async_copy(
-            in_ref.at[pl.ds(block * some, some)], taken_ref.at[slot], sems.at[slot]
+            in_ref.at[pl.ds(block * some, some)], taken_ref.at[block], sems.at[block]
         )
 
-    fetch(0, 0).start()
+    for block in range(blocks):
+        fetch(block).start()
     peak_ref[...] = jnp.zeros_like(peak_ref)
 
     def step(block, carry):
-        slot = lax.rem(block, 2)
-
-        @pl.when(block + 1 < blocks)
-        def _():
-            fetch(block + 1, 1 - slot).start()
-
-        fetch(block, slot).wait()
+        fetch(block).wait()
         base = pl.multiple_of(block * some, some)
         peak = peak_ref[...]
         for n in range(0, some, 16):
             for r in range(0, per, rows):
-                wide = taken_ref[slot, n : n + 16, r : r + rows, :].astype(jnp.float32)
-                start = (n * per) + 16 * r
-                wide_ref[start : start + 16 * rows, :] = wide.reshape(16 * rows, LANES)
-                peak = jnp.maximum(peak, jnp.max(jnp.abs(wide), axis=0))
+                start = (n // 16 * (per // rows) + r // rows) * 16 * pitch
+                for m in range(16):
+                    wide = taken_ref[block, n + m, r : r + rows, :].astype(jnp.float32)
+                    peak = jnp.maximum(peak, jnp.abs(wide))
+                    at = start + m * pitch
+                    wide_ref[at : at + rows, :] = wide
                 for k in range(rows):
-                    picked = wide_ref[pl.ds(start + k, 16, stride=rows), :]
+                    picked = wide_ref[pl.ds(start + k, 16, stride=pitch), :]
                     at = (r + k) * LANES
                     out_ref[pl.ds(base + n, 16), at : at + LANES] = picked.astype(jnp.bfloat16)
         peak_ref[...] = peak
@@ -71,24 +68,28 @@
     )
 
 
+def flat_rows(value, lead):
+    count, parts, coeffs = value.shape
+    groups = coeffs // LANES
+    value = value.reshape(count, parts, groups, LANES)
+    return value.transpose(0, 2, 1, 3).reshape(lead + (LANES,))
+
+
 def relay(images, rows=8, spare=16):
     count, parts, coeffs = images.shape
-    groups = coeffs // LANES
-    per = parts * groups
+    per = parts * (coeffs // LANES)
     some = min(count, 64)
-    flat = images.reshape(count, parts, groups, LANES)
-    flat = flat.transpose(0, 2, 1, 3).reshape(count, per, LANES)
-    flat = pltpu.with_memory_space_constraint(flat, pltpu.HBM)
+    flat = pltpu.with_memory_space_constraint(flat_rows(images, (count, per)), pltpu.HBM)
     return pl.pallas_call(
         relay_kernel,
         in_specs=[pl.BlockSpec(memory_space=pltpu.HBM)],
         out_specs=pl.BlockSpec(memory_space=pltpu.VMEM),
         out_shape=jax.ShapeDtypeStruct((count + spare, per * LANES), jnp.bfloat16),
         scratch_shapes=[
-            pltpu.VMEM((2, some, per, LANES), jnp.bfloat16),
-            pltpu.VMEM((some * per, LANES), jnp.float32),
+            pltpu.VMEM((count // some, some, per, LANES), jnp.bfloat16),
+            pltpu.VMEM((some * per // rows * (rows + 1), LANES), jnp.float32),
             pltpu.VMEM((rows, LANES), jnp.float32),
-            pltpu.SemaphoreType.DMA((2,)),
+            pltpu.SemaphoreType.DMA((count // some,)),
         ],
         compiler_params=pltpu.CompilerParams(vmem_limit_bytes=RELAY_LIMIT),
         cost_estimate=pl.CostEstimate(
@@ -97,6 +98,50 @@
             transcendentals=0,
         ),
     )(flat)
+
+
+def lay_kernel(in_ref, out_ref, wide_ref):
+    local, width = out_ref.shape
+    per = width // LANES
+    wide_ref[...] = in_ref[...].astype(jnp.float32)
+    for r in range(per):
+        picked = wide_ref[pl.ds(r, local, stride=per), :]
+        out_ref[:, r * LANES : (r + 1) * LANES] = picked.astype(out_ref.dtype)
+
+
+def unlay_kernel(in_ref, out_ref):
+    local, width = in_ref.shape
+    per = width // LANES
+    for r in range(per):
+        out_ref[pl.ds(r, local, stride=per), :] = in_ref[:, r * LANES : (r + 1) * LANES]
+
+
+def lay(templates):
+    local, parts, coeffs = templates.shape
+    width = parts * coeffs
+    rows = local * width // LANES
+    return pl.pallas_call(
+        lay_kernel,
+        in_specs=whole_in_vmem(1),
+        out_specs=whole_in_vmem(1)[0],
+        out_shape=jax.ShapeDtypeStruct((local, width), templates.dtype),
+        scratch_shapes=[pltpu.VMEM((rows, LANES), jnp.float32)],
+        compiler_params=PARAMS,
+    )(flat_rows(templates, (rows,)))
+
+
+def unlay(value, parts):
+    local, width = value.shape
+    groups = width // parts // LANES
+    flat = pl.pallas_call(
+        unlay_kernel,
+        in_specs=whole_in_vmem(1),
+        out_specs=whole_in_vmem(1)[0],
+        out_shape=jax.ShapeDtypeStruct((local * width // LANES, LANES), value.dtype),
+        compiler_params=PARAMS,
+    )(value)
+    flat = flat.reshape(local, groups, parts, LANES).transpose(0, 2, 1, 3)
+    return flat.reshape(local, parts, width // parts)
 
 
 def phase_kernel(local, quads, id_ref, shifts_ref, table_ref, *refs):
@@ -449,9 +494,7 @@
     width = parts * coeffs
     held = local * rows * quads
 
-    mine = templates.reshape(local, parts, groups, LANES)
-    mine = mine.transpose(0, 2, 1, 3).reshape(local, width)
-
+    mine = lay(templates)
     row_set = [mine]
     row_set += [exchange(mine, "row", rows, d) for d in range(1, rows)]
     own_set = [jnp.concatenate(row_set, axis=0)]
@@ -535,12 +578,13 @@
             d = number * per_set + place + 1
             received.append(unpack(exchange(piece, "col", cols, 2 * d)))
     whole = add(sums[0], *received)
-    got = [send(cut(whole, d, local), "row", rows, d) for d in range(1, rows)]
+    got = []
+    for d in range(1, rows):
+        got.append(send(cut(whole, d, local), "row", rows, d))
     summed, totals, _ = add(cut(whole, 0, local), *got)
     prior = mine.astype(jnp.float32)
     out = (summed + PRIOR_WEIGHT * prior) / (totals + PRIOR_WEIGHT)
-    out = out.reshape(local, groups, parts, LANES).transpose(0, 2, 1, 3)
-    return out.reshape(local, parts, coeffs)
+    return unlay(out, parts)
 
 
 def solution(mesh):

time: 83 us -> 81.4 us (0.981)
    reshape x2 -> x0, local copies, waits for them, and re-layouts: 1.65 us -> none  [the longest x1 0.86 us: body(): mine = mine.transpose(0, 2, 1, 3).reshape(local, width)]
    pallas_call x1, Pallas kernels: 7.87 us -> 6.43 us  [relay(): pl.pallas_call(relay_kernel, in_specs=[pl.BlockSpec(memory_space=pltpu.HB...]
    unnamed x6 -> x8, local copies, waits for them, and re-layouts: 0.01 us -> 0.85 us
    pallas_call x0 -> x2, Pallas kernels: none -> 0.83 us  [the longest x1 0.74 us: unlay(): pl.pallas_call(unlay_kernel, in_specs=whole_in_vmem(1), out_specs=whole_i...]
  transfers between devices with their start and end apart: 17 -> 17, of which waited for: 7 -> 7; matrix products, arithmetic and copies ran while one was open for 1% -> 1% of each run, Pallas kernels for 25% -> 24%
where the time goes in v6:
time: 81.4 us; the launch traced here: 81.3 us
  Pallas kernels  34.8 us (43%)
  waiting for transfers between devices  21.5 us (26%)
  starting transfers between devices  18.6 us (23%)
  other arithmetic  4.57 us (6%)
  local copies, waits for them, and re-layouts  1.42 us (2%)
    ppermute x17, waiting for transfers between devices, exchange(): return lax.ppermute(value, axis, [(i, i ^ bit) for i in range(size)])  21.5 us
    ppermute x17, starting transfers between devices, exchange(): return lax.ppermute(value, axis, [(i, i ^ bit) for i in range(size)])  18.6 us
    pallas_call x3, Pallas kernels, back_of(): pl.pallas_call(functools.partial(back_kernel, first, pieces, shifts), in_...  12.7 us
    pallas_call x3, Pallas kernels, scores_of(): pl.pallas_call(functools.partial(score_kernel, places, shifts), in_specs=...  10.4 us
    pallas_call x1, Pallas kernels, relay(): pl.pallas_call(relay_kernel, in_specs=[pl.BlockSpec(memory_space=pltpu.HB...  6.43 us
    pallas_call x1, Pallas kernels, phases_of(): pl.pallas_call(functools.partial(phase_kernel, local, quads), in_specs=wh...  3.2 us
  transfers between devices with their start and end apart: 17, of which 7 were waited for; matrix products, arithmetic and copies ran while one was open for 1% of the time, Pallas kernels for 24%

profile of v6, /device:TPU:0, one launch (start us, length us, event | category | flops | bytes accessed | tf_op | source)
XLA Modules:
  0.0 81.3 jit_solution(13781529443352314258)
XLA Ops:
  0.0 0.8 %copy-done = bf16[4,2,4096]{2,1,0:T(2,128)(2,1)S(1)} copy-done((bf16[4,2,4096]{2,1,0:T(2,128)(2,1)S(1)}, bf16[4,2,4096]{2,1,0:T(2,128)(2,1)}, u32[]{:S(2)}) %copy-start) | copy-done | bytes 65560
  0.9 3.1 %collective-permute-start = (bf16[4,8192]{1,0:T(4,128)(2,1)S(1)}, bf16[4,8192]{1,0:T(4,128)(2,1)S(1)}, u32[]{:S(2)}, u32[]{:S(2)}) collective-permute-start(bf16[4,8192]{1,0:T(4,128)(2,1)S(1)} %shard_map.55), channel_id=1, source_target_pairs={{0,8},{8,0},{16,24},{24,16},{1,9},{9,1},{17,25},{25,17},{2,10},{10... | collective-permute-start | bytes 196616 | tf_op jit(solution)/shard_map/ppermute | solution.py:484
  4.1 2.6 %collective-permute-start.1 = (bf16[4,8192]{1,0:T(4,128)(2,1)S(1)}, bf16[4,8192]{1,0:T(4,128)(2,1)S(1)}, u32[]{:S(2)}, u32[]{:S(2)}) collective-permute-start(bf16[4,8192]{1,0:T(4,128)(2,1)S(1)} %shard_map.55), channel_id=1, source_target_pairs={{0,16},{8,24},{16,0},{24,8},{1,17},{9,25},{17,1},{25,9},{2,18},{10... | collective-permute-start | bytes 196616 | tf_op jit(solution)/shard_map/ppermute | solution.py:484
  6.8 0.2 fusion.16
  7.1 4.2 %collective-permute-done.1 = bf16[4,8192]{1,0:T(4,128)(2,1)S(1)} collective-permute-done((bf16[4,8192]{1,0:T(4,128)(2,1)S(1)}, bf16[4,8192]{1,0:T(4,128)(2,1)S(1)}, u32[]{:S(2)}, u32[]{:S(2)}) %collective-permute-start.1) | collective-permute-done | bytes 65568 | tf_op jit(solution)/shard_map/ppermute | solution.py:484
  11.3 1.4 %collective-permute-done.2 = bf16[4,8192]{1,0:T(4,128)(2,1)S(1)} collective-permute-done((bf16[4,8192]{1,0:T(4,128)(2,1)S(1)}, bf16[4,8192]{1,0:T(4,128)(2,1)S(1)}, u32[]{:S(2)}, u32[]{:S(2)}) %collective-permute-start.2) | collective-permute-done | bytes 65568 | tf_op jit(solution)/shard_map/ppermute | solution.py:484
  12.7 0.2 pad_maximum_fusion.4.refs_0_
  12.9 2.5 %collective-permute-start.8 = (bf16[16,8192]{1,0:T(8,128)(2,1)S(1)}, bf16[16,8192]{1,0:T(8,128)(2,1)S(1)}, u32[]{:S(2)}, u32[]{:S(2)}) collective-permute-start(bf16[16,8192]{1,0:T(8,128)(2,1)S(1)} %pad_maximum_fusion.4.refs_0_), channel_id=1, source_target_pairs={{0,6},{1,7},{2,4},{3,5},{4,2},{5,3},{6,0},{7,1},{8,14},{9,15},{10,... | collective-permute-start | bytes 786440 | tf_op jit(solution)/shard_map/ppermute | solution.py:484
  15.4 0.5 collective-permute-start.3
  15.9 0.5 collective-permute-start.4
  16.5 6.4 %shard_map.57.refs_9_.refs_8_.refs_7_.x_ref = bf16[528,8192]{1,0:T(8,128)(2,1)S(1)} custom-call(bf16[512,64,128]{2,1,0:T(8,128)(2,1)} %bitcast.22), custom_call_target="tpu_custom_call" | custom-call | flops 4194304 | bytes 16777216 | tf_op jit(solution)/shard_map/pallas_call | solution.py:83
  22.9 3.2 %shard_map.56 = (f32[16,512,128]{2,1,0:T(8,128)S(1)}, f32[16,512,128]{2,1,0:T(8,128)S(1)}, f32[512,128]{1,0:T(8,128)S(1)}, f32[16,512,128]{2,1,0:T(8,128)S(1)}, ...) custom-call(s32[1,128]{1,0:T(1,128)S(1)} %bitcast.21, s32[8,128]{1,0:T(8,128)S(1)} %bitcast.19, ...), custom_call_target="tpu_custom_call" | custom-call | flops 12582912 | bytes 16777216 | tf_op jit(solution)/shard_map/pallas_call | solution.py:218
  26.2 0.5 collective-permute-start.9
  26.8 0.4 collective-permute-start.7
  27.3 3.9 %shard_map.58 = (f32[384,512]{1,0:T(8,128)S(1)}, f32[48,128]{1,0:T(8,128)S(1)}) custom-call(bf16[16,8192]{1,0:T(8,128)(2,1)S(1)} %pad_maximum_fusion.4.refs_0_, bf16[16,8192]{1,0:T(8,128)(2,1)S(1)} %collective-permute-done.3.refs_1_, bf16[16,8192]{1,0:T(8,128)(2,1)S(1)} %collective-permute-done.4.refs_2_, ...), custom_call_target="tpu_custom_call" | custom-call | flops 3221225472 | bytes 9961472 | tf_op jit(solution)/shard_map/pallas_call | solution.py:316
  31.2 2.7 %shard_map.60 = (f32[256,512]{1,0:T(8,128)S(1)}, f32[32,128]{1,0:T(8,128)S(1)}) custom-call(bf16[16,8192]{1,0:T(8,128)(2,1)S(1)} %collective-permute-done.8.refs_0_, bf16[16,8192]{1,0:T(8,128)(2,1)S(1)} %collective-permute-done.9.refs_1_, f32[16,512,128]{2,1,0:T(8,128)S(1)} %get-tuple-element.26.refs_3_.refs_2_.cos_ref, ...), custom_call_target="tpu_custom_call" | custom-call | flops 2147483648 | bytes 9437184 | tf_op jit(solution)/shard_map/pallas_call | solution.py:316
  33.9 3.8 %shard_map.59 = (f32[384,512]{1,0:T(8,128)S(1)}, f32[48,128]{1,0:T(8,128)S(1)}) custom-call(bf16[16,8192]{1,0:T(8,128)(2,1)S(1)} %collective-permute-done.5.refs_0_, bf16[16,8192]{1,0:T(8,128)(2,1)S(1)} %collective-permute-done.6.refs_1_, bf16[16,8192]{1,0:T(8,128)(2,1)S(1)} %collective-permute-done.7.refs_2_, ...), custom_call_target="tpu_custom_call" | custom-call | flops 3221225472 | bytes 9961472 | tf_op jit(solution)/shard_map/pallas_call | solution.py:316
  37.8 1.2 %shard_map.61 = (bf16[512,512]{1,0:T(8,128)(2,1)S(1)}, bf16[512,512]{1,0:T(8,128)(2,1)S(1)}, f32[64,128]{1,0:T(8,128)S(1)}, f32[64,128]{1,0:T(8,128)S(1)}, f32[64,128]{1,0:T(8,128)S(1)}, /*index=5*/f32[64,128]{1,0:T(8,128)S(1)}) custom-call(f32[384,512]{1,0:T(8,128)S(1)} %get-tuple-element.32.refs_0_, f32[384,512]{1,0:T(8,128)S(1)} %get-tuple-element.33.refs_1_, ...), custom_call_target="tpu_custom_call" | custom-call | flops 10485760 | bytes 6291456 | tf_op jit(solution)/shard_map/pallas_call | solution.py:385
  39.0 6.0 %shard_map.63 = f32[64,8192]{1,0:T(8,128)S(1)} custom-call(bf16[512,512]{1,0:T(8,128)(2,1)S(1)} %get-tuple-element.39.w_ref, f32[16,512,128]{2,1,0:T(8,128)S(1)} %get-tuple-element.29.refs_6_.refs_5_.cos_ref, f32[16,512,128]{2,1,0:T(8,128)S(1)} %get-tuple-element.30.refs_7_.refs_6_.sin_ref, f32[512,128]{1,0:T(8,128)S(1)} %get-tuple-element.31.refs_8_.refs_7_.sign_ref, ...), custom_call_target="tpu_custom_call" | custom-call | flops 4294967296 | bytes 9043968 | tf_op jit(solution)/shard_map/pallas_call | solution.py:468
  45.2 0.2 multiply_convert_fusion
  45.6 0.2 pad_maximum_fusion
  45.8 0.1 collective-permute-start.10
  46.0 3.3 %shard_map.62 = f32[32,8192]{1,0:T(8,128)S(1)} custom-call(bf16[512,512]{1,0:T(8,128)(2,1)S(1)} %get-tuple-element.44.w_ref, f32[16,512,128]{2,1,0:T(8,128)S(1)} %get-tuple-element.26.refs_3_.refs_2_.cos_ref, f32[16,512,128]{2,1,0:T(8,128)S(1)} %get-tuple-element.27.refs_4_.refs_3_.sin_ref, f32[512,128]{1,0:T(8,128)S(1)} %get-tuple-element.28.refs_5_.refs_4_.sign_ref, ...), custom_call_target="tpu_custom_call" | custom-call | flops 2147483648 | bytes 8716288 | tf_op jit(solution)/shard_map/pallas_call | solution.py:468
  49.5 0.2 exponential_reduce_fusion
  49.7 0.2 slice_multiply_fusion
  49.9 0.2 exponential_reduce_fusion.6
  50.4 0.2 slice_add_fusion.1
  50.6 0.2 fusion.4
  51.0 3.3 %shard_map.64 = f32[32,8192]{1,0:T(8,128)S(1)} custom-call(bf16[512,512]{1,0:T(8,128)(2,1)S(1)} %get-tuple-element.44.w_ref, f32[16,512,128]{2,1,0:T(8,128)S(1)} %get-tuple-element.26.refs_3_.refs_2_.cos_ref, f32[16,512,128]{2,1,0:T(8,128)S(1)} %get-tuple-element.27.refs_4_.refs_3_.sin_ref, f32[512,128]{1,0:T(8,128)S(1)} %get-tuple-element.28.refs_5_.refs_4_.sign_ref, ...), custom_call_target="tpu_custom_call" | custom-call | flops 2147483648 | bytes 8716288 | tf_op jit(solution)/shard_map/pallas_call | solution.py:468
  54.4 0.2 slice_add_fusion
  54.7 2.5 %collective-permute-start.13 = (f16[16,8320]{1,0:T(8,128)(2,1)S(1)}, f16[16,8320]{1,0:T(8,128)(2,1)S(1)}, u32[]{:S(2)}, u32[]{:S(2)}) collective-permute-start(f16[16,8320]{1,0:T(8,128)(2,1)S(1)} %pad_maximum_fusion.3), channel_id=1, source_target_pairs={{0,6},{1,7},{2,4},{3,5},{4,2},{5,3},{6,0},{7,1},{8,14},{9,15},{10,... | collective-permute-start | bytes 798728 | tf_op jit(solution)/shard_map/ppermute | solution.py:484
  57.2 0.5 collective-permute-start.11
  57.8 0.5 collective-permute-start.12
  58.3 6.7 %collective-permute-done.13 = f16[16,8320]{1,0:T(8,128)(2,1)S(1)} collective-permute-done((f16[16,8320]{1,0:T(8,128)(2,1)S(1)}, f16[16,8320]{1,0:T(8,128)(2,1)S(1)}, u32[]{:S(2)}, u32[]{:S(2)}) %collective-permute-start.13) | collective-permute-done | bytes 266272 | tf_op jit(solution)/shard_map/ppermute | solution.py:484
  65.0 5.2 %collective-permute-done.11 = f16[16,8320]{1,0:T(8,128)(2,1)S(1)} collective-permute-done((f16[16,8320]{1,0:T(8,128)(2,1)S(1)}, f16[16,8320]{1,0:T(8,128)(2,1)S(1)}, u32[]{:S(2)}, u32[]{:S(2)}) %collective-permute-start.11) | collective-permute-done | bytes 266272 | tf_op jit(solution)/shard_map/ppermute | solution.py:484
  70.3 0.2 slice_add_fusion.6
  70.5 0.2 exponential_reduce_fusion.10
  70.8 0.1 slice_reduce_fusion.6
  70.9 0.2 fusion
  71.1 0.2 fusion.13
  71.6 2.4 %collective-permute-start.15 = (f16[4,8320]{1,0:T(4,128)(2,1)S(1)}, f16[4,8320]{1,0:T(4,128)(2,1)S(1)}, u32[]{:S(2)}, u32[]{:S(2)}) collective-permute-start(f16[4,8320]{1,0:T(4,128)(2,1)S(1)} %pad_maximum_fusion.7), channel_id=1, source_target_pairs={{0,16},{8,24},{16,0},{24,8},{1,17},{9,25},{17,1},{25,9},{2,18},{10... | collective-permute-start | bytes 199688 | tf_op jit(solution)/shard_map/ppermute | solution.py:484
  74.0 2.1 %collective-permute-start.16 = (f16[4,8320]{1,0:T(4,128)(2,1)S(1)}, f16[4,8320]{1,0:T(4,128)(2,1)S(1)}, u32[]{:S(2)}, u32[]{:S(2)}) collective-permute-start(f16[4,8320]{1,0:T(4,128)(2,1)S(1)} %pad_maximum_fusion.8), channel_id=1, source_target_pairs={{0,24},{8,16},{16,8},{24,0},{1,25},{9,17},{17,9},{25,1},{2,26},{10... | collective-permute-start | bytes 199688 | tf_op jit(solution)/shard_map/ppermute | solution.py:484
  76.1 0.6 collective-permute-done.14
  76.7 2.6 %collective-permute-done.15 = f16[4,8320]{1,0:T(4,128)(2,1)S(1)} collective-permute-done((f16[4,8320]{1,0:T(4,128)(2,1)S(1)}, f16[4,8320]{1,0:T(4,128)(2,1)S(1)}, u32[]{:S(2)}, u32[]{:S(2)}) %collective-permute-start.15) | collective-permute-done | bytes 66592 | tf_op jit(solution)/shard_map/ppermute | solution.py:484
  79.4 0.8 collective-permute-done.16
  80.2 0.2 fusion.51
  80.4 0.2 fusion.8.in_ref
  80.5 0.7 shard_map.65
  (55 shorter events, 2.2 us)
Async XLA Ops:
  0.0 0.8 %copy-start = (bf16[4,2,4096]{2,1,0:T(2,128)(2,1)S(1)}, bf16[4,2,4096]{2,1,0:T(2,128)(2,1)}, u32[]{:S(2)}) copy-start(bf16[4,2,4096]{2,1,0:T(2,128)(2,1)} %param.7) | copy-start | bytes 196612
  0.9 6.2 %collective-permute-start = (bf16[4,8192]{1,0:T(4,128)(2,1)S(1)}, bf16[4,8192]{1,0:T(4,128)(2,1)S(1)}, u32[]{:S(2)}, u32[]{:S(2)}) collective-permute-start(bf16[4,8192]{1,0:T(4,128)(2,1)S(1)} %shard_map.55), channel_id=1, source_target_pairs={{0,8},{8,0},{16,24},{24,16},{1,9},{9,1},{17,25},{25,17},{2,10},{10... | collective-permute-start | bytes 196616 | tf_op jit(solution)/shard_map/ppermute | solution.py:484
  4.1 7.3 %collective-permute-start.1 = (bf16[4,8192]{1,0:T(4,128)(2,1)S(1)}, bf16[4,8192]{1,0:T(4,128)(2,1)S(1)}, u32[]{:S(2)}, u32[]{:S(2)}) collective-permute-start(bf16[4,8192]{1,0:T(4,128)(2,1)S(1)} %shard_map.55), channel_id=1, source_target_pairs={{0,16},{8,24},{16,0},{24,8},{1,17},{9,25},{17,1},{25,9},{2,18},{10... | collective-permute-start | bytes 196616 | tf_op jit(solution)/shard_map/ppermute | solution.py:484
  6.6 6.1 %collective-permute-start.2 = (bf16[4,8192]{1,0:T(4,128)(2,1)S(1)}, bf16[4,8192]{1,0:T(4,128)(2,1)S(1)}, u32[]{:S(2)}, u32[]{:S(2)}) collective-permute-start(bf16[4,8192]{1,0:T(4,128)(2,1)S(1)} %shard_map.55), channel_id=1, source_target_pairs={{0,24},{8,16},{16,8},{24,0},{1,25},{9,17},{17,9},{25,1},{2,26},{10... | collective-permute-start | bytes 196616 | tf_op jit(solution)/shard_map/ppermute | solution.py:484
  12.9 13.4 %collective-permute-start.8 = (bf16[16,8192]{1,0:T(8,128)(2,1)S(1)}, bf16[16,8192]{1,0:T(8,128)(2,1)S(1)}, u32[]{:S(2)}, u32[]{:S(2)}) collective-permute-start(bf16[16,8192]{1,0:T(8,128)(2,1)S(1)} %pad_maximum_fusion.4.refs_0_), channel_id=1, source_target_pairs={{0,6},{1,7},{2,4},{3,5},{4,2},{5,3},{6,0},{7,1},{8,14},{9,15},{10,... | collective-permute-start | bytes 786440 | tf_op jit(solution)/shard_map/ppermute | solution.py:484
  15.4 11.3 %collective-permute-start.3 = (bf16[16,8192]{1,0:T(8,128)(2,1)S(1)}, bf16[16,8192]{1,0:T(8,128)(2,1)S(1)}, u32[]{:S(2)}, u32[]{:S(2)}) collective-permute-start(bf16[16,8192]{1,0:T(8,128)(2,1)S(1)} %pad_maximum_fusion.4.refs_0_), channel_id=1, source_target_pairs={{0,2},{1,3},{2,0},{3,1},{4,6},{5,7},{6,4},{7,5},{8,10},{9,11},{10,... | collective-permute-start | bytes 786440 | tf_op jit(solution)/shard_map/ppermute | solution.py:484
  15.9 10.9 %collective-permute-start.4 = (bf16[16,8192]{1,0:T(8,128)(2,1)S(1)}, bf16[16,8192]{1,0:T(8,128)(2,1)S(1)}, u32[]{:S(2)}, u32[]{:S(2)}) collective-permute-start(bf16[16,8192]{1,0:T(8,128)(2,1)S(1)} %pad_maximum_fusion.4.refs_0_), channel_id=1, source_target_pairs={{0,4},{1,5},{2,6},{3,7},{4,0},{5,1},{6,2},{7,3},{8,12},{9,13},{10,... | collective-permute-start | bytes 786440 | tf_op jit(solution)/shard_map/ppermute | solution.py:484
  16.4 6.5 %copy-start.1 = (s32[128,8]{0,1:T(8,128)S(1)}, s32[128,8]{0,1:T(8,128)}, u32[]{:S(2)}) copy-start(s32[128,8]{0,1:T(8,128)} %param.9) | copy-start | bytes 12292
  16.4 6.5 %copy-start.3 = (s32[128]{0:T(128)S(1)}, s32[128]{0:T(128)}, u32[]{:S(2)}) copy-start(s32[128]{0:T(128)} %param.8) | copy-start | bytes 1540
  26.2 7.7 %collective-permute-start.5 = (bf16[16,8192]{1,0:T(8,128)(2,1)S(1)}, bf16[16,8192]{1,0:T(8,128)(2,1)S(1)}, u32[]{:S(2)}, u32[]{:S(2)}) collective-permute-start(bf16[16,8192]{1,0:T(8,128)(2,1)S(1)} %pad_maximum_fusion.4.refs_0_), channel_id=1, source_target_pairs={{0,1},{1,0},{2,3},{3,2},{4,5},{5,4},{6,7},{7,6},{8,9},{9,8},{10,11... | collective-permute-start | bytes 786440 | tf_op jit(solution)/shard_map/ppermute | solution.py:484
  26.2 4.9 %collective-permute-start.9 = (bf16[16,8192]{1,0:T(8,128)(2,1)S(1)}, bf16[16,8192]{1,0:T(8,128)(2,1)S(1)}, u32[]{:S(2)}, u32[]{:S(2)}) collective-permute-start(bf16[16,8192]{1,0:T(8,128)(2,1)S(1)} %collective-permute-done.8.refs_0_), channel_id=1, source_target_pairs={{0,1},{1,0},{2,3},{3,2},{4,5},{5,4},{6,7},{7,6},{8,9},{9,8},{10,11... | collective-permute-start | bytes 786440 | tf_op jit(solution)/shard_map/ppermute | solution.py:484
  26.7 7.2 %collective-permute-start.6 = (bf16[16,8192]{1,0:T(8,128)(2,1)S(1)}, bf16[16,8192]{1,0:T(8,128)(2,1)S(1)}, u32[]{:S(2)}, u32[]{:S(2)}) collective-permute-start(bf16[16,8192]{1,0:T(8,128)(2,1)S(1)} %collective-permute-done.3.refs_1_), channel_id=1, source_target_pairs={{0,1},{1,0},{2,3},{3,2},{4,5},{5,4},{6,7},{7,6},{8,9},{9,8},{10,11... | collective-permute-start | bytes 786440 | tf_op jit(solution)/shard_map/ppermute | solution.py:484
  26.8 7.1 %collective-permute-start.7 = (bf16[16,8192]{1,0:T(8,128)(2,1)S(1)}, bf16[16,8192]{1,0:T(8,128)(2,1)S(1)}, u32[]{:S(2)}, u32[]{:S(2)}) collective-permute-start(bf16[16,8192]{1,0:T(8,128)(2,1)S(1)} %collective-permute-done.4.refs_2_), channel_id=1, source_target_pairs={{0,1},{1,0},{2,3},{3,2},{4,5},{5,4},{6,7},{7,6},{8,9},{9,8},{10,11... | collective-permute-start | bytes 786440 | tf_op jit(solution)/shard_map/ppermute | solution.py:484
  33.9 3.9 %copy-start.2 = (f32[512]{0:T(512)S(1)}, f32[512]{0:T(512)}, u32[]{:S(2)}) copy-start(f32[512]{0:T(512)} %param.6) | copy-start | bytes 6148
  45.8 3.5 %collective-permute-start.10 = (f16[64,8320]{1,0:T(8,128)(2,1)S(1)}, f16[64,8320]{1,0:T(8,128)(2,1)S(1)}, u32[]{:S(2)}, u32[]{:S(2)}) collective-permute-start(f16[64,8320]{1,0:T(8,128)(2,1)S(1)} %pad_maximum_fusion), channel_id=1, source_target_pairs={{0,1},{1,0},{2,3},{3,2},{4,5},{5,4},{6,7},{7,6},{8,9},{9,8},{10,11... | collective-permute-start | bytes 3194888 | tf_op jit(solution)/shard_map/ppermute | solution.py:484
  54.7 10.3 %collective-permute-start.13 = (f16[16,8320]{1,0:T(8,128)(2,1)S(1)}, f16[16,8320]{1,0:T(8,128)(2,1)S(1)}, u32[]{:S(2)}, u32[]{:S(2)}) collective-permute-start(f16[16,8320]{1,0:T(8,128)(2,1)S(1)} %pad_maximum_fusion.3), channel_id=1, source_target_pairs={{0,6},{1,7},{2,4},{3,5},{4,2},{5,3},{6,0},{7,1},{8,14},{9,15},{10,... | collective-permute-start | bytes 798728 | tf_op jit(solution)/shard_map/ppermute | solution.py:484
  57.2 13.0 %collective-permute-start.11 = (f16[16,8320]{1,0:T(8,128)(2,1)S(1)}, f16[16,8320]{1,0:T(8,128)(2,1)S(1)}, u32[]{:S(2)}, u32[]{:S(2)}) collective-permute-start(f16[16,8320]{1,0:T(8,128)(2,1)S(1)} %pad_maximum_fusion.1), channel_id=1, source_target_pairs={{0,2},{1,3},{2,0},{3,1},{4,6},{5,7},{6,4},{7,5},{8,10},{9,11},{10,... | collective-permute-start | bytes 798728 | tf_op jit(solution)/shard_map/ppermute | solution.py:484
  57.8 12.5 %collective-permute-start.12 = (f16[16,8320]{1,0:T(8,128)(2,1)S(1)}, f16[16,8320]{1,0:T(8,128)(2,1)S(1)}, u32[]{:S(2)}, u32[]{:S(2)}) collective-permute-start(f16[16,8320]{1,0:T(8,128)(2,1)S(1)} %pad_maximum_fusion.2), channel_id=1, source_target_pairs={{0,4},{1,5},{2,6},{3,7},{4,0},{5,1},{6,2},{7,3},{8,12},{9,13},{10,... | collective-permute-start | bytes 798728 | tf_op jit(solution)/shard_map/ppermute | solution.py:484
  71.4 5.3 %collective-permute-start.14 = (f16[4,8320]{1,0:T(4,128)(2,1)S(1)}, f16[4,8320]{1,0:T(4,128)(2,1)S(1)}, u32[]{:S(2)}, u32[]{:S(2)}) collective-permute-start(f16[4,8320]{1,0:T(4,128)(2,1)S(1)} %pad_maximum_fusion.6), channel_id=1, source_target_pairs={{0,8},{8,0},{16,24},{24,16},{1,9},{9,1},{17,25},{25,17},{2,10},{10... | collective-permute-start | bytes 199688 | tf_op jit(solution)/shard_map/ppermute | solution.py:484
  71.6 7.8 %collective-permute-start.15 = (f16[4,8320]{1,0:T(4,128)(2,1)S(1)}, f16[4,8320]{1,0:T(4,128)(2,1)S(1)}, u32[]{:S(2)}, u32[]{:S(2)}) collective-permute-start(f16[4,8320]{1,0:T(4,128)(2,1)S(1)} %pad_maximum_fusion.7), channel_id=1, source_target_pairs={{0,16},{8,24},{16,0},{24,8},{1,17},{9,25},{17,1},{25,9},{2,18},{10... | collective-permute-start | bytes 199688 | tf_op jit(solution)/shard_map/ppermute | solution.py:484
  74.0 6.1 %collective-permute-start.16 = (f16[4,8320]{1,0:T(4,128)(2,1)S(1)}, f16[4,8320]{1,0:T(4,128)(2,1)S(1)}, u32[]{:S(2)}, u32[]{:S(2)}) collective-permute-start(f16[4,8320]{1,0:T(4,128)(2,1)S(1)} %pad_maximum_fusion.8), channel_id=1, source_target_pairs={{0,24},{8,16},{16,8},{24,0},{1,25},{9,17},{17,9},{25,1},{2,26},{10... | collective-permute-start | bytes 199688 | tf_op jit(solution)/shard_map/ppermute | solution.py:484

commit v7 on v6

--- a/solution.py
+++ b/solution.py
@@ -499,7 +499,13 @@
     row_set += [exchange(mine, "row", rows, d) for d in range(1, rows)]
     own_set = [jnp.concatenate(row_set, axis=0)]
     for d in range(1, quads):
-        own_set.append(exchange(own_set[0], "col", cols, 2 * d))
+        low, high = d & -d, 1 << (d.bit_length() - 1)
+        if low == high:
+            own_set.append(exchange(own_set[0], "col", cols, 2 * d))
+            continue
+        first = exchange(own_set[d ^ low][:, : width // 2], "col", cols, 2 * low)
+        second = exchange(own_set[d ^ high][:, width // 2 :], "col", cols, 2 * high)
+        own_set.append(jnp.concatenate([first, second], axis=1))
     other_set = []
     for d in range(quads):
         other_set.append(exchange(own_set[d], "col", cols, 1))

time: 81.4 us -> 82.3 us (1.011)
    ppermute x17 -> x18, starting transfers between devices: 18.6 us -> 19.3 us  [exchange(): return lax.ppermute(value, axis, [(i, i ^ bit) for i in range(size)])]
    ppermute x17 -> x18, waiting for transfers between devices: 21.5 us -> 21.6 us  [exchange(): return lax.ppermute(value, axis, [(i, i ^ bit) for i in range(size)])]
  transfers between devices with their start and end apart: 17 -> 18, of which waited for: 7 -> 10; matrix products, arithmetic and copies ran while one was open for 1% -> 1% of each run, Pallas kernels for 24% -> 25%
where the time goes in v7:
time: 82.3 us; the launch traced here: 82.2 us
  Pallas kernels  34.8 us (42%)
  waiting for transfers between devices  21.6 us (26%)
  starting transfers between devices  19.3 us (23%)
  other arithmetic  4.59 us (6%)
  local copies, waits for them, and re-layouts  1.46 us (2%)
    ppermute x18, waiting for transfers between devices, exchange(): return lax.ppermute(value, axis, [(i, i ^ bit) for i in range(size)])  21.6 us
    ppermute x18, starting transfers between devices, exchange(): return lax.ppermute(value, axis, [(i, i ^ bit) for i in range(size)])  19.3 us
    pallas_call x3, Pallas kernels, back_of(): pl.pallas_call(functools.partial(back_kernel, first, pieces, shifts), in_...  12.7 us
    pallas_call x3, Pallas kernels, scores_of(): pl.pallas_call(functools.partial(score_kernel, places, shifts), in_specs=...  10.4 us
    pallas_call x1, Pallas kernels, relay(): pl.pallas_call(relay_kernel, in_specs=[pl.BlockSpec(memory_space=pltpu.HB...  6.43 us
    pallas_call x1, Pallas kernels, phases_of(): pl.pallas_call(functools.partial(phase_kernel, local, quads), in_specs=wh...  3.21 us
  transfers between devices with their start and end apart: 18, of which 10 were waited for; matrix products, arithmetic and copies ran while one was open for 1% of the time, Pallas kernels for 25%

profile of v7, /device:TPU:0, one launch (start us, length us, event | category | flops | bytes accessed | tf_op | source)
XLA Modules:
  0.0 82.2 jit_solution(12520562277535377527)
XLA Ops:
  0.0 0.8 %copy-done = bf16[4,2,4096]{2,1,0:T(2,128)(2,1)S(1)} copy-done((bf16[4,2,4096]{2,1,0:T(2,128)(2,1)S(1)}, bf16[4,2,4096]{2,1,0:T(2,128)(2,1)}, u32[]{:S(2)}) %copy-start) | copy-done | bytes 65560
  0.9 3.1 %collective-permute-start = (bf16[4,8192]{1,0:T(4,128)(2,1)S(1)}, bf16[4,8192]{1,0:T(4,128)(2,1)S(1)}, u32[]{:S(2)}, u32[]{:S(2)}) collective-permute-start(bf16[4,8192]{1,0:T(4,128)(2,1)S(1)} %shard_map.55), channel_id=1, source_target_pairs={{0,8},{8,0},{16,24},{24,16},{1,9},{9,1},{17,25},{25,17},{2,10},{10... | collective-permute-start | bytes 196616 | tf_op jit(solution)/shard_map/ppermute | solution.py:484
  4.1 2.6 %collective-permute-start.1 = (bf16[4,8192]{1,0:T(4,128)(2,1)S(1)}, bf16[4,8192]{1,0:T(4,128)(2,1)S(1)}, u32[]{:S(2)}, u32[]{:S(2)}) collective-permute-start(bf16[4,8192]{1,0:T(4,128)(2,1)S(1)} %shard_map.55), channel_id=1, source_target_pairs={{0,16},{8,24},{16,0},{24,8},{1,17},{9,25},{17,1},{25,9},{2,18},{10... | collective-permute-start | bytes 196616 | tf_op jit(solution)/shard_map/ppermute | solution.py:484
  6.8 0.2 fusion.16
  7.1 4.2 %collective-permute-done.1 = bf16[4,8192]{1,0:T(4,128)(2,1)S(1)} collective-permute-done((bf16[4,8192]{1,0:T(4,128)(2,1)S(1)}, bf16[4,8192]{1,0:T(4,128)(2,1)S(1)}, u32[]{:S(2)}, u32[]{:S(2)}) %collective-permute-start.1) | collective-permute-done | bytes 65568 | tf_op jit(solution)/shard_map/ppermute | solution.py:484
  11.3 1.4 %collective-permute-done.2 = bf16[4,8192]{1,0:T(4,128)(2,1)S(1)} collective-permute-done((bf16[4,8192]{1,0:T(4,128)(2,1)S(1)}, bf16[4,8192]{1,0:T(4,128)(2,1)S(1)}, u32[]{:S(2)}, u32[]{:S(2)}) %collective-permute-start.2) | collective-permute-done | bytes 65568 | tf_op jit(solution)/shard_map/ppermute | solution.py:484
  12.9 1.6 %collective-permute-start.4 = (bf16[16,8192]{1,0:T(8,128)(2,1)S(1)}, bf16[16,8192]{1,0:T(8,128)(2,1)S(1)}, u32[]{:S(2)}, u32[]{:S(2)}) collective-permute-start(bf16[16,8192]{1,0:T(8,128)(2,1)S(1)} %pad_maximum_fusion.4.refs_0_), channel_id=1, source_target_pairs={{0,4},{1,5},{2,6},{3,7},{4,0},{5,1},{6,2},{7,3},{8,12},{9,13},{10,... | collective-permute-start | bytes 786440 | tf_op jit(solution)/shard_map/ppermute | solution.py:484
  14.5 1.5 %collective-permute-start.3 = (bf16[16,8192]{1,0:T(8,128)(2,1)S(1)}, bf16[16,8192]{1,0:T(8,128)(2,1)S(1)}, u32[]{:S(2)}, u32[]{:S(2)}) collective-permute-start(bf16[16,8192]{1,0:T(8,128)(2,1)S(1)} %pad_maximum_fusion.4.refs_0_), channel_id=1, source_target_pairs={{0,2},{1,3},{2,0},{3,1},{4,6},{5,7},{6,4},{7,5},{8,10},{9,11},{10,... | collective-permute-start | bytes 786440 | tf_op jit(solution)/shard_map/ppermute | solution.py:484
  16.0 6.4 %shard_map.57.refs_9_.refs_8_.refs_7_.x_ref = bf16[528,8192]{1,0:T(8,128)(2,1)S(1)} custom-call(bf16[512,64,128]{2,1,0:T(8,128)(2,1)} %bitcast.22), custom_call_target="tpu_custom_call" | custom-call | flops 4194304 | bytes 16777216 | tf_op jit(solution)/shard_map/pallas_call | solution.py:83
  22.5 3.2 %shard_map.56 = (f32[16,512,128]{2,1,0:T(8,128)S(1)}, f32[16,512,128]{2,1,0:T(8,128)S(1)}, f32[512,128]{1,0:T(8,128)S(1)}, f32[16,512,128]{2,1,0:T(8,128)S(1)}, ...) custom-call(s32[1,128]{1,0:T(1,128)S(1)} %bitcast.21, s32[8,128]{1,0:T(8,128)S(1)} %bitcast.19, ...), custom_call_target="tpu_custom_call" | custom-call | flops 12582912 | bytes 16777216 | tf_op jit(solution)/shard_map/pallas_call | solution.py:218
  25.8 0.6 collective-permute-start.8
  26.4 0.6 collective-permute-start.9
  27.0 0.5 collective-permute-start.7
  27.5 3.9 %shard_map.58 = (f32[384,512]{1,0:T(8,128)S(1)}, f32[48,128]{1,0:T(8,128)S(1)}) custom-call(bf16[16,8192]{1,0:T(8,128)(2,1)S(1)} %pad_maximum_fusion.4.refs_0_, bf16[16,8192]{1,0:T(8,128)(2,1)S(1)} %collective-permute-done.3.refs_1_, bf16[16,8192]{1,0:T(8,128)(2,1)S(1)} %collective-permute-done.4.refs_2_, ...), custom_call_target="tpu_custom_call" | custom-call | flops 3221225472 | bytes 9961472 | tf_op jit(solution)/shard_map/pallas_call | solution.py:316
  31.4 0.4 collective-permute-done.8
  31.8 0.3 collective-permute-done.9
  32.2 3.8 %shard_map.59 = (f32[384,512]{1,0:T(8,128)S(1)}, f32[48,128]{1,0:T(8,128)S(1)}) custom-call(bf16[16,8192]{1,0:T(8,128)(2,1)S(1)} %collective-permute-done.5.refs_0_, bf16[16,8192]{1,0:T(8,128)(2,1)S(1)} %collective-permute-done.6.refs_1_, bf16[16,8192]{1,0:T(8,128)(2,1)S(1)} %collective-permute-done.7.refs_2_, ...), custom_call_target="tpu_custom_call" | custom-call | flops 3221225472 | bytes 9961472 | tf_op jit(solution)/shard_map/pallas_call | solution.py:316
  36.1 2.7 %shard_map.60 = (f32[256,512]{1,0:T(8,128)S(1)}, f32[32,128]{1,0:T(8,128)S(1)}) custom-call(bf16[16,8192]{1,0:T(8,128)(2,1)S(1)} %constant_dynamic-update-slice_fusion.refs_0_, bf16[16,8192]{1,0:T(8,128)(2,1)S(1)} %collective-permute-done.10.refs_1_, f32[16,512,128]{2,1,0:T(8,128)S(1)} %get-tuple-element.26.refs_3_.refs_2_.cos_ref, ...), custom_call_target="tpu_custom_call" | custom-call | flops 2147483648 | bytes 9437184 | tf_op jit(solution)/shard_map/pallas_call | solution.py:316
  38.8 1.2 %shard_map.61 = (bf16[512,512]{1,0:T(8,128)(2,1)S(1)}, bf16[512,512]{1,0:T(8,128)(2,1)S(1)}, f32[64,128]{1,0:T(8,128)S(1)}, f32[64,128]{1,0:T(8,128)S(1)}, f32[64,128]{1,0:T(8,128)S(1)}, /*index=5*/f32[64,128]{1,0:T(8,128)S(1)}) custom-call(f32[384,512]{1,0:T(8,128)S(1)} %get-tuple-element.32.refs_0_, f32[384,512]{1,0:T(8,128)S(1)} %get-tuple-element.33.refs_1_, ...), custom_call_target="tpu_custom_call" | custom-call | flops 10485760 | bytes 6291456 | tf_op jit(solution)/shard_map/pallas_call | solution.py:385
  40.0 6.0 %shard_map.63 = f32[64,8192]{1,0:T(8,128)S(1)} custom-call(bf16[512,512]{1,0:T(8,128)(2,1)S(1)} %get-tuple-element.39.w_ref, f32[16,512,128]{2,1,0:T(8,128)S(1)} %get-tuple-element.29.refs_6_.refs_5_.cos_ref, f32[16,512,128]{2,1,0:T(8,128)S(1)} %get-tuple-element.30.refs_7_.refs_6_.sin_ref, f32[512,128]{1,0:T(8,128)S(1)} %get-tuple-element.31.refs_8_.refs_7_.sign_ref, ...), custom_call_target="tpu_custom_call" | custom-call | flops 4294967296 | bytes 9043968 | tf_op jit(solution)/shard_map/pallas_call | solution.py:468
  46.2 0.2 multiply_convert_fusion
  46.6 0.2 pad_maximum_fusion
  46.8 0.5 collective-permute-start.11
  47.4 3.3 %shard_map.62 = f32[32,8192]{1,0:T(8,128)S(1)} custom-call(bf16[512,512]{1,0:T(8,128)(2,1)S(1)} %get-tuple-element.44.w_ref, f32[16,512,128]{2,1,0:T(8,128)S(1)} %get-tuple-element.26.refs_3_.refs_2_.cos_ref, f32[16,512,128]{2,1,0:T(8,128)S(1)} %get-tuple-element.27.refs_4_.refs_3_.sin_ref, f32[512,128]{1,0:T(8,128)S(1)} %get-tuple-element.28.refs_5_.refs_4_.sign_ref, ...), custom_call_target="tpu_custom_call" | custom-call | flops 2147483648 | bytes 8716288 | tf_op jit(solution)/shard_map/pallas_call | solution.py:468
  50.9 0.2 exponential_reduce_fusion
  51.1 0.2 slice_multiply_fusion
  51.3 0.2 exponential_reduce_fusion.6
  51.9 0.2 slice_add_fusion.1
  52.4 3.3 %shard_map.64 = f32[32,8192]{1,0:T(8,128)S(1)} custom-call(bf16[512,512]{1,0:T(8,128)(2,1)S(1)} %get-tuple-element.44.w_ref, f32[16,512,128]{2,1,0:T(8,128)S(1)} %get-tuple-element.26.refs_3_.refs_2_.cos_ref, f32[16,512,128]{2,1,0:T(8,128)S(1)} %get-tuple-element.27.refs_4_.refs_3_.sin_ref, f32[512,128]{1,0:T(8,128)S(1)} %get-tuple-element.28.refs_5_.refs_4_.sign_ref, ...), custom_call_target="tpu_custom_call" | custom-call | flops 2147483648 | bytes 8716288 | tf_op jit(solution)/shard_map/pallas_call | solution.py:468
  55.8 0.2 slice_add_fusion
  56.1 1.9 %collective-permute-start.14 = (f16[16,8320]{1,0:T(8,128)(2,1)S(1)}, f16[16,8320]{1,0:T(8,128)(2,1)S(1)}, u32[]{:S(2)}, u32[]{:S(2)}) collective-permute-start(f16[16,8320]{1,0:T(8,128)(2,1)S(1)} %pad_maximum_fusion.3), channel_id=1, source_target_pairs={{0,6},{1,7},{2,4},{3,5},{4,2},{5,3},{6,0},{7,1},{8,14},{9,15},{10,... | collective-permute-start | bytes 798728 | tf_op jit(solution)/shard_map/ppermute | solution.py:484
  58.0 0.5 collective-permute-start.12
  58.5 1.2 %collective-permute-start.13 = (f16[16,8320]{1,0:T(8,128)(2,1)S(1)}, f16[16,8320]{1,0:T(8,128)(2,1)S(1)}, u32[]{:S(2)}, u32[]{:S(2)}) collective-permute-start(f16[16,8320]{1,0:T(8,128)(2,1)S(1)} %pad_maximum_fusion.2), channel_id=1, source_target_pairs={{0,4},{1,5},{2,6},{3,7},{4,0},{5,1},{6,2},{7,3},{8,12},{9,13},{10,... | collective-permute-start | bytes 798728 | tf_op jit(solution)/shard_map/ppermute | solution.py:484
  59.7 6.7 %collective-permute-done.14 = f16[16,8320]{1,0:T(8,128)(2,1)S(1)} collective-permute-done((f16[16,8320]{1,0:T(8,128)(2,1)S(1)}, f16[16,8320]{1,0:T(8,128)(2,1)S(1)}, u32[]{:S(2)}, u32[]{:S(2)}) %collective-permute-start.14) | collective-permute-done | bytes 266272 | tf_op jit(solution)/shard_map/ppermute | solution.py:484
  66.4 4.1 %collective-permute-done.12 = f16[16,8320]{1,0:T(8,128)(2,1)S(1)} collective-permute-done((f16[16,8320]{1,0:T(8,128)(2,1)S(1)}, f16[16,8320]{1,0:T(8,128)(2,1)S(1)}, u32[]{:S(2)}, u32[]{:S(2)}) %collective-permute-start.12) | collective-permute-done | bytes 266272 | tf_op jit(solution)/shard_map/ppermute | solution.py:484
  70.6 0.5 collective-permute-done.13
  71.2 0.2 slice_add_fusion.6
  71.4 0.2 exponential_reduce_fusion.10
  71.8 0.2 fusion
  72.0 0.2 fusion.13
  72.4 2.4 %collective-permute-start.16 = (f16[4,8320]{1,0:T(4,128)(2,1)S(1)}, f16[4,8320]{1,0:T(4,128)(2,1)S(1)}, u32[]{:S(2)}, u32[]{:S(2)}) collective-permute-start(f16[4,8320]{1,0:T(4,128)(2,1)S(1)} %pad_maximum_fusion.7), channel_id=1, source_target_pairs={{0,16},{8,24},{16,0},{24,8},{1,17},{9,25},{17,1},{25,9},{2,18},{10... | collective-permute-start | bytes 199688 | tf_op jit(solution)/shard_map/ppermute | solution.py:484
  74.9 2.1 %collective-permute-start.17 = (f16[4,8320]{1,0:T(4,128)(2,1)S(1)}, f16[4,8320]{1,0:T(4,128)(2,1)S(1)}, u32[]{:S(2)}, u32[]{:S(2)}) collective-permute-start(f16[4,8320]{1,0:T(4,128)(2,1)S(1)} %pad_maximum_fusion.8), channel_id=1, source_target_pairs={{0,24},{8,16},{16,8},{24,0},{1,25},{9,17},{17,9},{25,1},{2,26},{10... | collective-permute-start | bytes 199688 | tf_op jit(solution)/shard_map/ppermute | solution.py:484
  77.0 0.9 %collective-permute-done.15 = f16[4,8320]{1,0:T(4,128)(2,1)S(1)} collective-permute-done((f16[4,8320]{1,0:T(4,128)(2,1)S(1)}, f16[4,8320]{1,0:T(4,128)(2,1)S(1)}, u32[]{:S(2)}, u32[]{:S(2)}) %collective-permute-start.15) | collective-permute-done | bytes 66592 | tf_op jit(solution)/shard_map/ppermute | solution.py:484
  77.9 2.2 %collective-permute-done.16 = f16[4,8320]{1,0:T(4,128)(2,1)S(1)} collective-permute-done((f16[4,8320]{1,0:T(4,128)(2,1)S(1)}, f16[4,8320]{1,0:T(4,128)(2,1)S(1)}, u32[]{:S(2)}, u32[]{:S(2)}) %collective-permute-start.16) | collective-permute-done | bytes 66592 | tf_op jit(solution)/shard_map/ppermute | solution.py:484
  80.1 0.9 %collective-permute-done.17 = f16[4,8320]{1,0:T(4,128)(2,1)S(1)} collective-permute-done((f16[4,8320]{1,0:T(4,128)(2,1)S(1)}, f16[4,8320]{1,0:T(4,128)(2,1)S(1)}, u32[]{:S(2)}, u32[]{:S(2)}) %collective-permute-start.17) | collective-permute-done | bytes 66592 | tf_op jit(solution)/shard_map/ppermute | solution.py:484
  81.0 0.2 fusion.51
  81.3 0.2 fusion.8.in_ref
  81.4 0.7 shard_map.65
  (61 shorter events, 2.7 us)
Async XLA Ops:
  0.0 0.8 %copy-start = (bf16[4,2,4096]{2,1,0:T(2,128)(2,1)S(1)}, bf16[4,2,4096]{2,1,0:T(2,128)(2,1)}, u32[]{:S(2)}) copy-start(bf16[4,2,4096]{2,1,0:T(2,128)(2,1)} %param.7) | copy-start | bytes 196612
  0.9 6.2 %collective-permute-start = (bf16[4,8192]{1,0:T(4,128)(2,1)S(1)}, bf16[4,8192]{1,0:T(4,128)(2,1)S(1)}, u32[]{:S(2)}, u32[]{:S(2)}) collective-permute-start(bf16[4,8192]{1,0:T(4,128)(2,1)S(1)} %shard_map.55), channel_id=1, source_target_pairs={{0,8},{8,0},{16,24},{24,16},{1,9},{9,1},{17,25},{25,17},{2,10},{10... | collective-permute-start | bytes 196616 | tf_op jit(solution)/shard_map/ppermute | solution.py:484
  4.1 7.3 %collective-permute-start.1 = (bf16[4,8192]{1,0:T(4,128)(2,1)S(1)}, bf16[4,8192]{1,0:T(4,128)(2,1)S(1)}, u32[]{:S(2)}, u32[]{:S(2)}) collective-permute-start(bf16[4,8192]{1,0:T(4,128)(2,1)S(1)} %shard_map.55), channel_id=1, source_target_pairs={{0,16},{8,24},{16,0},{24,8},{1,17},{9,25},{17,1},{25,9},{2,18},{10... | collective-permute-start | bytes 196616 | tf_op jit(solution)/shard_map/ppermute | solution.py:484
  6.6 6.1 %collective-permute-start.2 = (bf16[4,8192]{1,0:T(4,128)(2,1)S(1)}, bf16[4,8192]{1,0:T(4,128)(2,1)S(1)}, u32[]{:S(2)}, u32[]{:S(2)}) collective-permute-start(bf16[4,8192]{1,0:T(4,128)(2,1)S(1)} %shard_map.55), channel_id=1, source_target_pairs={{0,24},{8,16},{16,8},{24,0},{1,25},{9,17},{17,9},{25,1},{2,26},{10... | collective-permute-start | bytes 196616 | tf_op jit(solution)/shard_map/ppermute | solution.py:484
  12.9 12.9 %collective-permute-start.4 = (bf16[16,8192]{1,0:T(8,128)(2,1)S(1)}, bf16[16,8192]{1,0:T(8,128)(2,1)S(1)}, u32[]{:S(2)}, u32[]{:S(2)}) collective-permute-start(bf16[16,8192]{1,0:T(8,128)(2,1)S(1)} %pad_maximum_fusion.4.refs_0_), channel_id=1, source_target_pairs={{0,4},{1,5},{2,6},{3,7},{4,0},{5,1},{6,2},{7,3},{8,12},{9,13},{10,... | collective-permute-start | bytes 786440 | tf_op jit(solution)/shard_map/ppermute | solution.py:484
  14.5 11.9 %collective-permute-start.3 = (bf16[16,8192]{1,0:T(8,128)(2,1)S(1)}, bf16[16,8192]{1,0:T(8,128)(2,1)S(1)}, u32[]{:S(2)}, u32[]{:S(2)}) collective-permute-start(bf16[16,8192]{1,0:T(8,128)(2,1)S(1)} %pad_maximum_fusion.4.refs_0_), channel_id=1, source_target_pairs={{0,2},{1,3},{2,0},{3,1},{4,6},{5,7},{6,4},{7,5},{8,10},{9,11},{10,... | collective-permute-start | bytes 786440 | tf_op jit(solution)/shard_map/ppermute | solution.py:484
  16.0 6.5 %copy-start.1 = (s32[128,8]{0,1:T(8,128)S(1)}, s32[128,8]{0,1:T(8,128)}, u32[]{:S(2)}) copy-start(s32[128,8]{0,1:T(8,128)} %param.9) | copy-start | bytes 12292
  16.0 6.5 %copy-start.3 = (s32[128]{0:T(128)S(1)}, s32[128]{0:T(128)}, u32[]{:S(2)}) copy-start(s32[128]{0:T(128)} %param.8) | copy-start | bytes 1540
  25.7 6.5 %collective-permute-start.5 = (bf16[16,8192]{1,0:T(8,128)(2,1)S(1)}, bf16[16,8192]{1,0:T(8,128)(2,1)S(1)}, u32[]{:S(2)}, u32[]{:S(2)}) collective-permute-start(bf16[16,8192]{1,0:T(8,128)(2,1)S(1)} %pad_maximum_fusion.4.refs_0_), channel_id=1, source_target_pairs={{0,1},{1,0},{2,3},{3,2},{4,5},{5,4},{6,7},{7,6},{8,9},{9,8},{10,11... | collective-permute-start | bytes 786440 | tf_op jit(solution)/shard_map/ppermute | solution.py:484
  25.8 6.0 %collective-permute-start.8 = (bf16[16,4096]{1,0:T(8,128)(2,1)S(1)}, bf16[16,4096]{1,0:T(8,128)(2,1)S(1)}, u32[]{:S(2)}, u32[]{:S(2)}) collective-permute-start(bf16[16,4096]{1,0:T(8,128)(2,1)S(1)} %slice.257), channel_id=1, source_target_pairs={{0,2},{1,3},{2,0},{3,1},{4,6},{5,7},{6,4},{7,5},{8,10},{9,11},{10,... | collective-permute-start | bytes 393224 | tf_op jit(solution)/shard_map/ppermute | solution.py:484
  26.4 5.7 %collective-permute-start.9 = (bf16[16,4096]{1,0:T(8,128)(2,1)S(1)}, bf16[16,4096]{1,0:T(8,128)(2,1)S(1)}, u32[]{:S(2)}, u32[]{:S(2)}) collective-permute-start(bf16[16,4096]{1,0:T(8,128)(2,1)S(1)} %slice.258), channel_id=1, source_target_pairs={{0,4},{1,5},{2,6},{3,7},{4,0},{5,1},{6,2},{7,3},{8,12},{9,13},{10,... | collective-permute-start | bytes 393224 | tf_op jit(solution)/shard_map/ppermute | solution.py:484
  27.0 5.2 %collective-permute-start.6 = (bf16[16,8192]{1,0:T(8,128)(2,1)S(1)}, bf16[16,8192]{1,0:T(8,128)(2,1)S(1)}, u32[]{:S(2)}, u32[]{:S(2)}) collective-permute-start(bf16[16,8192]{1,0:T(8,128)(2,1)S(1)} %collective-permute-done.3.refs_1_), channel_id=1, source_target_pairs={{0,1},{1,0},{2,3},{3,2},{4,5},{5,4},{6,7},{7,6},{8,9},{9,8},{10,11... | collective-permute-start | bytes 786440 | tf_op jit(solution)/shard_map/ppermute | solution.py:484
  27.0 5.2 %collective-permute-start.7 = (bf16[16,8192]{1,0:T(8,128)(2,1)S(1)}, bf16[16,8192]{1,0:T(8,128)(2,1)S(1)}, u32[]{:S(2)}, u32[]{:S(2)}) collective-permute-start(bf16[16,8192]{1,0:T(8,128)(2,1)S(1)} %collective-permute-done.4.refs_2_), channel_id=1, source_target_pairs={{0,1},{1,0},{2,3},{3,2},{4,5},{5,4},{6,7},{7,6},{8,9},{9,8},{10,11... | collective-permute-start | bytes 786440 | tf_op jit(solution)/shard_map/ppermute | solution.py:484
  32.1 4.0 %collective-permute-start.10 = (bf16[16,8192]{1,0:T(8,128)(2,1)S(1)}, bf16[16,8192]{1,0:T(8,128)(2,1)S(1)}, u32[]{:S(2)}, u32[]{:S(2)}) collective-permute-start(bf16[16,8192]{1,0:T(8,128)(2,1)S(1)} %constant_dynamic-update-slice_fusion.refs_0_), channel_id=1, source_target_pairs={{0,1},{1,0},{2,3},{3,2},{4,5},{5,4},{6,7},{7,6},{8,9},{9,8},{10,11... | collective-permute-start | bytes 786440 | tf_op jit(solution)/shard_map/ppermute | solution.py:484
  36.0 2.7 %copy-start.2 = (f32[512]{0:T(512)S(1)}, f32[512]{0:T(512)}, u32[]{:S(2)}) copy-start(f32[512]{0:T(512)} %param.6) | copy-start | bytes 6148
  46.8 3.9 %collective-permute-start.11 = (f16[64,8320]{1,0:T(8,128)(2,1)S(1)}, f16[64,8320]{1,0:T(8,128)(2,1)S(1)}, u32[]{:S(2)}, u32[]{:S(2)}) collective-permute-start(f16[64,8320]{1,0:T(8,128)(2,1)S(1)} %pad_maximum_fusion), channel_id=1, source_target_pairs={{0,1},{1,0},{2,3},{3,2},{4,5},{5,4},{6,7},{7,6},{8,9},{9,8},{10,11... | collective-permute-start | bytes 3194888 | tf_op jit(solution)/shard_map/ppermute | solution.py:484
  56.1 10.3 %collective-permute-start.14 = (f16[16,8320]{1,0:T(8,128)(2,1)S(1)}, f16[16,8320]{1,0:T(8,128)(2,1)S(1)}, u32[]{:S(2)}, u32[]{:S(2)}) collective-permute-start(f16[16,8320]{1,0:T(8,128)(2,1)S(1)} %pad_maximum_fusion.3), channel_id=1, source_target_pairs={{0,6},{1,7},{2,4},{3,5},{4,2},{5,3},{6,0},{7,1},{8,14},{9,15},{10,... | collective-permute-start | bytes 798728 | tf_op jit(solution)/shard_map/ppermute | solution.py:484
  58.0 12.6 %collective-permute-start.12 = (f16[16,8320]{1,0:T(8,128)(2,1)S(1)}, f16[16,8320]{1,0:T(8,128)(2,1)S(1)}, u32[]{:S(2)}, u32[]{:S(2)}) collective-permute-start(f16[16,8320]{1,0:T(8,128)(2,1)S(1)} %pad_maximum_fusion.1), channel_id=1, source_target_pairs={{0,2},{1,3},{2,0},{3,1},{4,6},{5,7},{6,4},{7,5},{8,10},{9,11},{10,... | collective-permute-start | bytes 798728 | tf_op jit(solution)/shard_map/ppermute | solution.py:484
  58.5 12.6 %collective-permute-start.13 = (f16[16,8320]{1,0:T(8,128)(2,1)S(1)}, f16[16,8320]{1,0:T(8,128)(2,1)S(1)}, u32[]{:S(2)}, u32[]{:S(2)}) collective-permute-start(f16[16,8320]{1,0:T(8,128)(2,1)S(1)} %pad_maximum_fusion.2), channel_id=1, source_target_pairs={{0,4},{1,5},{2,6},{3,7},{4,0},{5,1},{6,2},{7,3},{8,12},{9,13},{10,... | collective-permute-start | bytes 798728 | tf_op jit(solution)/shard_map/ppermute | solution.py:484
  72.3 5.6 %collective-permute-start.15 = (f16[4,8320]{1,0:T(4,128)(2,1)S(1)}, f16[4,8320]{1,0:T(4,128)(2,1)S(1)}, u32[]{:S(2)}, u32[]{:S(2)}) collective-permute-start(f16[4,8320]{1,0:T(4,128)(2,1)S(1)} %pad_maximum_fusion.6), channel_id=1, source_target_pairs={{0,8},{8,0},{16,24},{24,16},{1,9},{9,1},{17,25},{25,17},{2,10},{10... | collective-permute-start | bytes 199688 | tf_op jit(solution)/shard_map/ppermute | solution.py:484
  72.4 7.6 %collective-permute-start.16 = (f16[4,8320]{1,0:T(4,128)(2,1)S(1)}, f16[4,8320]{1,0:T(4,128)(2,1)S(1)}, u32[]{:S(2)}, u32[]{:S(2)}) collective-permute-start(f16[4,8320]{1,0:T(4,128)(2,1)S(1)} %pad_maximum_fusion.7), channel_id=1, source_target_pairs={{0,16},{8,24},{16,0},{24,8},{1,17},{9,25},{17,1},{25,9},{2,18},{10... | collective-permute-start | bytes 199688 | tf_op jit(solution)/shard_map/ppermute | solution.py:484
  74.9 6.1 %collective-permute-start.17 = (f16[4,8320]{1,0:T(4,128)(2,1)S(1)}, f16[4,8320]{1,0:T(4,128)(2,1)S(1)}, u32[]{:S(2)}, u32[]{:S(2)}) collective-permute-start(f16[4,8320]{1,0:T(4,128)(2,1)S(1)} %pad_maximum_fusion.8), channel_id=1, source_target_pairs={{0,24},{8,16},{16,8},{24,0},{1,25},{9,17},{17,9},{25,1},{2,26},{10... | collective-permute-start | bytes 199688 | tf_op jit(solution)/shard_map/ppermute | solution.py:484

commit v8 on v7

--- a/solution.py
+++ b/solution.py
@@ -15,6 +15,7 @@
 LANES = 128
 PAIR = 2 * LANES
 UNROLL = 8
+BACK_UNROLL = 16
 WIRE = jnp.float16
 VMEM_LIMIT = 8 << 20
 RELAY_LIMIT = 14 << 20
@@ -449,15 +450,15 @@
     mix(jnp.int32(0), mix_a)
 
     def step(i, carry):
-        for at in range(0, UNROLL, 2):
-            index = i * UNROLL + at
+        for at in range(0, BACK_UNROLL, 2):
+            index = i * BACK_UNROLL + at
             mix(index + 1, mix_b)
             turn(index, mix_a)
             mix(index + 2, mix_a)
             turn(index + 1, mix_b)
         return carry
 
-    lax.fori_loop(0, count // UNROLL, step, 0)
+    lax.fori_loop(0, count // BACK_UNROLL, step, 0)
 
 
 def back_of(weight, x, phases, shifts, first, pieces, piece_rows):

time: 82.3 us -> 80.6 us (0.979)
  Pallas kernels: 34.8 us -> 33 us
    pallas_call x3, Pallas kernels: 12.7 us -> 10.9 us  [back_of(): pl.pallas_call(functools.partial(back_kernel, first, pieces, shifts), in_...]
where the time goes in v8:
time: 80.6 us; the launch traced here: 80.4 us
  Pallas kernels  33 us (41%)
  waiting for transfers between devices  21.7 us (27%)
  starting transfers between devices  19.3 us (24%)
  other arithmetic  4.59 us (6%)
  local copies, waits for them, and re-layouts  1.46 us (2%)
    ppermute x18, waiting for transfers between devices, exchange(): return lax.ppermute(value, axis, [(i, i ^ bit) for i in range(size)])  21.7 us
    ppermute x18, starting transfers between devices, exchange(): return lax.ppermute(value, axis, [(i, i ^ bit) for i in range(size)])  19.3 us
    pallas_call x3, Pallas kernels, back_of(): pl.pallas_call(functools.partial(back_kernel, first, pieces, shifts), in_...  10.9 us
    pallas_call x3, Pallas kernels, scores_of(): pl.pallas_call(functools.partial(score_kernel, places, shifts), in_specs=...  10.4 us
    pallas_call x1, Pallas kernels, relay(): pl.pallas_call(relay_kernel, in_specs=[pl.BlockSpec(memory_space=pltpu.HB...  6.43 us
    pallas_call x1, Pallas kernels, phases_of(): pl.pallas_call(functools.partial(phase_kernel, local, quads), in_specs=wh...  3.21 us
  transfers between devices with their start and end apart: 18, of which 10 were waited for; matrix products, arithmetic and copies ran while one was open for 1% of the time, Pallas kernels for 25%

profile of v8, /device:TPU:0, one launch (start us, length us, event | category | flops | bytes accessed | tf_op | source)
XLA Modules:
  0.0 80.4 jit_solution(2102211578605933342)
XLA Ops:
  0.0 0.8 %copy-done = bf16[4,2,4096]{2,1,0:T(2,128)(2,1)S(1)} copy-done((bf16[4,2,4096]{2,1,0:T(2,128)(2,1)S(1)}, bf16[4,2,4096]{2,1,0:T(2,128)(2,1)}, u32[]{:S(2)}) %copy-start) | copy-done | bytes 65560
  0.9 3.1 %collective-permute-start = (bf16[4,8192]{1,0:T(4,128)(2,1)S(1)}, bf16[4,8192]{1,0:T(4,128)(2,1)S(1)}, u32[]{:S(2)}, u32[]{:S(2)}) collective-permute-start(bf16[4,8192]{1,0:T(4,128)(2,1)S(1)} %shard_map.55), channel_id=1, source_target_pairs={{0,8},{8,0},{16,24},{24,16},{1,9},{9,1},{17,25},{25,17},{2,10},{10... | collective-permute-start | bytes 196616 | tf_op jit(solution)/shard_map/ppermute | solution.py:485
  4.1 2.6 %collective-permute-start.1 = (bf16[4,8192]{1,0:T(4,128)(2,1)S(1)}, bf16[4,8192]{1,0:T(4,128)(2,1)S(1)}, u32[]{:S(2)}, u32[]{:S(2)}) collective-permute-start(bf16[4,8192]{1,0:T(4,128)(2,1)S(1)} %shard_map.55), channel_id=1, source_target_pairs={{0,16},{8,24},{16,0},{24,8},{1,17},{9,25},{17,1},{25,9},{2,18},{10... | collective-permute-start | bytes 196616 | tf_op jit(solution)/shard_map/ppermute | solution.py:485
  6.8 0.2 fusion.16
  7.1 4.2 %collective-permute-done.1 = bf16[4,8192]{1,0:T(4,128)(2,1)S(1)} collective-permute-done((bf16[4,8192]{1,0:T(4,128)(2,1)S(1)}, bf16[4,8192]{1,0:T(4,128)(2,1)S(1)}, u32[]{:S(2)}, u32[]{:S(2)}) %collective-permute-start.1) | collective-permute-done | bytes 65568 | tf_op jit(solution)/shard_map/ppermute | solution.py:485
  11.3 1.4 %collective-permute-done.2 = bf16[4,8192]{1,0:T(4,128)(2,1)S(1)} collective-permute-done((bf16[4,8192]{1,0:T(4,128)(2,1)S(1)}, bf16[4,8192]{1,0:T(4,128)(2,1)S(1)}, u32[]{:S(2)}, u32[]{:S(2)}) %collective-permute-start.2) | collective-permute-done | bytes 65568 | tf_op jit(solution)/shard_map/ppermute | solution.py:485
  12.9 1.6 %collective-permute-start.4 = (bf16[16,8192]{1,0:T(8,128)(2,1)S(1)}, bf16[16,8192]{1,0:T(8,128)(2,1)S(1)}, u32[]{:S(2)}, u32[]{:S(2)}) collective-permute-start(bf16[16,8192]{1,0:T(8,128)(2,1)S(1)} %pad_maximum_fusion.4.refs_0_), channel_id=1, source_target_pairs={{0,4},{1,5},{2,6},{3,7},{4,0},{5,1},{6,2},{7,3},{8,12},{9,13},{10,... | collective-permute-start | bytes 786440 | tf_op jit(solution)/shard_map/ppermute | solution.py:485
  14.5 1.5 %collective-permute-start.3 = (bf16[16,8192]{1,0:T(8,128)(2,1)S(1)}, bf16[16,8192]{1,0:T(8,128)(2,1)S(1)}, u32[]{:S(2)}, u32[]{:S(2)}) collective-permute-start(bf16[16,8192]{1,0:T(8,128)(2,1)S(1)} %pad_maximum_fusion.4.refs_0_), channel_id=1, source_target_pairs={{0,2},{1,3},{2,0},{3,1},{4,6},{5,7},{6,4},{7,5},{8,10},{9,11},{10,... | collective-permute-start | bytes 786440 | tf_op jit(solution)/shard_map/ppermute | solution.py:485
  16.0 6.4 %shard_map.57.refs_9_.refs_8_.refs_7_.x_ref = bf16[528,8192]{1,0:T(8,128)(2,1)S(1)} custom-call(bf16[512,64,128]{2,1,0:T(8,128)(2,1)} %bitcast.22), custom_call_target="tpu_custom_call" | custom-call | flops 4194304 | bytes 16777216 | tf_op jit(solution)/shard_map/pallas_call | solution.py:84
  22.5 3.2 %shard_map.56 = (f32[16,512,128]{2,1,0:T(8,128)S(1)}, f32[16,512,128]{2,1,0:T(8,128)S(1)}, f32[512,128]{1,0:T(8,128)S(1)}, f32[16,512,128]{2,1,0:T(8,128)S(1)}, ...) custom-call(s32[1,128]{1,0:T(1,128)S(1)} %bitcast.21, s32[8,128]{1,0:T(8,128)S(1)} %bitcast.19, ...), custom_call_target="tpu_custom_call" | custom-call | flops 12582912 | bytes 16777216 | tf_op jit(solution)/shard_map/pallas_call | solution.py:219
  25.8 0.6 collective-permute-start.8
  26.4 0.6 collective-permute-start.9
  27.0 0.5 collective-permute-start.7
  27.5 3.9 %shard_map.58 = (f32[384,512]{1,0:T(8,128)S(1)}, f32[48,128]{1,0:T(8,128)S(1)}) custom-call(bf16[16,8192]{1,0:T(8,128)(2,1)S(1)} %pad_maximum_fusion.4.refs_0_, bf16[16,8192]{1,0:T(8,128)(2,1)S(1)} %collective-permute-done.3.refs_1_, bf16[16,8192]{1,0:T(8,128)(2,1)S(1)} %collective-permute-done.4.refs_2_, ...), custom_call_target="tpu_custom_call" | custom-call | flops 3221225472 | bytes 9961472 | tf_op jit(solution)/shard_map/pallas_call | solution.py:317
  31.4 0.4 collective-permute-done.8
  31.8 0.3 collective-permute-done.9
  32.2 3.8 %shard_map.59 = (f32[384,512]{1,0:T(8,128)S(1)}, f32[48,128]{1,0:T(8,128)S(1)}) custom-call(bf16[16,8192]{1,0:T(8,128)(2,1)S(1)} %collective-permute-done.5.refs_0_, bf16[16,8192]{1,0:T(8,128)(2,1)S(1)} %collective-permute-done.6.refs_1_, bf16[16,8192]{1,0:T(8,128)(2,1)S(1)} %collective-permute-done.7.refs_2_, ...), custom_call_target="tpu_custom_call" | custom-call | flops 3221225472 | bytes 9961472 | tf_op jit(solution)/shard_map/pallas_call | solution.py:317
  36.1 2.7 %shard_map.60 = (f32[256,512]{1,0:T(8,128)S(1)}, f32[32,128]{1,0:T(8,128)S(1)}) custom-call(bf16[16,8192]{1,0:T(8,128)(2,1)S(1)} %constant_dynamic-update-slice_fusion.refs_0_, bf16[16,8192]{1,0:T(8,128)(2,1)S(1)} %collective-permute-done.10.refs_1_, f32[16,512,128]{2,1,0:T(8,128)S(1)} %get-tuple-element.26.refs_3_.refs_2_.cos_ref, ...), custom_call_target="tpu_custom_call" | custom-call | flops 2147483648 | bytes 9437184 | tf_op jit(solution)/shard_map/pallas_call | solution.py:317
  38.8 1.2 %shard_map.61 = (bf16[512,512]{1,0:T(8,128)(2,1)S(1)}, bf16[512,512]{1,0:T(8,128)(2,1)S(1)}, f32[64,128]{1,0:T(8,128)S(1)}, f32[64,128]{1,0:T(8,128)S(1)}, f32[64,128]{1,0:T(8,128)S(1)}, /*index=5*/f32[64,128]{1,0:T(8,128)S(1)}) custom-call(f32[384,512]{1,0:T(8,128)S(1)} %get-tuple-element.32.refs_0_, f32[384,512]{1,0:T(8,128)S(1)} %get-tuple-element.33.refs_1_, ...), custom_call_target="tpu_custom_call" | custom-call | flops 10485760 | bytes 6291456 | tf_op jit(solution)/shard_map/pallas_call | solution.py:386
  40.0 5.4 %shard_map.63 = f32[64,8192]{1,0:T(8,128)S(1)} custom-call(bf16[512,512]{1,0:T(8,128)(2,1)S(1)} %get-tuple-element.39.w_ref, f32[16,512,128]{2,1,0:T(8,128)S(1)} %get-tuple-element.29.refs_6_.refs_5_.cos_ref, f32[16,512,128]{2,1,0:T(8,128)S(1)} %get-tuple-element.30.refs_7_.refs_6_.sin_ref, f32[512,128]{1,0:T(8,128)S(1)} %get-tuple-element.31.refs_8_.refs_7_.sign_ref, ...), custom_call_target="tpu_custom_call" | custom-call | flops 4294967296 | bytes 9043968 | tf_op jit(solution)/shard_map/pallas_call | solution.py:469
  45.6 0.2 multiply_convert_fusion
  46.0 0.2 pad_maximum_fusion
  46.2 0.5 collective-permute-start.11
  46.7 2.8 %shard_map.62 = f32[32,8192]{1,0:T(8,128)S(1)} custom-call(bf16[512,512]{1,0:T(8,128)(2,1)S(1)} %get-tuple-element.44.w_ref, f32[16,512,128]{2,1,0:T(8,128)S(1)} %get-tuple-element.26.refs_3_.refs_2_.cos_ref, f32[16,512,128]{2,1,0:T(8,128)S(1)} %get-tuple-element.27.refs_4_.refs_3_.sin_ref, f32[512,128]{1,0:T(8,128)S(1)} %get-tuple-element.28.refs_5_.refs_4_.sign_ref, ...), custom_call_target="tpu_custom_call" | custom-call | flops 2147483648 | bytes 8716288 | tf_op jit(solution)/shard_map/pallas_call | solution.py:469
  49.7 0.2 exponential_reduce_fusion
  49.9 0.2 slice_multiply_fusion
  50.1 0.2 exponential_reduce_fusion.6
  50.7 0.2 slice_add_fusion.1
  51.2 2.8 %shard_map.64 = f32[32,8192]{1,0:T(8,128)S(1)} custom-call(bf16[512,512]{1,0:T(8,128)(2,1)S(1)} %get-tuple-element.44.w_ref, f32[16,512,128]{2,1,0:T(8,128)S(1)} %get-tuple-element.26.refs_3_.refs_2_.cos_ref, f32[16,512,128]{2,1,0:T(8,128)S(1)} %get-tuple-element.27.refs_4_.refs_3_.sin_ref, f32[512,128]{1,0:T(8,128)S(1)} %get-tuple-element.28.refs_5_.refs_4_.sign_ref, ...), custom_call_target="tpu_custom_call" | custom-call | flops 2147483648 | bytes 8716288 | tf_op jit(solution)/shard_map/pallas_call | solution.py:469
  54.0 0.2 slice_add_fusion
  54.4 1.9 %collective-permute-start.14 = (f16[16,8320]{1,0:T(8,128)(2,1)S(1)}, f16[16,8320]{1,0:T(8,128)(2,1)S(1)}, u32[]{:S(2)}, u32[]{:S(2)}) collective-permute-start(f16[16,8320]{1,0:T(8,128)(2,1)S(1)} %pad_maximum_fusion.3), channel_id=1, source_target_pairs={{0,6},{1,7},{2,4},{3,5},{4,2},{5,3},{6,0},{7,1},{8,14},{9,15},{10,... | collective-permute-start | bytes 798728 | tf_op jit(solution)/shard_map/ppermute | solution.py:485
  56.2 0.5 collective-permute-start.12
  56.8 1.2 %collective-permute-start.13 = (f16[16,8320]{1,0:T(8,128)(2,1)S(1)}, f16[16,8320]{1,0:T(8,128)(2,1)S(1)}, u32[]{:S(2)}, u32[]{:S(2)}) collective-permute-start(f16[16,8320]{1,0:T(8,128)(2,1)S(1)} %pad_maximum_fusion.2), channel_id=1, source_target_pairs={{0,4},{1,5},{2,6},{3,7},{4,0},{5,1},{6,2},{7,3},{8,12},{9,13},{10,... | collective-permute-start | bytes 798728 | tf_op jit(solution)/shard_map/ppermute | solution.py:485
  57.9 6.7 %collective-permute-done.14 = f16[16,8320]{1,0:T(8,128)(2,1)S(1)} collective-permute-done((f16[16,8320]{1,0:T(8,128)(2,1)S(1)}, f16[16,8320]{1,0:T(8,128)(2,1)S(1)}, u32[]{:S(2)}, u32[]{:S(2)}) %collective-permute-start.14) | collective-permute-done | bytes 266272 | tf_op jit(solution)/shard_map/ppermute | solution.py:485
  64.7 4.1 %collective-permute-done.12 = f16[16,8320]{1,0:T(8,128)(2,1)S(1)} collective-permute-done((f16[16,8320]{1,0:T(8,128)(2,1)S(1)}, f16[16,8320]{1,0:T(8,128)(2,1)S(1)}, u32[]{:S(2)}, u32[]{:S(2)}) %collective-permute-start.12) | collective-permute-done | bytes 266272 | tf_op jit(solution)/shard_map/ppermute | solution.py:485
  68.9 0.5 collective-permute-done.13
  69.4 0.2 slice_add_fusion.6
  69.7 0.2 exponential_reduce_fusion.10
  70.0 0.2 fusion
  70.3 0.2 fusion.13
  70.7 2.4 %collective-permute-start.16 = (f16[4,8320]{1,0:T(4,128)(2,1)S(1)}, f16[4,8320]{1,0:T(4,128)(2,1)S(1)}, u32[]{:S(2)}, u32[]{:S(2)}) collective-permute-start(f16[4,8320]{1,0:T(4,128)(2,1)S(1)} %pad_maximum_fusion.7), channel_id=1, source_target_pairs={{0,16},{8,24},{16,0},{24,8},{1,17},{9,25},{17,1},{25,9},{2,18},{10... | collective-permute-start | bytes 199688 | tf_op jit(solution)/shard_map/ppermute | solution.py:485
  73.2 2.1 %collective-permute-start.17 = (f16[4,8320]{1,0:T(4,128)(2,1)S(1)}, f16[4,8320]{1,0:T(4,128)(2,1)S(1)}, u32[]{:S(2)}, u32[]{:S(2)}) collective-permute-start(f16[4,8320]{1,0:T(4,128)(2,1)S(1)} %pad_maximum_fusion.8), channel_id=1, source_target_pairs={{0,24},{8,16},{16,8},{24,0},{1,25},{9,17},{17,9},{25,1},{2,26},{10... | collective-permute-start | bytes 199688 | tf_op jit(solution)/shard_map/ppermute | solution.py:485
  75.3 0.9 %collective-permute-done.15 = f16[4,8320]{1,0:T(4,128)(2,1)S(1)} collective-permute-done((f16[4,8320]{1,0:T(4,128)(2,1)S(1)}, f16[4,8320]{1,0:T(4,128)(2,1)S(1)}, u32[]{:S(2)}, u32[]{:S(2)}) %collective-permute-start.15) | collective-permute-done | bytes 66592 | tf_op jit(solution)/shard_map/ppermute | solution.py:485
  76.2 2.2 %collective-permute-done.16 = f16[4,8320]{1,0:T(4,128)(2,1)S(1)} collective-permute-done((f16[4,8320]{1,0:T(4,128)(2,1)S(1)}, f16[4,8320]{1,0:T(4,128)(2,1)S(1)}, u32[]{:S(2)}, u32[]{:S(2)}) %collective-permute-start.16) | collective-permute-done | bytes 66592 | tf_op jit(solution)/shard_map/ppermute | solution.py:485
  78.4 0.9 %collective-permute-done.17 = f16[4,8320]{1,0:T(4,128)(2,1)S(1)} collective-permute-done((f16[4,8320]{1,0:T(4,128)(2,1)S(1)}, f16[4,8320]{1,0:T(4,128)(2,1)S(1)}, u32[]{:S(2)}, u32[]{:S(2)}) %collective-permute-start.17) | collective-permute-done | bytes 66592 | tf_op jit(solution)/shard_map/ppermute | solution.py:485
  79.3 0.2 fusion.51
  79.5 0.2 fusion.8.in_ref
  79.7 0.7 shard_map.65
  (61 shorter events, 2.7 us)
Async XLA Ops:
  0.0 0.8 %copy-start = (bf16[4,2,4096]{2,1,0:T(2,128)(2,1)S(1)}, bf16[4,2,4096]{2,1,0:T(2,128)(2,1)}, u32[]{:S(2)}) copy-start(bf16[4,2,4096]{2,1,0:T(2,128)(2,1)} %param.7) | copy-start | bytes 196612
  0.9 6.2 %collective-permute-start = (bf16[4,8192]{1,0:T(4,128)(2,1)S(1)}, bf16[4,8192]{1,0:T(4,128)(2,1)S(1)}, u32[]{:S(2)}, u32[]{:S(2)}) collective-permute-start(bf16[4,8192]{1,0:T(4,128)(2,1)S(1)} %shard_map.55), channel_id=1, source_target_pairs={{0,8},{8,0},{16,24},{24,16},{1,9},{9,1},{17,25},{25,17},{2,10},{10... | collective-permute-start | bytes 196616 | tf_op jit(solution)/shard_map/ppermute | solution.py:485
  4.1 7.3 %collective-permute-start.1 = (bf16[4,8192]{1,0:T(4,128)(2,1)S(1)}, bf16[4,8192]{1,0:T(4,128)(2,1)S(1)}, u32[]{:S(2)}, u32[]{:S(2)}) collective-permute-start(bf16[4,8192]{1,0:T(4,128)(2,1)S(1)} %shard_map.55), channel_id=1, source_target_pairs={{0,16},{8,24},{16,0},{24,8},{1,17},{9,25},{17,1},{25,9},{2,18},{10... | collective-permute-start | bytes 196616 | tf_op jit(solution)/shard_map/ppermute | solution.py:485
  6.6 6.1 %collective-permute-start.2 = (bf16[4,8192]{1,0:T(4,128)(2,1)S(1)}, bf16[4,8192]{1,0:T(4,128)(2,1)S(1)}, u32[]{:S(2)}, u32[]{:S(2)}) collective-permute-start(bf16[4,8192]{1,0:T(4,128)(2,1)S(1)} %shard_map.55), channel_id=1, source_target_pairs={{0,24},{8,16},{16,8},{24,0},{1,25},{9,17},{17,9},{25,1},{2,26},{10... | collective-permute-start | bytes 196616 | tf_op jit(solution)/shard_map/ppermute | solution.py:485
  12.9 12.9 %collective-permute-start.4 = (bf16[16,8192]{1,0:T(8,128)(2,1)S(1)}, bf16[16,8192]{1,0:T(8,128)(2,1)S(1)}, u32[]{:S(2)}, u32[]{:S(2)}) collective-permute-start(bf16[16,8192]{1,0:T(8,128)(2,1)S(1)} %pad_maximum_fusion.4.refs_0_), channel_id=1, source_target_pairs={{0,4},{1,5},{2,6},{3,7},{4,0},{5,1},{6,2},{7,3},{8,12},{9,13},{10,... | collective-permute-start | bytes 786440 | tf_op jit(solution)/shard_map/ppermute | solution.py:485
  14.5 11.9 %collective-permute-start.3 = (bf16[16,8192]{1,0:T(8,128)(2,1)S(1)}, bf16[16,8192]{1,0:T(8,128)(2,1)S(1)}, u32[]{:S(2)}, u32[]{:S(2)}) collective-permute-start(bf16[16,8192]{1,0:T(8,128)(2,1)S(1)} %pad_maximum_fusion.4.refs_0_), channel_id=1, source_target_pairs={{0,2},{1,3},{2,0},{3,1},{4,6},{5,7},{6,4},{7,5},{8,10},{9,11},{10,... | collective-permute-start | bytes 786440 | tf_op jit(solution)/shard_map/ppermute | solution.py:485
  16.0 6.5 %copy-start.1 = (s32[128,8]{0,1:T(8,128)S(1)}, s32[128,8]{0,1:T(8,128)}, u32[]{:S(2)}) copy-start(s32[128,8]{0,1:T(8,128)} %param.9) | copy-start | bytes 12292
  16.0 6.5 %copy-start.3 = (s32[128]{0:T(128)S(1)}, s32[128]{0:T(128)}, u32[]{:S(2)}) copy-start(s32[128]{0:T(128)} %param.8) | copy-start | bytes 1540
  25.7 6.5 %collective-permute-start.5 = (bf16[16,8192]{1,0:T(8,128)(2,1)S(1)}, bf16[16,8192]{1,0:T(8,128)(2,1)S(1)}, u32[]{:S(2)}, u32[]{:S(2)}) collective-permute-start(bf16[16,8192]{1,0:T(8,128)(2,1)S(1)} %pad_maximum_fusion.4.refs_0_), channel_id=1, source_target_pairs={{0,1},{1,0},{2,3},{3,2},{4,5},{5,4},{6,7},{7,6},{8,9},{9,8},{10,11... | collective-permute-start | bytes 786440 | tf_op jit(solution)/shard_map/ppermute | solution.py:485
  25.8 6.0 %collective-permute-start.8 = (bf16[16,4096]{1,0:T(8,128)(2,1)S(1)}, bf16[16,4096]{1,0:T(8,128)(2,1)S(1)}, u32[]{:S(2)}, u32[]{:S(2)}) collective-permute-start(bf16[16,4096]{1,0:T(8,128)(2,1)S(1)} %slice.257), channel_id=1, source_target_pairs={{0,2},{1,3},{2,0},{3,1},{4,6},{5,7},{6,4},{7,5},{8,10},{9,11},{10,... | collective-permute-start | bytes 393224 | tf_op jit(solution)/shard_map/ppermute | solution.py:485
  26.4 5.7 %collective-permute-start.9 = (bf16[16,4096]{1,0:T(8,128)(2,1)S(1)}, bf16[16,4096]{1,0:T(8,128)(2,1)S(1)}, u32[]{:S(2)}, u32[]{:S(2)}) collective-permute-start(bf16[16,4096]{1,0:T(8,128)(2,1)S(1)} %slice.258), channel_id=1, source_target_pairs={{0,4},{1,5},{2,6},{3,7},{4,0},{5,1},{6,2},{7,3},{8,12},{9,13},{10,... | collective-permute-start | bytes 393224 | tf_op jit(solution)/shard_map/ppermute | solution.py:485
  27.0 5.2 %collective-permute-start.6 = (bf16[16,8192]{1,0:T(8,128)(2,1)S(1)}, bf16[16,8192]{1,0:T(8,128)(2,1)S(1)}, u32[]{:S(2)}, u32[]{:S(2)}) collective-permute-start(bf16[16,8192]{1,0:T(8,128)(2,1)S(1)} %collective-permute-done.3.refs_1_), channel_id=1, source_target_pairs={{0,1},{1,0},{2,3},{3,2},{4,5},{5,4},{6,7},{7,6},{8,9},{9,8},{10,11... | collective-permute-start | bytes 786440 | tf_op jit(solution)/shard_map/ppermute | solution.py:485
  27.0 5.2 %collective-permute-start.7 = (bf16[16,8192]{1,0:T(8,128)(2,1)S(1)}, bf16[16,8192]{1,0:T(8,128)(2,1)S(1)}, u32[]{:S(2)}, u32[]{:S(2)}) collective-permute-start(bf16[16,8192]{1,0:T(8,128)(2,1)S(1)} %collective-permute-done.4.refs_2_), channel_id=1, source_target_pairs={{0,1},{1,0},{2,3},{3,2},{4,5},{5,4},{6,7},{7,6},{8,9},{9,8},{10,11... | collective-permute-start | bytes 786440 | tf_op jit(solution)/shard_map/ppermute | solution.py:485
  32.1 4.0 %collective-permute-start.10 = (bf16[16,8192]{1,0:T(8,128)(2,1)S(1)}, bf16[16,8192]{1,0:T(8,128)(2,1)S(1)}, u32[]{:S(2)}, u32[]{:S(2)}) collective-permute-start(bf16[16,8192]{1,0:T(8,128)(2,1)S(1)} %constant_dynamic-update-slice_fusion.refs_0_), channel_id=1, source_target_pairs={{0,1},{1,0},{2,3},{3,2},{4,5},{5,4},{6,7},{7,6},{8,9},{9,8},{10,11... | collective-permute-start | bytes 786440 | tf_op jit(solution)/shard_map/ppermute | solution.py:485
  36.0 2.7 %copy-start.2 = (f32[512]{0:T(512)S(1)}, f32[512]{0:T(512)}, u32[]{:S(2)}) copy-start(f32[512]{0:T(512)} %param.6) | copy-start | bytes 6148
  46.2 3.3 %collective-permute-start.11 = (f16[64,8320]{1,0:T(8,128)(2,1)S(1)}, f16[64,8320]{1,0:T(8,128)(2,1)S(1)}, u32[]{:S(2)}, u32[]{:S(2)}) collective-permute-start(f16[64,8320]{1,0:T(8,128)(2,1)S(1)} %pad_maximum_fusion), channel_id=1, source_target_pairs={{0,1},{1,0},{2,3},{3,2},{4,5},{5,4},{6,7},{7,6},{8,9},{9,8},{10,11... | collective-permute-start | bytes 3194888 | tf_op jit(solution)/shard_map/ppermute | solution.py:485
  54.4 10.3 %collective-permute-start.14 = (f16[16,8320]{1,0:T(8,128)(2,1)S(1)}, f16[16,8320]{1,0:T(8,128)(2,1)S(1)}, u32[]{:S(2)}, u32[]{:S(2)}) collective-permute-start(f16[16,8320]{1,0:T(8,128)(2,1)S(1)} %pad_maximum_fusion.3), channel_id=1, source_target_pairs={{0,6},{1,7},{2,4},{3,5},{4,2},{5,3},{6,0},{7,1},{8,14},{9,15},{10,... | collective-permute-start | bytes 798728 | tf_op jit(solution)/shard_map/ppermute | solution.py:485
  56.2 12.6 %collective-permute-start.12 = (f16[16,8320]{1,0:T(8,128)(2,1)S(1)}, f16[16,8320]{1,0:T(8,128)(2,1)S(1)}, u32[]{:S(2)}, u32[]{:S(2)}) collective-permute-start(f16[16,8320]{1,0:T(8,128)(2,1)S(1)} %pad_maximum_fusion.1), channel_id=1, source_target_pairs={{0,2},{1,3},{2,0},{3,1},{4,6},{5,7},{6,4},{7,5},{8,10},{9,11},{10,... | collective-permute-start | bytes 798728 | tf_op jit(solution)/shard_map/ppermute | solution.py:485
  56.8 12.6 %collective-permute-start.13 = (f16[16,8320]{1,0:T(8,128)(2,1)S(1)}, f16[16,8320]{1,0:T(8,128)(2,1)S(1)}, u32[]{:S(2)}, u32[]{:S(2)}) collective-permute-start(f16[16,8320]{1,0:T(8,128)(2,1)S(1)} %pad_maximum_fusion.2), channel_id=1, source_target_pairs={{0,4},{1,5},{2,6},{3,7},{4,0},{5,1},{6,2},{7,3},{8,12},{9,13},{10,... | collective-permute-start | bytes 798728 | tf_op jit(solution)/shard_map/ppermute | solution.py:485
  70.6 5.6 %collective-permute-start.15 = (f16[4,8320]{1,0:T(4,128)(2,1)S(1)}, f16[4,8320]{1,0:T(4,128)(2,1)S(1)}, u32[]{:S(2)}, u32[]{:S(2)}) collective-permute-start(f16[4,8320]{1,0:T(4,128)(2,1)S(1)} %pad_maximum_fusion.6), channel_id=1, source_target_pairs={{0,8},{8,0},{16,24},{24,16},{1,9},{9,1},{17,25},{25,17},{2,10},{10... | collective-permute-start | bytes 199688 | tf_op jit(solution)/shard_map/ppermute | solution.py:485
  70.7 7.6 %collective-permute-start.16 = (f16[4,8320]{1,0:T(4,128)(2,1)S(1)}, f16[4,8320]{1,0:T(4,128)(2,1)S(1)}, u32[]{:S(2)}, u32[]{:S(2)}) collective-permute-start(f16[4,8320]{1,0:T(4,128)(2,1)S(1)} %pad_maximum_fusion.7), channel_id=1, source_target_pairs={{0,16},{8,24},{16,0},{24,8},{1,17},{9,25},{17,1},{25,9},{2,18},{10... | collective-permute-start | bytes 199688 | tf_op jit(solution)/shard_map/ppermute | solution.py:485
  73.2 6.1 %collective-permute-start.17 = (f16[4,8320]{1,0:T(4,128)(2,1)S(1)}, f16[4,8320]{1,0:T(4,128)(2,1)S(1)}, u32[]{:S(2)}, u32[]{:S(2)}) collective-permute-start(f16[4,8320]{1,0:T(4,128)(2,1)S(1)} %pad_maximum_fusion.8), channel_id=1, source_target_pairs={{0,24},{8,16},{16,8},{24,0},{1,25},{9,17},{17,9},{25,1},{2,26},{10... | collective-permute-start | bytes 199688 | tf_op jit(solution)/shard_map/ppermute | solution.py:485
